TPU v7x, 128 devices: a whole 4x4x4 slice. The times are simulated.
128 devices in a mesh: dp: 8 (over y, core), mp: 16 (over x, z).
Axes of the slice: x: 4, y: 4, z: 4, core: 2. Of those that a mesh axis runs over, the one named last changes fastest.
Arguments:
- span_tokens: bfloat16 [128, 256, 2560], P(('dp', 'mp')), may hold values from -6 to 6
- decode_tokens: bfloat16 [256, 2560], P(('dp', 'mp')), may hold values from -6 to 6
- norm_gain: float32 [2560], replicated, may hold values from 0.5 to 1.5
- query_weight: bfloat16 [2560, 2560], P(('dp', 'mp')), may hold values from -0.125 to 0.125
- keyval_weight: bfloat16 [2560, 512], P(('dp', 'mp')), may hold values from -0.125 to 0.125
- output_weight: bfloat16 [2560, 2560], P(('dp', 'mp')), may hold values from -0.125 to 0.125
- span_cache: bfloat16 [128, 2048, 512], P(('dp', 'mp')), may hold values from -360 to 360
- decode_cache: bfloat16 [256, 2048, 512], P(('dp', 'mp')), may hold values from -360 to 360
- span_index: int32 [128], P(('dp', 'mp')), may hold values from 0 to 15
- decode_length: int32 [256], P(('dp', 'mp')), may hold values from 1 to 32768
- cache_slot: int32 [256], replicated, may hold values from 0 to 255, each once
Outputs:
- span_output: bfloat16 [128, 256, 2560], P(('dp', 'mp'))
- span_keyval: bfloat16 [128, 256, 512], P(('dp', 'mp'))
- decode_output: bfloat16 [256, 2560], P(('dp', 'mp'))
- decode_keyval: bfloat16 [256, 512], P(('dp', 'mp'))
Inputs may be any that keep to these rules, and one draw needn't show every extreme that they name: `cache_slot`: each cache slot belongs to exactly one request.
All inputs are finite; a program needn't handle non-finite values.
Results may differ from a plain program's by a relative error of at most 0.024.
Values may be sent and summed in bfloat16 or wider, within the bound.
No kernel may reach another device: no remote copies, remote signals or barrier semaphores. Data moves between devices by JAX's collectives and lax.ppermute only.
A program may use at most 128 MiB of HBM per device.

v0:
```python
import jax
import jax.numpy as jnp
from jax import lax
from jax.sharding import PartitionSpec as P


def rms_normed(rows_in, norm_gain):
    widened = rows_in.astype(jnp.float32)
    spread = jnp.mean(widened * widened, axis=-1, keepdims=True)
    return (widened * lax.rsqrt(spread + 1e-06) * norm_gain).astype(jnp.bfloat16)


def rotate(values, positions):
    quarter = values.shape[-1] // 4
    frequency = 10000.0 ** (-jnp.arange(quarter, dtype=jnp.float32) / quarter)
    angles = positions.astype(jnp.float32)[..., None] * frequency
    cos_part = jnp.cos(angles)
    sin_part = jnp.sin(angles)
    first_half = values[..., :quarter]
    second_half = values[..., quarter : 2 * quarter]
    return jnp.concatenate(
        [
            first_half * cos_part - second_half * sin_part,
            second_half * cos_part + first_half * sin_part,
            values[..., 2 * quarter :],
        ],
        -1,
    )


def span_attend(queries, keyval, stored, offset):
    head_dim = queries.shape[-1]
    length = queries.shape[0]
    window = stored.shape[0]
    key_rows = jnp.concatenate([stored[:, :head_dim], keyval[:, :head_dim]], 0)
    value_rows = jnp.concatenate([stored[:, head_dim:], keyval[:, head_dim:]], 0)
    row_ids = jnp.arange(length, dtype=jnp.int32)
    slot_ids = jnp.arange(window, dtype=jnp.int32)
    held_pos = offset - 1 - jnp.mod(offset - 1 - slot_ids, window)
    cache_ok = (held_pos[None, :] >= 0) & (
        held_pos[None, :] >= offset + row_ids[:, None] - window + 1
    )
    own_ok = row_ids[None, :] <= row_ids[:, None]
    allowed = jnp.concatenate([cache_ok, own_ok], 1)

    def one_head(head_queries):
        scores = jnp.dot(
            head_queries, key_rows.T, preferred_element_type=jnp.float32
        ) * head_dim ** (-0.5)
        highest = jnp.max(jnp.where(allowed, scores, -1e30), -1, keepdims=True)
        exp_terms = jnp.where(allowed, jnp.exp(scores - highest), 0.0)
        weights = (exp_terms / jnp.sum(exp_terms, -1, keepdims=True)).astype(jnp.bfloat16)
        return jnp.dot(weights, value_rows, preferred_element_type=jnp.float32).astype(jnp.bfloat16)

    per_head = lax.map(one_head, jnp.transpose(queries, (1, 0, 2)))
    return jnp.transpose(per_head, (1, 0, 2)).reshape(length, -1)


def decode_attend(queries, keyval, stored, length):
    head_dim = queries.shape[-1]
    window = stored.shape[1]
    score_scale = head_dim ** (-0.5)
    exp_scores = (
        jnp.einsum(
            "ehd,ewd->ehw", queries, stored[..., :head_dim], preferred_element_type=jnp.float32
        )
        * score_scale
    )
    self_scores = (
        jnp.einsum("ehd,ed->eh", queries, keyval[:, :head_dim], preferred_element_type=jnp.float32)
        * score_scale
    )
    slot_ids = jnp.arange(window, dtype=jnp.int32)
    allowed = (slot_ids[None, :] < length[:, None]) & (
        slot_ids[None, :] != jnp.mod(length, window)[:, None]
    )
    allowed = allowed[:, None, :]
    highest = jnp.maximum(jnp.max(jnp.where(allowed, exp_scores, -1e30), -1), self_scores)
    exp_cache = jnp.where(allowed, jnp.exp(exp_scores - highest[..., None]), 0.0)
    exp_self = jnp.exp(self_scores - highest)
    denominator = jnp.sum(exp_cache, -1) + exp_self
    weight_cache = (exp_cache / denominator[..., None]).astype(jnp.bfloat16)
    weight_self = (exp_self / denominator).astype(jnp.bfloat16)
    attended = jnp.einsum(
        "ehw,ewd->ehd", weight_cache, stored[..., head_dim:], preferred_element_type=jnp.float32
    )
    attended = attended + weight_self.astype(jnp.float32)[..., None] * keyval[
        :, None, head_dim:
    ].astype(jnp.float32)
    return attended.astype(jnp.bfloat16).reshape(queries.shape[0], -1)


def shards(
    span_tokens,
    decode_tokens,
    norm_gain,
    query_weight,
    keyval_weight,
    output_weight,
    span_cache,
    decode_cache,
    span_index,
    decode_length,
    cache_slot,
):
    span_len = span_tokens.shape[1]
    own_slots = decode_cache.shape[0]
    requests = cache_slot.shape[0]
    head_dim = keyval_weight.shape[1] // 2
    device = lax.axis_index(("dp", "mp"))
    arrived, arrived_len = (
        lax.all_gather(decode_tokens, ("dp", "mp"), axis=0, tiled=True),
        lax.all_gather(decode_length, ("dp", "mp"), axis=0, tiled=True),
    )
    slot_ids = device * own_slots + jnp.arange(own_slots, dtype=jnp.int32)
    picker = cache_slot[None, :] == slot_ids[:, None]
    own_tokens = jnp.dot(
        picker.astype(jnp.bfloat16), arrived, preferred_element_type=jnp.float32
    ).astype(jnp.bfloat16)
    own_length = jnp.sum(jnp.where(picker, arrived_len[None, :], 0), axis=1).astype(jnp.int32)
    offset = span_index[0] * span_len
    positions = jnp.concatenate([offset + jnp.arange(span_len, dtype=jnp.int32), own_length])
    rows_all = jnp.concatenate([span_tokens[0], own_tokens], 0)
    normed = rms_normed(rows_all, norm_gain)
    row_count = rows_all.shape[0]
    columns = normed
    query_all = jnp.dot(
        columns,
        lax.all_gather(query_weight, ("dp", "mp"), axis=0, tiled=True),
        preferred_element_type=jnp.float32,
    )
    keyval_all = jnp.dot(
        columns,
        lax.all_gather(keyval_weight, ("dp", "mp"), axis=0, tiled=True),
        preferred_element_type=jnp.float32,
    )
    queries = rotate(query_all.reshape(row_count, -1, head_dim), positions[:, None]).astype(
        jnp.bfloat16
    )
    key_rows = rotate(keyval_all[:, :head_dim], positions).astype(jnp.bfloat16)
    keyval = jnp.concatenate([key_rows, keyval_all[:, head_dim:].astype(jnp.bfloat16)], 1)
    span_mixed = span_attend(queries[:span_len], keyval[:span_len], span_cache[0], offset)
    decode_mixed = decode_attend(queries[span_len:], keyval[span_len:], decode_cache, own_length)
    attended = jnp.concatenate([span_mixed, decode_mixed], 0)
    columns = attended
    projected = jnp.dot(
        columns,
        lax.all_gather(output_weight, ("dp", "mp"), axis=0, tiled=True),
        preferred_element_type=jnp.float32,
    )
    finished = (rows_all.astype(jnp.float32) + projected).astype(jnp.bfloat16)
    span_output = finished[:span_len][None]
    span_keyval = keyval[:span_len][None]
    served = finished[span_len:]
    decode_keyval = keyval[span_len:]
    everything = lax.all_gather(served, ("dp", "mp"), axis=0, tiled=True)
    arriving_slots = lax.dynamic_slice_in_dim(cache_slot, device * own_slots, own_slots)
    chooser = arriving_slots[:, None] == jnp.arange(requests, dtype=jnp.int32)[None, :]
    decode_output = jnp.dot(
        chooser.astype(jnp.bfloat16), everything, preferred_element_type=jnp.float32
    ).astype(jnp.bfloat16)
    return (span_output, span_keyval, decode_output, decode_keyval)


def solution(mesh):
    return jax.shard_map(
        shards,
        mesh=mesh,
        in_specs=(
            P(("dp", "mp"), None, None),
            P(("dp", "mp"), None),
            P(),
            P(("dp", "mp"), None),
            P(("dp", "mp"), None),
            P(("dp", "mp"), None),
            P(("dp", "mp"), None, None),
            P(("dp", "mp"), None, None),
            P(("dp", "mp")),
            P(("dp", "mp")),
            P(),
        ),
        out_specs=(
            P(("dp", "mp"), None, None),
            P(("dp", "mp"), None, None),
            P(("dp", "mp"), None),
            P(("dp", "mp"), None),
        ),
        check_vma=False,
    )
```

profile of v0, /device:TPU:1, one launch (start us, length us, event | category | flops | bytes accessed | tf_op | source)
XLA Modules:
  0.0 406.3 jit_solution(6080341818031185715)
XLA Ops:
  7.2 0.7 all-gather.11.cloned.1.call-update
  7.9 0.7 all-gather.15.cloned.1.call-update
  8.7 0.7 all-gather.13.cloned.1.call-update
  10.7 0.9 dynamic-update-slice
  11.5 69.1 %all-reduce = s32[256]{0:T(256)S(1)} all-reduce(s32[256]{0:T(256)S(1)} %dynamic-update-slice), channel_id=1, replica_groups=mesh['dp'=8,'mp'=16] {'dp','mp'}, use_global_device_ids=true, to_apply=%add | all-reduce | flops 256 | bytes 2048
  80.7 0.9 fusion.37
  82.2 2.7 fusion.54
  84.8 3.2 reshape.227
  88.4 1.0 copy-done.1
  89.7 55.2 %all-gather.15.cloned.1.call-done = bf16[128,20,512]{2,1,0:T(8,128)(2,1)} async-done(((bf16[1,20,512]{2,1,0:T(8,128)(2,1)}), bf16[128,20,512]{2,1,0:T(8,128)(2,1)}) %all-gather.15.cloned.1.call-update) | async-done | bytes 2621456 | tf_op jit(solution)/shard_map/all_gather | solution.py:134
  144.9 5.2 %reshape.231 = bf16[2560,512]{1,0:T(8,128)(2,1)} reshape(bf16[128,20,512]{2,1,0:T(8,128)(2,1)} %all-gather.15.cloned.1.call-done) | data formatting | bytes 5242880
  150.1 2.7 fusion.55
  152.9 1.3 subtract_convert_fusion.1
  154.4 1.2 pad_maximum_fusion.2
  155.6 68.3 %all-gather.13.cloned.1.call-done = bf16[128,20,2560]{2,1,0:T(8,128)(2,1)} async-done(((bf16[1,20,2560]{2,1,0:T(8,128)(2,1)}), bf16[128,20,2560]{2,1,0:T(8,128)(2,1)}) %all-gather.13.cloned.1.call-update) | async-done | bytes 13107216 | tf_op jit(solution)/shard_map/all_gather | solution.py:129
  223.8 18.0 %reshape.229 = bf16[2560,2560]{1,0:T(8,128)(2,1)} reshape(bf16[128,20,2560]{2,1,0:T(8,128)(2,1)} %all-gather.13.cloned.1.call-done) | data formatting | bytes 26214400
  241.8 8.5 %fusion.52 = f32[258,2560]{1,0:T(8,128)} fusion(bf16[2560,2560]{1,0:T(8,128)(2,1)} %reshape.229, f32[2560]{0:T(1024)S(1)} %copy-done.12, f32[258]{0:T(512)S(1)} %add_rsqrt_fusion, bf16[2,2560]{1,0:T(2,128)(2,1)S(1)} %convolution_convert_fusion.1, bf16[256,2560]{1,0:T(8,128)(2,1)S(1)} %bitcast.48), kind=kOutput, calls=%fused_computation.102 | convolution fusion | flops 3386280960 | bytes 17081352 | tf_op jit(solution)/shard_map/dot_general | solution.py:127
  250.3 4.5 %reshape.221 = f32[258,10,256]{2,1,0:T(8,128)} reshape(f32[258,2560]{1,0:T(8,128)} %fusion.52) | data formatting | bytes 5283840 | tf_op jit(solution)/shard_map/reshape | solution.py:137
  254.8 1.8 slice.140
  256.6 3.1 subtract_convert_fusion
  259.7 1.1 maximum_bitcast_fusion
  261.4 1.7 copy-done.6
  263.1 0.8 select_reduce_fusion.1
  264.5 1.2 copy.27
  265.7 35.7 %while.10 = (s32[]{:T(128)}, bf16[10,256,256]{1,2,0:T(8,128)(2,1)}, bf16[10,256,256]{2,1,0:T(8,128)(2,1)S(1)}, bf16[2304,256]{1,0:T(8,128)(2,1)S(1)}, pred[256,2...) while((s32[]{:T(128)}, bf16[10,256,256]{1,2,0:T(8,128)(2,1)}, ...), condition=%wide.region_5.6_spmd, body=%wide.region_2.5_spmd.sunk | while | flops 609943040 | bytes 16717421 | solution.py:55
  265.7 0.7 select_reduce_fusion.3
  266.4 0.7 fusion.69
  267.7 0.8 fusion.70
  269.3 0.7 select_reduce_fusion.3
  270.0 0.7 fusion.69
  271.2 0.8 fusion.70
  272.8 0.7 select_reduce_fusion.3
  273.5 0.7 fusion.69
  274.8 0.8 fusion.70
  276.3 0.7 select_reduce_fusion.3
  277.0 0.7 fusion.69
  277.7 0.9 copy-done.5
  278.6 0.8 fusion.70
  280.2 0.7 select_reduce_fusion.3
  280.9 0.7 fusion.69
  282.1 0.8 fusion.70
  283.7 0.7 select_reduce_fusion.3
  284.4 0.7 fusion.69
  285.7 0.8 fusion.70
  287.3 0.7 select_reduce_fusion.3
  287.9 0.7 fusion.69
  289.2 0.8 fusion.70
  291.5 0.7 fusion.69
  292.7 0.8 fusion.70
  294.3 0.7 select_reduce_fusion.3
  295.0 0.7 fusion.69
  296.3 0.8 fusion.70
  297.9 0.7 select_reduce_fusion.3
  298.6 0.7 fusion.69
  299.8 0.8 fusion.70
  301.4 3.2 all-gather.17.cloned.1.call-done
  304.7 18.0 %reshape.233 = bf16[2560,2560]{1,0:T(8,128)(2,1)} reshape(bf16[128,20,2560]{2,1,0:T(8,128)(2,1)} %all-gather.17.cloned.1.call-done) | data formatting | bytes 26214400
  322.6 8.8 %fusion.8 = bf16[258,2560]{1,0:T(8,128)(2,1)S(1)} fusion(bf16[2560,2560]{1,0:T(8,128)(2,1)} %reshape.233, bf16[2,2560]{0,1:T(8,128)(2,1)S(1)} %bitcast.50, bf16[256,2560]{0,1:T(8,128)(2,1)} %bitcast.57, bf16[2,2560]{1,0:T(2,128)(2,1)S(1)} %convolution_convert_fusion.1, bf16[256,2560]{1,0:T(8,128)(2,1)S(1)} %bitcast.49), kind=kOutput, calls=%fused_computation.16 | convolution fusion | flops 3388262400 | bytes 17070080 | tf_op jit(solution)/shard_map/dot_general | solution.py:146
  332.2 1.0 slice.116
  333.9 0.7 slice_bitcast_fusion.1
  334.7 1.1 slice_bitcast_fusion
  335.8 59.9 %all-gather.19.cloned.1.call-done = bf16[128,2,2560]{2,1,0:T(2,128)(2,1)} async-done(((bf16[1,2,2560]{2,1,0:T(2,128)(2,1)}), bf16[128,2,2560]{2,1,0:T(2,128)(2,1)}) %all-gather.19.cloned.1.call-update) | async-done | bytes 1310736 | tf_op jit(solution)/shard_map/all_gather | solution.py:156
  395.7 3.2 reshape.235
  398.9 0.9 convolution_convert_fusion
  (103 shorter events, 18.7 us)
Async XLA Ops:
  7.2 77.7 %all-gather.11.cloned.1.call-start = ((), (), s32[]{:S(2)}) async-start(), calls=%async_computation | async-start | bytes 1320960 | tf_op jit(solution)/shard_map/all_gather | solution.py:112
  7.9 137.0 %all-gather.15.cloned.1.call-start = ((), (), s32[]{:S(2)}) async-start(), calls=%async_computation.2 | async-start | bytes 3170304 | tf_op jit(solution)/shard_map/all_gather | solution.py:134
  8.6 215.2 %all-gather.13.cloned.1.call-start = ((), (), s32[]{:S(2)}) async-start(), calls=%async_computation.1 | async-start | bytes 15851520 | tf_op jit(solution)/shard_map/all_gather | solution.py:129
  9.4 295.3 %all-gather.17.cloned.1.call-start = ((), (), s32[]{:S(2)}) async-start(), calls=%async_computation.3 | async-start | bytes 15851520 | tf_op jit(solution)/shard_map/all_gather | solution.py:148
  10.0 385.7 %all-gather.19.cloned.1.call-start = ((), (), s32[]{:S(2)}) async-start(), calls=%async_computation.4 | async-start | bytes 1320960 | tf_op jit(solution)/shard_map/all_gather | solution.py:156
  84.8 3.2 copy-start.11
  88.0 1.3 copy-start.1
  89.7 60.4 %copy-start.2 = (bf16[1,256,2560]{2,1,0:T(8,128)(2,1)S(1)}, bf16[1,256,2560]{2,1,0:T(8,128)(2,1)}, u32[]{:S(2)}) copy-start(bf16[1,256,2560]{2,1,0:T(8,128)(2,1)} %param.13) | copy-start | bytes 3932164
  89.7 60.4 %copy-start.12 = (f32[2560]{0:T(1024)S(1)}, f32[2560]{0:T(1024)}, u32[]{:S(2)}) copy-start(f32[2560]{0:T(1024)} %param.15) | copy-start | bytes 30724
  152.8 1.6 copy-start.8
  152.8 1.6 copy-start
  155.6 86.3 %copy-start.3 = (bf16[1,256,2560]{2,1,0:T(8,128)(2,1)S(1)}, bf16[1,256,2560]{2,1,0:T(8,128)(2,1)}, u32[]{:S(2)}) copy-start(bf16[1,256,2560]{2,1,0:T(8,128)(2,1)} %param.13) | copy-start | bytes 3932164
  254.8 1.8 copy-start.9
  254.8 1.8 copy-start.10
  260.8 2.3 copy-start.6
  266.4 1.3 copy-start.5
  269.9 1.3 copy-start.5
  273.5 1.3 copy-start.5
  277.0 1.6 copy-start.5
  280.9 1.3 copy-start.5
  284.4 1.3 copy-start.5
  287.9 1.3 copy-start.5
  291.5 1.3 copy-start.5
  295.0 1.3 copy-start.5
  298.6 1.3 copy-start.5
  301.4 21.2 %copy-start.4 = (bf16[1,256,2560]{2,1,0:T(8,128)(2,1)S(1)}, bf16[1,256,2560]{2,1,0:T(8,128)(2,1)}, u32[]{:S(2)}) copy-start(bf16[1,256,2560]{2,1,0:T(8,128)(2,1)} %param.13) | copy-start | bytes 3932164
  301.4 21.2 %copy-start.7 = (bf16[2,10,256]{0,2,1:T(8,128)(2,1)S(1)}, bf16[2,10,256]{0,2,1:T(8,128)(2,1)}, u32[]{:S(2)}) copy-start(bf16[2,10,256]{0,2,1:T(8,128)(2,1)} %copy.27) | copy-start | bytes 30724
Sparse Core Ops, SparseCore 0:
  10.8 67.5 all-gather.10
  81.5 63.4 all-gather.14
  148.0 75.7 all-gather.12
  226.8 77.8 all-gather.16
  332.2 63.3 all-gather.18
where the time goes:
time: 408 us; the launch traced here: 406 us
  waiting for transfers between devices  189 us (46%)
  local copies, waits for them, and re-layouts  78.9 us (19%)
  blocking collectives  69.1 us (17%)
  matrix products  37.4 us (9%)
  other arithmetic  16.6 us (4%)
  between operations  14.7 us (4%)
    unnamed x1, blocking collectives  69.1 us
    all_gather x1, waiting for transfers between devices, shards(): lax.all_gather(query_weight, ('dp', 'mp'), axis=0, tiled=True)  68.3 us
    all_gather x1, waiting for transfers between devices, shards(): everything = lax.all_gather(served, ('dp', 'mp'), axis=0, tiled=True)  59.9 us
    all_gather x1, waiting for transfers between devices, shards(): lax.all_gather(keyval_weight, ('dp', 'mp'), axis=0, tiled=True)  55.2 us
    unnamed x32, local copies, waits for them, and re-layouts  51.7 us
    dot_general x1, matrix products, shards(): jnp.dot(columns, lax.all_gather(output_weight, ('dp', 'mp'), axis=0, tile...  8.85 us
    dot_general x1, matrix products, shards(): jnp.dot(columns, lax.all_gather(query_weight, ('dp', 'mp'), axis=0, tiled...  8.51 us
  transfers between devices with their start and end apart: 5, of which 4 were waited for; matrix products, arithmetic and copies ran while one was open for 23% of the time, Pallas kernels for 0%

commit v1 on v0

v1 whole, which is shorter than its diff:
```python
import functools

import jax
import jax.numpy as jnp
import numpy as np
from jax import lax
from jax.experimental import pallas as pl
from jax.experimental.pallas import tpu as pltpu
from jax.sharding import PartitionSpec as P

AXES = ("dp", "mp")
LOG2E = 1.4426950408889634
NEG = -1e30
F32 = jnp.float32
BF16 = jnp.bfloat16
EXTRA = 16


def params(mib, *semantics):
    return pltpu.CompilerParams(vmem_limit_bytes=mib << 20, dimension_semantics=semantics or None)


def dot(a, b):
    return jnp.dot(a, b, preferred_element_type=F32)


def dot_t(a, b):
    return lax.dot_general(a, b, (((1,), (1,)), ((), ())), preferred_element_type=F32)


def spreader(run, padded, runs):
    src = np.arange(run * runs)
    to = (src // run) * padded + src % run
    return (jnp.asarray(to, jnp.int32)[:, None] == jnp.arange(padded * runs)[None, :]).astype(BF16)


def norm_body(x_ref, gain_ref, spread_ref, out_ref):
    x = x_ref[...].astype(F32)
    mean = jnp.mean(x * x, axis=-1, keepdims=True)
    normed = (x * lax.rsqrt(mean + 1e-06) * gain_ref[...]).astype(BF16)
    k, kp = spread_ref.shape
    for g in range(x.shape[1] // k):
        out_ref[:, g * kp : (g + 1) * kp] = dot(
            normed[:, g * k : (g + 1) * k], spread_ref[...]
        ).astype(BF16)


def norm_spread(x, gain, spread):
    rows, width = x.shape
    return pl.pallas_call(
        norm_body,
        out_shape=jax.ShapeDtypeStruct((rows, width // spread.shape[0] * spread.shape[1]), BF16),
        compiler_params=params(40),
        name="norm_spread",
    )(x, gain[None], spread)


def rotate(v, cos_ref, sin_ref):
    half = v[:, :128]
    turned = half * cos_ref[...] + pltpu.roll(half, 64, 1) * sin_ref[...]
    return jnp.concatenate([turned, v[:, 128:]], 1)


def project_body(last, x_ref, w_ref, cos_ref, sin_ref, out_ref):
    v = dot(x_ref[...], w_ref[...])

    @pl.when(pl.program_id(0) < last)
    def _():
        out_ref[0] = rotate(v, cos_ref, sin_ref).astype(BF16)

    @pl.when(pl.program_id(0) == last)
    def _():
        out_ref[0] = v.astype(BF16)


def project(x, w, cos, sin, hd):
    rows, depth = x.shape
    blocks = w.shape[1] // hd
    return pl.pallas_call(
        functools.partial(project_body, blocks - 1),
        grid=(blocks,),
        in_specs=[
            pl.BlockSpec((rows, depth), lambda i: (0, 0)),
            pl.BlockSpec((depth, hd), lambda i: (0, i)),
            pl.BlockSpec((rows, 128), lambda i: (0, 0)),
            pl.BlockSpec((rows, 128), lambda i: (0, 0)),
        ],
        out_specs=pl.BlockSpec((1, rows, hd), lambda i: (i, 0, 0)),
        out_shape=jax.ShapeDtypeStruct((blocks, rows, hd), BF16),
        compiler_params=params(40, "arbitrary"),
        cost_estimate=pl.CostEstimate(
            flops=2 * rows * depth * w.shape[1], bytes_accessed=2 * depth * w.shape[1], transcendentals=0
        ),
        name="project",
    )(x, w, cos, sin)


def decode_body(len_ref, q_ref, own_ref, cache_ref, out_ref):
    length = len_ref[pl.program_id(0)]
    q = q_ref[0]
    hd = q.shape[1]
    window = cache_ref.shape[1]
    scores = dot_t(q, cache_ref[0, :, :hd])
    own_key = own_ref[0, :, :hd].astype(F32)
    own = jnp.sum(q.astype(F32) * own_key, axis=1, keepdims=True)
    slot = lax.broadcasted_iota(jnp.int32, scores.shape, 1)
    met = (slot < length) & (slot != lax.rem(length, window))
    scores = jnp.where(met, scores, NEG)
    top = jnp.maximum(jnp.max(scores, 1, keepdims=True), own)
    scale = LOG2E * hd**-0.5
    terms = jnp.where(met, jnp.exp2((scores - top) * scale), 0.0)
    own_term = jnp.exp2((own - top) * scale)
    total = jnp.sum(terms, 1, keepdims=True) + own_term
    weights = (terms / total).astype(BF16)
    own_weight = (own_term / total).astype(BF16).astype(F32)
    mixed = dot(weights, cache_ref[0, :, hd:]) + own_weight * own_ref[0, :, hd:].astype(F32)
    out_ref[0] = mixed.astype(BF16)


def decode_attend(lengths, q, own, cache):
    n, heads, hd = q.shape
    window = cache.shape[1]
    return pl.pallas_call(
        decode_body,
        grid_spec=pltpu.PrefetchScalarGridSpec(
            num_scalar_prefetch=1,
            grid=(n,),
            in_specs=[
                pl.BlockSpec((1, heads, hd), lambda i, s: (i, 0, 0)),
                pl.BlockSpec((1, 1, 2 * hd), lambda i, s: (i, 0, 0)),
                pl.BlockSpec((1, window, 2 * hd), lambda i, s: (i, 0, 0)),
            ],
            out_specs=pl.BlockSpec((1, heads, hd), lambda i, s: (i, 0, 0)),
        ),
        out_shape=jax.ShapeDtypeStruct((n, heads, hd), BF16),
        compiler_params=params(32, "arbitrary"),
        cost_estimate=pl.CostEstimate(
            flops=4 * n * heads * hd * window, bytes_accessed=4 * n * hd * window, transcendentals=0
        ),
        name="decode_attend",
    )(lengths, q, own[:, None], cache)


def span_body(index_ref, q_ref, k_ref, v_ref, cache_ref, out_ref):
    index = index_ref[0]
    q = q_ref[0]
    rows, hd = q.shape
    blocks = cache_ref.shape[1] // rows
    wrapped = index >= blocks
    row = lax.broadcasted_iota(jnp.int32, (rows, rows), 0)
    col = lax.broadcasted_iota(jnp.int32, (rows, rows), 1)
    own = col <= row
    starts, scores, shifts = [], [], []
    top = None
    for rel in range(blocks):
        block = lax.rem(index + rel, blocks)
        start = pl.multiple_of(block * rows, rows)
        starts.append(start)
        s = dot_t(q, cache_ref[0, pl.ds(start, rows), :hd])
        if rel == 0:
            s = jnp.where(own, dot_t(q, k_ref[0]), jnp.where(wrapped, s, NEG))
            shift = jnp.float32(0)
        else:
            shift = jnp.where(wrapped | (block < index), jnp.float32(0), jnp.float32(NEG))
        scores.append(s)
        shifts.append(shift)
        peak = jnp.max(s, 1, keepdims=True) + shift
        top = peak if top is None else jnp.maximum(top, peak)
    scale = LOG2E * hd**-0.5
    base = top * scale
    total = jnp.zeros((rows, 1), F32)
    mixed = jnp.zeros((rows, hd), F32)
    for rel in range(blocks):
        terms = jnp.exp2(scores[rel] * scale - (base - shifts[rel]))
        total += jnp.sum(terms, 1, keepdims=True)
        old_values = cache_ref[0, pl.ds(starts[rel], rows), hd:]
        if rel == 0:
            mixed += dot(jnp.where(own, terms, 0.0).astype(BF16), v_ref[0])
            mixed += dot(jnp.where(own, 0.0, terms).astype(BF16), old_values)
        else:
            mixed += dot(terms.astype(BF16), old_values)
    out_ref[...] = (mixed / total).astype(BF16)


def span_attend(index, qkv, rows, cache):
    heads, hd = qkv.shape[0] - 2, qkv.shape[2]
    window = cache.shape[1]
    return pl.pallas_call(
        span_body,
        grid_spec=pltpu.PrefetchScalarGridSpec(
            num_scalar_prefetch=1,
            grid=(heads,),
            in_specs=[
                pl.BlockSpec((1, rows, hd), lambda h, s: (h, 0, 0)),
                pl.BlockSpec((1, rows, hd), lambda h, s: (heads, 0, 0)),
                pl.BlockSpec((1, rows, hd), lambda h, s: (heads + 1, 0, 0)),
                pl.BlockSpec((1, window, 2 * hd), lambda h, s: (0, 0, 0)),
            ],
            out_specs=pl.BlockSpec((rows, hd), lambda h, s: (0, h)),
        ),
        out_shape=jax.ShapeDtypeStruct((rows, heads * hd), BF16),
        compiler_params=params(48, "arbitrary"),
        cost_estimate=pl.CostEstimate(
            flops=4 * heads * rows * hd * (window + rows),
            bytes_accessed=4 * hd * window,
            transcendentals=heads * rows * window,
        ),
        name="span_attend",
    )(index, qkv, qkv, qkv, cache)


def finish_body(att_ref, datt_ref, x_ref, dx_ref, spread_ref, w_ref, out_ref, dout_ref, lhs):
    rows = att_ref.shape[0]
    k, kp = spread_ref.shape

    @pl.when(pl.program_id(0) == 0)
    def _():
        for g in range(att_ref.shape[1] // k):
            from_, to = slice(g * k, (g + 1) * k), slice(g * kp, (g + 1) * kp)
            lhs[:rows, to] = dot(att_ref[:, from_], spread_ref[...]).astype(BF16)
            lhs[rows:, to] = dot(datt_ref[:, from_], spread_ref[...]).astype(BF16)

    y = dot(lhs[...], w_ref[...])
    out_ref[...] = (x_ref[...].astype(F32) + y[:rows]).astype(BF16)
    dout_ref[...] = (dx_ref[...].astype(F32) + y[rows:]).astype(BF16)


def finish(att, datt, x, dx, spread, w):
    rows, width = x.shape
    drows = dx.shape[0]
    depth, n = w.shape
    bn = 512
    return pl.pallas_call(
        finish_body,
        grid=(n // bn,),
        in_specs=[
            pl.BlockSpec(att.shape, lambda i: (0, 0)),
            pl.BlockSpec(datt.shape, lambda i: (0, 0)),
            pl.BlockSpec((rows, bn), lambda i: (0, i)),
            pl.BlockSpec((drows, bn), lambda i: (0, i)),
            pl.BlockSpec(spread.shape, lambda i: (0, 0)),
            pl.BlockSpec((depth, bn), lambda i: (0, i)),
        ],
        out_specs=[
            pl.BlockSpec((rows, bn), lambda i: (0, i)),
            pl.BlockSpec((drows, bn), lambda i: (0, i)),
        ],
        out_shape=[
            jax.ShapeDtypeStruct((rows, n), BF16),
            jax.ShapeDtypeStruct((drows, n), BF16),
        ],
        scratch_shapes=[pltpu.VMEM((rows + drows, depth), BF16)],
        compiler_params=params(48, "arbitrary"),
        cost_estimate=pl.CostEstimate(
            flops=2 * rows * depth * n, bytes_accessed=2 * depth * n, transcendentals=0
        ),
        name="finish",
    )(att, datt, x, dx, spread, w)


def route(rows, to, devices):
    places = jnp.arange(devices * rows.shape[0], dtype=jnp.int32)
    sent = jnp.zeros((places.shape[0], rows.shape[1]), BF16)
    for i in range(rows.shape[0]):
        sent = jnp.where((places == to[i])[:, None], rows[i][None], sent)
    sent = sent.reshape(devices, rows.shape[0], rows.shape[1])
    return lax.all_to_all(sent, AXES, 0, 0)


def pick(arrived, came_from):
    each = arrived.shape[1]
    return jnp.concatenate(
        [
            lax.dynamic_slice(arrived, (came_from[i] // each, i, 0), (1, 1, arrived.shape[2]))[0]
            for i in range(each)
        ],
        0,
    )


def shards(
    devices,
    span_tokens,
    decode_tokens,
    norm_gain,
    query_weight,
    keyval_weight,
    output_weight,
    span_cache,
    decode_cache,
    span_index,
    decode_length,
    cache_slot,
):
    rows, width = span_tokens.shape[1:]
    own = decode_cache.shape[0]
    hd = keyval_weight.shape[1] // 2
    heads = query_weight.shape[1] // hd
    device = lax.axis_index(AXES)
    run = query_weight.shape[0]
    padded = -(-run // 8) * 8

    def gathered(w):
        return lax.all_gather(jnp.pad(w, ((0, padded - run), (0, 0))), AXES, axis=0, tiled=True)

    first_weight = gathered(jnp.concatenate([query_weight, keyval_weight], 1))
    spread = spreader(run, padded, 32)

    mine = device * own + jnp.arange(own, dtype=jnp.int32)
    slot_of_mine = lax.dynamic_slice_in_dim(cache_slot, device * own, own)
    request_of_mine = jnp.argmax(cache_slot[None, :] == mine[:, None], 1).astype(jnp.int32)
    digits = jnp.stack([decode_length // 256, decode_length % 256], 1).astype(BF16)
    tagged = jnp.concatenate([decode_tokens, jnp.pad(digits, ((0, 0), (0, 126)))], 1)
    arrived = pick(route(tagged, slot_of_mine, devices), request_of_mine)
    own_tokens = arrived[:, :width]
    tags = arrived[:, width : width + 2].astype(jnp.int32)
    own_length = tags[:, 0] * 256 + tags[:, 1]

    offset = span_index[0] * rows
    positions = jnp.concatenate(
        [offset + jnp.arange(rows, dtype=jnp.int32), own_length, jnp.zeros(EXTRA - own, jnp.int32)]
    )
    quarter = hd // 4
    frequency = 10000.0 ** (-jnp.arange(quarter, dtype=F32) / quarter)
    angles = positions.astype(F32)[:, None] * frequency
    cos, sin = jnp.cos(angles), jnp.sin(angles)
    cos = jnp.concatenate([cos, cos], 1)
    sin = jnp.concatenate([-sin, sin], 1)

    rows_all = jnp.concatenate([span_tokens[0], jnp.pad(own_tokens, ((0, EXTRA - own), (0, 0)))], 0)
    lhs = norm_spread(rows_all, norm_gain, spread)
    qkv = project(lhs, first_weight, cos, sin, hd)

    keyval = jnp.concatenate([qkv[heads], qkv[heads + 1]], 1)
    decode_keyval = keyval[rows : rows + own]
    decode_q = jnp.transpose(qkv[:heads, rows : rows + own], (1, 0, 2))
    decode_q = jnp.pad(decode_q, ((0, 0), (0, 16 - heads), (0, 0)))
    decode_mixed = decode_attend(own_length, decode_q, decode_keyval, decode_cache)
    decode_mixed = decode_mixed[:, :heads].reshape(own, width)
    home = route(decode_mixed, request_of_mine, devices)

    span_mixed = span_attend(span_index, qkv, rows, span_cache)
    home = jnp.pad(pick(home, slot_of_mine), ((0, EXTRA - own), (0, 0)))
    last_weight = gathered(output_weight)
    span_output, decode_output = finish(
        span_mixed,
        home,
        span_tokens[0],
        jnp.pad(decode_tokens, ((0, EXTRA - own), (0, 0))),
        spread,
        last_weight,
    )
    return span_output[None], keyval[:rows][None], decode_output[:own], decode_keyval


def solution(mesh):
    both = P(AXES)
    return jax.shard_map(
        functools.partial(shards, mesh.size),
        mesh=mesh,
        in_specs=(both, both, P(), both, both, both, both, both, both, both, P()),
        out_specs=(both, both, both, both),
        check_vma=False,
    )
```

time: 408 us -> 217 us (0.53)
  waiting for transfers between devices: 189 us -> 98.9 us
  blocking collectives: 69.1 us -> 0 us
  local copies, waits for them, and re-layouts: 78.9 us -> 11.3 us
  Pallas kernels: 0 us -> 46.5 us
  matrix products: 37.4 us -> 0 us
  starting transfers between devices: 0.19 us -> 19.7 us
  between operations: 14.7 us -> 25.4 us
    all_gather x5 -> x2, waiting for transfers between devices: 187 us -> 85 us  [gathered(): lax.all_gather(jnp.pad(w, ((0, padded - run), (0, 0))), AXES, axis=0, til...]
    unnamed x1 -> x0, blocking collectives: 69.1 us -> none
    pallas_call x0 -> x5, Pallas kernels: none -> 46.5 us  [the longest x1 16.4 us: span_attend(): pl.pallas_call(span_body, grid_spec=pltpu.PrefetchScalarGridSpec(num_scal...]
    unnamed x32 -> x28, local copies, waits for them, and re-layouts: 51.7 us -> 5.55 us
    dot_general x28 -> x0, matrix products: 37.4 us -> none  [the longest x1 8.85 us: shards(): jnp.dot(columns, lax.all_gather(output_weight, ('dp', 'mp'), axis=0, tile...]
    all_to_all x0 -> x2, starting transfers between devices: none -> 19.6 us  [route(): return lax.all_to_all(sent, AXES, 0, 0)]
    all_to_all x0 -> x2, waiting for transfers between devices: none -> 13.9 us  [route(): return lax.all_to_all(sent, AXES, 0, 0)]
    reduce_sum x13 -> x0, other arithmetic: 8.39 us -> none  [the longest x10 6.97 us: one_head(): jnp.sum(exp_terms, -1, keepdims=True)]
  transfers between devices with their start and end apart: 5 -> 4, of which waited for: 4 -> 3; matrix products, arithmetic and copies ran while one was open for 23% -> 8% of each run, Pallas kernels for 0% -> 16%
where the time goes in v1:
time: 217 us; the launch traced here: 216 us
  waiting for transfers between devices  98.9 us (46%)
  Pallas kernels  46.5 us (21%)
  between operations  25.4 us (12%)
  starting transfers between devices  19.7 us (9%)
  other arithmetic  14.4 us (7%)
  local copies, waits for them, and re-layouts  11.3 us (5%)
    all_gather x2, waiting for transfers between devices, gathered(): lax.all_gather(jnp.pad(w, ((0, padded - run), (0, 0))), AXES, axis=0, til...  85 us
    all_to_all x2, starting transfers between devices, route(): return lax.all_to_all(sent, AXES, 0, 0)  19.6 us
    pallas_call x1, Pallas kernels, span_attend(): pl.pallas_call(span_body, grid_spec=pltpu.PrefetchScalarGridSpec(num_scal...  16.4 us
    pallas_call x1, Pallas kernels, project(): pl.pallas_call(functools.partial(project_body, blocks - 1), grid=(blocks,...  13.9 us
    all_to_all x2, waiting for transfers between devices, route(): return lax.all_to_all(sent, AXES, 0, 0)  13.9 us
    pallas_call x1, Pallas kernels, finish(): pl.pallas_call(finish_body, grid=(n // bn,), in_specs=[pl.BlockSpec(att.s...  11.7 us
    select_n x2, other arithmetic, route(): sent = jnp.where((places == to[i])[:, None], rows[i][None], sent)  5.94 us
    unnamed x28, local copies, waits for them, and re-layouts  5.55 us
  transfers between devices with their start and end apart: 4, of which 3 were waited for; matrix products, arithmetic and copies ran while one was open for 8% of the time, Pallas kernels for 16%

profile of v1, /device:TPU:1, one launch (start us, length us, event | category | flops | bytes accessed | tf_op | source)
XLA Modules:
  0.0 216.1 jit_solution(2631887348395783466)
XLA Ops:
  7.2 0.0 all-gather.3.cloned.1.call-start
  7.2 1.6 fusion.8
  8.8 0.0 all-gather.3.cloned.1.call-update
  8.8 0.0 all-gather.5.cloned.1.call-start
  8.9 1.6 pad.32
  10.5 0.0 all-gather.5.cloned.1.call-update
  10.5 0.7 convert_bitcast_fusion
  11.2 0.1 copy.25
  11.3 0.8 dynamic_slice.15
  12.0 0.6 fusion.22
  12.6 1.3 fusion.12
  13.9 0.7 fusion.15
  14.7 0.1 slice_reduce_fusion.1
  14.7 3.0 %broadcast_select_fusion.1 = bf16[128,2,2688]{2,1,0:T(2,128)(2,1)} fusion(pred[128,2]{1,0:T(8,128)(4,1)S(1)} %get-tuple-element.30, pred[128,2]{1,0:T(8,128)(4,1)S(1)} %get-tuple-element.29, bf16[2688]{0:T(1024)(128)(2,1)S(1)} %get-tuple-element.11, bf16[2688]{0:T(1024)(128)(2,1)S(1)} %get-tuple-element.10), kind=kLoop, calls=%fused_computation.3 | loop fusion | flops 1376256 | bytes 1387520 | tf_op jit(solution)/shard_map/jit(_where)/select_n | solution.py:265
  17.8 0.0 copy-start.12
  17.8 0.0 copy-start.9
  17.8 0.0 copy-start.11
  17.8 0.0 copy-start
  17.8 11.9 %all-to-all-start = ((bf16[128,2,2688]{2,1,0:T(2,128)(2,1)}), bf16[128,2,2688]{2,1,0:T(2,128)(2,1)}, u32[]{:S(2)}, u32[]{:S(2)}) async-start(bf16[128,2,2688]{2,1,0:T(2,128)(2,1)} %broadcast_select_fusion.1), calls=%async_computation | async-start | bytes 2752512 | tf_op jit(solution)/shard_map/all_to_all | solution.py:267
  29.7 0.0 copy-done.12
  29.7 0.7 compare_reduce_fusion
  30.4 0.6 fusion.21
  36.8 0.0 copy-done.9
  36.8 1.3 fusion.10
  38.1 0.0 copy-done.11
  38.2 0.2 fusion.1.spread_ref
  38.4 13.8 %all-to-all-done = bf16[128,2,2688]{2,1,0:T(2,128)(2,1)} async-done(((bf16[128,2,2688]{2,1,0:T(2,128)(2,1)}), bf16[128,2,2688]{2,1,0:T(2,128)(2,1)}, u32[]{:S(2)}, u32[]{:S(2)}) %all-to-all-start) | async-done | bytes 1376288 | tf_op jit(solution)/shard_map/all_to_all | solution.py:267
  52.2 0.7 dynamic-slice_bitcast_fusion
  53.0 0.0 copy-done
  53.0 0.1 fusion.2.x_ref
  53.1 1.8 norm_spread.1.x_ref
  54.9 0.2 add_reduce_fusion.len_ref
  55.1 0.1 add_convert_fusion
  55.2 0.6 fusion.14
  55.7 0.1 pad_maximum_fusion.1.cos_ref
  55.9 0.1 pad_maximum_fusion.2.sin_ref
  56.0 52.1 %all-gather.3.cloned.1.call-done.w_ref = bf16[3072,3072]{1,0:T(8,128)(2,1)} async-done(((bf16[24,3072]{1,0:T(8,128)(2,1)}), bf16[3072,3072]{1,0:T(8,128)(2,1)}) %all-gather.3.cloned.1.call-update) | async-done | bytes 18874384 | tf_op jit(solution)/shard_map/all_gather | solution.py:304
  108.1 0.0 copy-start.2
  108.1 13.9 %project.1.q_ref.k_ref.v_ref = bf16[12,272,256]{2,1,0:T(8,128)(2,1)S(1)} custom-call(bf16[272,3072]{1,0:T(8,128)(2,1)S(1)} %norm_spread.1.x_ref, bf16[3072,3072]{1,0:T(8,128)(2,1)} %all-gather.3.cloned.1.call-done.w_ref, f32[272,128]{1,0:T(8,128)S(1)} %pad_maximum_fusion.1.cos_ref, f32[272,128]{1,0:T(8,128)S(1)} %pad_maximum_fusion.2.sin_ref), custom_call_target="tpu_custom_call" | custom-call | flops 5133828096 | bytes 18874368 | tf_op jit(solution)/shard_map/project/pallas_call | solution.py:79
  122.0 0.0 copy-start.3
  122.1 0.0 copy-start.10
  122.1 0.0 copy-done.2
  122.1 2.7 %decode_attend.1 = bf16[2,16,256]{2,1,0:T(8,128)(2,1)S(1)} custom-call(s32[2]{0:T(128)S(1)} %add_reduce_fusion.len_ref, bf16[2,16,256]{2,1,0:T(8,128)(2,1)S(1)} %pad.29.q_ref, bf16[2,1,512]{2,1,0:T(2,128)(2,1)S(1)} %copy.23.own_ref, bf16[2,2048,512]{2,1,0:T(8,128)(2,1)S(1)} %copy-done.2), custom_call_target="tpu_custom_call" | custom-call | flops 67108864 | bytes 4194304 | tf_op jit(solution)/shard_map/decode_attend/pallas_call | solution.py:123
  124.8 0.0 copy-done.3
  124.8 0.0 copy-done.10
  124.9 2.9 %broadcast_select_fusion.3 = bf16[128,2,2560]{2,1,0:T(2,128)(2,1)} fusion(pred[128,2]{1,0:T(8,128)(4,1)S(1)} %get-tuple-element.32, pred[128,2]{1,0:T(8,128)(4,1)S(1)} %get-tuple-element.31, bf16[2560]{0:T(1024)(128)(2,1)S(1)} %broadcast_in_dim.101, bf16[2560]{0:T(1024)(128)(2,1)S(1)} %broadcast_in_dim.98), kind=kLoop, calls=%fused_computation.5 | loop fusion | flops 1310720 | bytes 1321472 | tf_op jit(solution)/shard_map/jit(_where)/select_n | solution.py:265
  127.8 0.0 copy-start.8
  127.8 7.7 %all-to-all-start.1 = ((bf16[128,2,2560]{2,1,0:T(2,128)(2,1)}), bf16[128,2,2560]{2,1,0:T(2,128)(2,1)}, u32[]{:S(2)}, u32[]{:S(2)}) async-start(bf16[128,2,2560]{2,1,0:T(2,128)(2,1)} %broadcast_select_fusion.3), calls=%async_computation.1 | async-start | bytes 2621440 | tf_op jit(solution)/shard_map/all_to_all | solution.py:267
  140.7 0.0 copy-done.8
  140.7 0.7 fusion.5
  141.5 0.0 copy-start.4
  141.5 1.4 copy-done.4
  142.9 0.0 copy-start.7
  142.9 1.6 copy-done.7
  144.5 16.4 %span_attend.1.att_ref = bf16[256,2560]{1,0:T(8,128)(2,1)S(1)} custom-call(s32[1]{0:T(128)S(6)} %copy.28.index_ref, bf16[12,272,256]{2,1,0:T(8,128)(2,1)S(1)} %copy-done.4, bf16[12,272,256]{2,1,0:T(8,128)(2,1)S(1)} %copy-done.4, bf16[12,272,256]{2,1,0:T(8,128)(2,1)S(1)} %copy-done.4, bf16[1,2048,512]{2,1,0:T(8,128)(2,1)S(1)} %copy-done.7), custom_call_target="tpu_custom_call" | custom-call | flops 6039797760 | bytes 2097152 | tf_op jit(solution)/shard_map/span_attend/pallas_call | solution.py:188
  160.9 0.0 copy-start.5
  160.9 1.0 copy-done.5
  162.0 0.0 all-to-all-done.1
  162.0 0.7 dynamic-slice_bitcast_fusion.3
  162.8 32.9 %all-gather.5.cloned.1.call-done.w_ref = bf16[3072,2560]{1,0:T(8,128)(2,1)} async-done(((bf16[24,2560]{1,0:T(8,128)(2,1)}), bf16[3072,2560]{1,0:T(8,128)(2,1)}) %all-gather.5.cloned.1.call-update) | async-done | bytes 15728656 | tf_op jit(solution)/shard_map/all_gather | solution.py:304
  195.7 0.0 copy-done.1
  195.7 1.3 copy-done.6
  197.0 11.7 %finish.1 = (bf16[256,2560]{1,0:T(8,128)(2,1)}, bf16[16,2560]{1,0:T(8,128)(2,1)S(1)}) custom-call(bf16[256,2560]{1,0:T(8,128)(2,1)S(1)} %copy-done.6, bf16[16,2560]{1,0:T(8,128)(2,1)S(1)} %fusion.9.datt_ref, bf16[256,2560]{1,0:T(8,128)(2,1)S(1)} %bitcast.30, bf16[16,2560]{1,0:T(8,128)(2,1)S(1)} %pad.31.dx_ref, bf16[640,768]{1,0:T(8,128)(2,1)S(1)} %fusion.1.spread_ref, ...), custom_call_target="tpu_custom_call" | custom-call | flops 4026531840 | bytes 15728640 | tf_op jit(solution)/shard_map/finish/pallas_call | solution.py:233
  208.7 0.6 slice.80
  (21 shorter events, 0.2 us)
Async XLA Ops:
  7.2 100.9 %all-gather.3.cloned.1.call-start = ((), (), s32[]{:S(2)}) async-start(), calls=%async_computation.2 | async-start | bytes 19021824 | tf_op jit(solution)/shard_map/all_gather | solution.py:304
  8.8 186.9 %all-gather.5.cloned.1.call-start = ((), (), s32[]{:S(2)}) async-start(), calls=%async_computation.3 | async-start | bytes 15851520 | tf_op jit(solution)/shard_map/all_gather | solution.py:304
  17.8 11.9 %copy-start.12 = (s32[256]{0:T(256)S(1)}, s32[256]{0:T(256)}, u32[]{:S(2)}) copy-start(s32[256]{0:T(256)} %param.22) | copy-start | bytes 3076
  17.8 19.0 %copy-start.9 = (f32[2560]{0:T(1024)S(1)}, f32[2560]{0:T(1024)}, u32[]{:S(2)}) copy-start(f32[2560]{0:T(1024)} %param.14) | copy-start | bytes 30724
  17.8 20.4 %copy-start.11 = (s32[640]{0:T(1024)S(1)}, s32[640]{0:T(1024)}, u32[]{:S(2)}) copy-start(s32[640]{0:T(1024)} %constant.100.clone) | copy-start | bytes 7684
  17.8 35.2 %copy-start = (bf16[1,256,2560]{2,1,0:T(8,128)(2,1)S(1)}, bf16[1,256,2560]{2,1,0:T(8,128)(2,1)}, u32[]{:S(2)}) copy-start(bf16[1,256,2560]{2,1,0:T(8,128)(2,1)} %param.12) | copy-start | bytes 3932164
  17.8 34.5 %all-to-all-start = ((bf16[128,2,2688]{2,1,0:T(2,128)(2,1)}), bf16[128,2,2688]{2,1,0:T(2,128)(2,1)}, u32[]{:S(2)}, u32[]{:S(2)}) async-start(bf16[128,2,2688]{2,1,0:T(2,128)(2,1)} %broadcast_select_fusion.1), calls=%async_computation | async-start | bytes 2752512 | tf_op jit(solution)/shard_map/all_to_all | solution.py:267
  108.1 14.1 %copy-start.2 = (bf16[2,2048,512]{2,1,0:T(8,128)(2,1)S(1)}, bf16[2,2048,512]{2,1,0:T(8,128)(2,1)}, u32[]{:S(2)}) copy-start(bf16[2,2048,512]{2,1,0:T(8,128)(2,1)} %cache_ref.3) | copy-start | bytes 12582916
  122.0 2.8 %copy-start.3 = (bf16[12,272,256]{2,1,0:T(8,128)(2,1)}, bf16[12,272,256]{2,1,0:T(8,128)(2,1)S(1)}, u32[]{:S(2)}) copy-start(bf16[12,272,256]{2,1,0:T(8,128)(2,1)S(1)} %project.1.q_ref.k_ref.v_ref) | copy-start | bytes 5013508
  122.1 2.8 %copy-start.10 = (bf16[2,512]{1,0:T(2,128)(2,1)}, bf16[2,512]{1,0:T(2,128)(2,1)S(1)}, u32[]{:S(2)}) copy-start(bf16[2,512]{1,0:T(2,128)(2,1)S(1)} %pad_maximum_fusion.3) | copy-start | bytes 6148
  127.8 12.9 %copy-start.8 = (bf16[2,2560]{1,0:T(2,128)(2,1)S(1)}, bf16[2,2560]{1,0:T(2,128)(2,1)}, u32[]{:S(2)}) copy-start(bf16[2,2560]{1,0:T(2,128)(2,1)} %param.13) | copy-start | bytes 30724
  127.8 34.2 %all-to-all-start.1 = ((bf16[128,2,2560]{2,1,0:T(2,128)(2,1)}), bf16[128,2,2560]{2,1,0:T(2,128)(2,1)}, u32[]{:S(2)}, u32[]{:S(2)}) async-start(bf16[128,2,2560]{2,1,0:T(2,128)(2,1)} %broadcast_select_fusion.3), calls=%async_computation.1 | async-start | bytes 2621440 | tf_op jit(solution)/shard_map/all_to_all | solution.py:267
  141.5 1.4 copy-start.4
  142.9 1.6 copy-start.7
  144.5 51.2 %copy-start.1 = (bf16[1,256,2560]{2,1,0:T(8,128)(2,1)S(1)}, bf16[1,256,2560]{2,1,0:T(8,128)(2,1)}, u32[]{:S(2)}) copy-start(bf16[1,256,2560]{2,1,0:T(8,128)(2,1)} %param.12) | copy-start | bytes 3932164
  160.9 1.1 copy-start.5
  195.7 1.3 copy-start.6
Sparse Core Ops, SparseCore 0:
  11.7 96.3 all-gather.2
  111.2 84.4 all-gather.4

commit v2 on v1

v2 whole, which is shorter than its diff:
```python
import functools

import jax
import jax.numpy as jnp
import numpy as np
from jax import lax
from jax.experimental import pallas as pl
from jax.experimental.pallas import tpu as pltpu
from jax.sharding import Mesh
from jax.sharding import PartitionSpec as P

AXES = ("y", "c", "x", "z")
CHIPS = ("y", "x", "z")
LOG2E = 1.4426950408889634
NEG = -1e30
F32 = jnp.float32
BF16 = jnp.bfloat16
EXTRA = 16


def params(mib, *semantics):
    return pltpu.CompilerParams(vmem_limit_bytes=mib << 20, dimension_semantics=semantics or None)


def dot(a, b):
    return jnp.dot(a, b, preferred_element_type=F32)


def dot_t(a, b):
    return lax.dot_general(a, b, (((1,), (1,)), ((), ())), preferred_element_type=F32)


def mover(to, width):
    return (jnp.asarray(to, jnp.int32)[:, None] == jnp.arange(width)[None, :]).astype(BF16)


def arrival_order(run):
    core, x, z, r = np.meshgrid(*(np.arange(n) for n in (2, 4, 4, run)), indexing="ij")
    return mover((((x * 4 + z) * 2 + core) * run + r).reshape(-1), 32 * run)


def norm_body(x_ref, gain_ref, order_ref, *refs):
    out_ref = refs[-1]
    x = x_ref[...].astype(F32)
    rows = x.shape[0]
    mean = jnp.mean(x * x, axis=-1, keepdims=True)
    normed = (x * lax.rsqrt(mean + 1e-06) * gain_ref[...]).astype(BF16)
    k = order_ref.shape[0]
    blocks = jnp.concatenate([normed[:, y * k : (y + 1) * k] for y in range(4)], 0)
    moved = dot(blocks, order_ref[...]).astype(BF16)
    for y in range(4):
        out_ref[:, y * k : (y + 1) * k] = moved[y * rows : (y + 1) * rows]


def norm_ordered(x, gain, order, total, block, at, into=()):
    rows, width = x.shape
    return pl.pallas_call(
        norm_body,
        grid=(rows // block,),
        in_specs=[
            pl.BlockSpec((block, width), lambda i: (i, 0)),
            pl.BlockSpec((1, width), lambda i: (0, 0)),
            pl.BlockSpec(order.shape, lambda i: (0, 0)),
        ]
        + [pl.BlockSpec(memory_space=pl.ANY)] * len(into),
        out_specs=pl.BlockSpec((block, width), lambda i: (at + i, 0)),
        out_shape=jax.ShapeDtypeStruct((total, width), BF16),
        input_output_aliases={3 + i: i for i in range(len(into))},
        compiler_params=params(24, "arbitrary"),
        cost_estimate=pl.CostEstimate(
            flops=2 * rows * width * 640, bytes_accessed=4 * rows * width, transcendentals=0
        ),
        name="norm_ordered",
    )(x, gain[None], order, *into)


def rotate(v, cos_ref, sin_ref):
    half = v[:, :128]
    turned = half * cos_ref[...] + pltpu.roll(half, 64, 1) * sin_ref[...]
    return jnp.concatenate([turned, v[:, 128:]], 1)


def project_body(rows, x_ref, w_ref, cos_ref, sin_ref, ours_ref, other_ref):
    extra = ours_ref.shape[1] - rows
    made = rotate(dot(x_ref[...], w_ref[...]), cos_ref.at[0], sin_ref.at[0]).astype(BF16)
    ours_ref[0, :rows] = made[:rows]
    other_ref[0, :rows] = made[rows : 2 * rows]
    ours_ref[0, rows:] = made[2 * rows : 2 * rows + extra]
    other_ref[0, rows:] = made[2 * rows + extra :]


def project(first, count, rows, x, w, cos, sin, hd):
    total, depth = x.shape
    last = w.shape[1] // hd - 1
    shape = jax.ShapeDtypeStruct((count, total // 2, hd), BF16)
    table = pl.BlockSpec((1, total, 128), lambda i: ((first + i) // last, 0, 0))
    return pl.pallas_call(
        functools.partial(project_body, rows),
        grid=(count,),
        in_specs=[
            pl.BlockSpec((total, depth), lambda i: (0, 0)),
            pl.BlockSpec((depth, hd), lambda i: (0, first + i)),
            table,
            table,
        ],
        out_specs=[pl.BlockSpec((1, total // 2, hd), lambda i: (i, 0, 0))] * 2,
        out_shape=[shape, shape],
        compiler_params=params(32, "arbitrary"),
        cost_estimate=pl.CostEstimate(
            flops=2 * total * count * depth * hd,
            bytes_accessed=2 * count * depth * hd,
            transcendentals=0,
        ),
        name="project",
    )(x, w, cos, sin)


SLAB = 24


def decode_body(
    info_ref, oab_ref, oc_ref, tab_ref, tc_ref, own_ref, cache_ref, out_ref, gather_ref, spill_ref
):
    i = pl.program_id(0)
    length, to, core = info_ref[i], info_ref[2 + i], info_ref[4]
    hd = cache_ref.shape[2] // 2
    window = cache_ref.shape[1]
    for half, (ab_ref, c_ref) in enumerate(((oab_ref, oc_ref), (tab_ref, tc_ref))):
        for h in range(5):
            block = ab_ref[h] if h < 4 else c_ref[0]
            block = block.astype(F32)
            row = jnp.where(i == 0, block[0:1], block[1:2])
            gather_ref[half * 5 + h : half * 5 + h + 1] = row
    gather_ref[10:16] = jnp.zeros((6, hd), F32)
    q = gather_ref[...].astype(BF16)
    scores = dot_t(q, cache_ref[0, :, :hd])
    own_row = own_ref[...].astype(F32)
    own_row = jnp.where(i == 0, own_row[0:1], own_row[1:2])
    own = jnp.sum(gather_ref[...] * own_row[:, :hd], axis=1, keepdims=True)
    slot = lax.broadcasted_iota(jnp.int32, scores.shape, 1)
    met = (slot < length) & (slot != lax.rem(length, window))
    scores = jnp.where(met, scores, NEG)
    top = jnp.maximum(jnp.max(scores, 1, keepdims=True), own)
    scale = LOG2E * hd**-0.5
    terms = jnp.where(met, jnp.exp2((scores - top) * scale), 0.0)
    own_term = jnp.exp2((own - top) * scale)
    total = jnp.sum(terms, 1, keepdims=True) + own_term
    weights = (terms / total).astype(BF16)
    own_weight = (own_term / total).astype(BF16).astype(F32)
    mixed = dot(weights, cache_ref[0, :, hd:]) + own_weight * own_row[:, hd:]
    spill_ref[20:] = jnp.zeros((SLAB - 20, 128), F32)
    for h in range(10):
        head = jnp.where(core == 0, h, (h + 5) % 10)
        for part in range(2):
            spill_ref[pl.ds(2 * head + part, 1)] = mixed[h : h + 1, part * 128 : part * 128 + 128]
    out_ref[to] = spill_ref[...].astype(BF16)


def decode_attend(info, parts, own, cache, places):
    n, window, wide = cache.shape
    hd = wide // 2
    last = parts[0].shape[1] // EXTRA - 1
    return pl.pallas_call(
        decode_body,
        grid_spec=pltpu.PrefetchScalarGridSpec(
            num_scalar_prefetch=1,
            grid=(n,),
            in_specs=[
                pl.BlockSpec((p.shape[0], EXTRA, hd), lambda i, s: (0, last, 0)) for p in parts
            ]
            + [
                pl.BlockSpec((EXTRA, wide), lambda i, s: (last, 0)),
                pl.BlockSpec((1, window, wide), lambda i, s: (i, 0, 0)),
            ],
            out_specs=pl.BlockSpec((places, SLAB, 128), lambda i, s: (0, 0, 0)),
            scratch_shapes=[pltpu.VMEM((16, hd), F32), pltpu.VMEM((SLAB, 128), F32)],
        ),
        out_shape=jax.ShapeDtypeStruct((places, SLAB, 128), BF16),
        compiler_params=params(24, "arbitrary"),
        cost_estimate=pl.CostEstimate(
            flops=64 * n * hd * window, bytes_accessed=4 * n * hd * window, transcendentals=0
        ),
        name="decode_attend",
    )(info, *parts, own, cache)


def interleave_body(z_ref, *refs):
    pieces, out_ref = refs[:4], refs[4]
    run = pieces[0].shape[0] // 2
    for z in range(4):

        @pl.when(z_ref[0] == z)
        def _():
            for core in range(2):
                rows = [
                    pieces[(z - at) % 4][core * run : (core + 1) * run].astype(F32) for at in range(4)
                ]
                out_ref[core] = jnp.concatenate(rows, 0).astype(BF16)


def interleave(z, pieces):
    rows, cols = pieces[0].shape
    vmem = pl.BlockSpec(memory_space=pltpu.VMEM)
    return pl.pallas_call(
        interleave_body,
        in_specs=[pl.BlockSpec(memory_space=pltpu.SMEM)] + [vmem] * 4,
        out_specs=vmem,
        out_shape=jax.ShapeDtypeStruct((2, 2 * rows, cols), BF16),
        compiler_params=params(8),
        name="interleave",
    )(z, *pieces)


def place_body(to_ref, rows_ref, out_ref):
    for i in range(rows_ref.shape[0]):
        out_ref[to_ref[i]] = rows_ref[i]


def place(rows, to, places):
    return pl.pallas_call(
        place_body,
        in_specs=[pl.BlockSpec(memory_space=pltpu.SMEM), pl.BlockSpec(memory_space=pltpu.VMEM)],
        out_specs=pl.BlockSpec(memory_space=pltpu.VMEM),
        out_shape=jax.ShapeDtypeStruct((places,) + rows.shape[1:], BF16),
        compiler_params=params(8),
        name="place",
    )(to, rows)


def pick_body(came_ref, slab_ref, out_ref):
    out_ref[...] = slab_ref[...]


def pick(arrived, came_from):
    slab = arrived.shape[1:]
    return pl.pallas_call(
        pick_body,
        grid_spec=pltpu.PrefetchScalarGridSpec(
            num_scalar_prefetch=1,
            grid=(2,),
            in_specs=[
                pl.BlockSpec((1,) + slab, lambda i, s: (lax.shift_right_logical(s[i], 1) * 2 + i, 0, 0))
            ],
            out_specs=pl.BlockSpec((1,) + slab, lambda i, s: (i, 0, 0)),
        ),
        out_shape=jax.ShapeDtypeStruct((2,) + slab, BF16),
        compiler_params=params(8, "arbitrary"),
        name="pick",
    )(came_from, arrived)


def span_body(index_ref, ab_ref, c_ref, k_ref, v_ref, cache_ref, out_ref):
    index = index_ref[0]
    q = jnp.where(pl.program_id(0) < pl.num_programs(0) - 1, ab_ref[0], c_ref[0])
    rows, hd = q.shape
    blocks = cache_ref.shape[1] // rows
    wrapped = index >= blocks
    row = lax.broadcasted_iota(jnp.int32, (rows, rows), 0)
    col = lax.broadcasted_iota(jnp.int32, (rows, rows), 1)
    own = col <= row
    starts, scores, shifts = [], [], []
    top = None
    for rel in range(blocks):
        block = lax.rem(index + rel, blocks)
        start = pl.multiple_of(block * rows, rows)
        starts.append(start)
        s = dot_t(q, cache_ref[0, pl.ds(start, rows), :hd])
        if rel == 0:
            s = jnp.where(own, dot_t(q, k_ref[...]), jnp.where(wrapped, s, NEG))
            shift = jnp.float32(0)
        else:
            shift = jnp.where(wrapped | (block < index), jnp.float32(0), jnp.float32(NEG))
        scores.append(s)
        shifts.append(shift)
        peak = jnp.max(s, 1, keepdims=True) + shift
        top = peak if top is None else jnp.maximum(top, peak)
    scale = LOG2E * hd**-0.5
    base = top * scale
    total = jnp.zeros((rows, 1), F32)
    mixed = jnp.zeros((rows, hd), F32)
    for rel in range(blocks):
        terms = jnp.exp2(scores[rel] * scale - (base - shifts[rel]))
        total += jnp.sum(terms, 1, keepdims=True)
        old_values = cache_ref[0, pl.ds(starts[rel], rows), hd:]
        if rel == 0:
            mixed += dot(jnp.where(own, terms, 0.0).astype(BF16), v_ref[...])
            mixed += dot(jnp.where(own, 0.0, terms).astype(BF16), old_values)
        else:
            mixed += dot(terms.astype(BF16), old_values)
    out_ref[...] = (mixed / total).astype(BF16)


def span_attend(index, ab, c, key, value, rows, cache):
    heads, hd = ab.shape[0] + 1, ab.shape[2]
    window = cache.shape[1]
    return pl.pallas_call(
        span_body,
        grid_spec=pltpu.PrefetchScalarGridSpec(
            num_scalar_prefetch=1,
            grid=(heads,),
            in_specs=[
                pl.BlockSpec((1, rows, hd), lambda h, s: (jnp.minimum(h, heads - 2), 0, 0)),
                pl.BlockSpec((1, rows, hd), lambda h, s: (0, 0, 0)),
                pl.BlockSpec((rows, hd), lambda h, s: (0, 0)),
                pl.BlockSpec((rows, hd), lambda h, s: (0, 0)),
                pl.BlockSpec((1, window, 2 * hd), lambda h, s: (0, 0, 0)),
            ],
            out_specs=pl.BlockSpec((rows, hd), lambda h, s: (0, h)),
        ),
        out_shape=jax.ShapeDtypeStruct((rows, heads * hd), BF16),
        compiler_params=params(32, "arbitrary"),
        cost_estimate=pl.CostEstimate(
            flops=4 * heads * rows * hd * (window + rows),
            bytes_accessed=4 * hd * window,
            transcendentals=heads * rows * window,
        ),
        name="span_attend",
    )(index, ab, c, key, value, cache)


def finish_body(
    info_ref, att1_ref, att2_ref, datt_ref, x_ref, dx_ref, *refs
):
    chunks, (out_ref, dout_ref, lhs, w, sem) = refs[:16], refs[16:]
    rows, k = att1_ref.shape
    step = pl.program_id(0)
    core = info_ref[0]

    def copies(quarter):
        for i in range(4):
            place = info_ref[1 + quarter * 4 + i]
            if quarter % 2:
                to = w.at[quarter, place]
            else:
                to = w.at[quarter, :, :, place]
            yield pltpu.make_async_copy(chunks[quarter * 4 + i], to, sem.at[quarter, i])

    @pl.when(step == 0)
    def _():
        for quarter in range(4):
            for copy in copies(quarter):
                copy.start()
        lhs[core, :rows] = att1_ref[...]
        lhs[1 - core, :rows] = att2_ref[...]
        lhs[0, rows:] = datt_ref[:, :k]
        lhs[1, rows:] = datt_ref[:, k:]

    for quarter in range(4):

        @pl.when(step == quarter)
        def _():
            for copy in copies(quarter):
                copy.wait()

    total = None
    for half in range(2):
        right = w[step, 2 * half : 2 * half + 2].reshape(k, w.shape[-1])
        term = dot(lhs[half], right)
        total = term if total is None else total + term
    out_ref[...] = (x_ref[...].astype(F32) + total[:rows]).astype(BF16)
    dout_ref[...] = (dx_ref[...].astype(F32) + total[rows:]).astype(BF16)


def finish(info, att1, att2, datt, x, dx, chunks):
    rows, n = x.shape
    drows = dx.shape[0]
    run, bn = chunks[0].shape[2:]

    def column(i, s):
        return 0, lax.rem(s[0] * 2 + i, 4)

    return pl.pallas_call(
        finish_body,
        grid_spec=pltpu.PrefetchScalarGridSpec(
            num_scalar_prefetch=1,
            grid=(4,),
            in_specs=[
                pl.BlockSpec(att1.shape, lambda i, s: (0, 0)),
                pl.BlockSpec(att2.shape, lambda i, s: (0, 0)),
                pl.BlockSpec(datt.shape, lambda i, s: (0, 0)),
                pl.BlockSpec((rows, bn), column),
                pl.BlockSpec((drows, bn), column),
            ]
            + [pl.BlockSpec(memory_space=pl.ANY)] * 16,
            out_specs=[pl.BlockSpec((rows, bn), column), pl.BlockSpec((drows, bn), column)],
            scratch_shapes=[
                pltpu.VMEM((2, rows + drows, n // 2), BF16),
                pltpu.VMEM((4, 4, 2, 4, run, bn), BF16),
                pltpu.SemaphoreType.DMA((4, 4)),
            ],
        ),
        out_shape=[
            jax.ShapeDtypeStruct((rows, n), BF16),
            jax.ShapeDtypeStruct((drows, n), BF16),
        ],
        compiler_params=params(48, "arbitrary"),
        cost_estimate=pl.CostEstimate(
            flops=2 * rows * n * n, bytes_accessed=2 * n * n, transcendentals=0
        ),
        name="finish",
    )(info, att1, att2, datt, x, dx, *chunks)


def exchange(sent, devices):
    got = lax.all_to_all(sent.reshape((devices, -1) + sent.shape[1:]), AXES, 0, 0)
    return got.reshape(sent.shape)


STRIDE = {"y": 32, "x": 4, "z": 1}
DEVICES = np.arange(128)


def spot(axis):
    return DEVICES // STRIDE[axis] % 4


def send(v, axis, by):
    at = spot(axis)
    to = DEVICES + ((at + by) % 4 - at) * STRIDE[axis]
    return lax.ppermute(v, AXES, list(zip(DEVICES.tolist(), to.tolist())))


def swap(v):
    return lax.ppermute(v, AXES, list(zip(DEVICES.tolist(), (DEVICES ^ 16).tolist())))


RING = np.where(DEVICES // 16 % 2 == 0, 1, 3)


def put(whole, piece, index, place):
    start = [jnp.uint32(0)] * whole.ndim
    start[place] = index
    return lax.dynamic_update_slice(whole, jnp.expand_dims(piece, place), start)


def shards(
    devices,
    span_tokens,
    decode_tokens,
    norm_gain,
    query_weight,
    keyval_weight,
    output_weight,
    span_cache,
    decode_cache,
    span_index,
    decode_length,
    cache_slot,
):
    rows, width = span_tokens.shape[1:]
    own = decode_cache.shape[0]
    hd = keyval_weight.shape[1] // 2
    device = lax.axis_index(AXES).astype(jnp.uint32)
    core = ((device >> 4) & 1).astype(jnp.int32)
    first_core = core == 0
    run = query_weight.shape[0]

    half_q, half_kv = width // 2, hd
    halves = [
        jnp.concatenate(
            [
                query_weight[:, i * half_q : (i + 1) * half_q],
                keyval_weight[:, i * half_kv : (i + 1) * half_kv],
                output_weight[:, i * half_q : (i + 1) * half_q],
            ],
            1,
        )
        for i in range(2)
    ]
    got = swap(jnp.where(first_core, halves[1], halves[0]))
    piece = jnp.where(
        first_core, jnp.concatenate([halves[0], got], 0), jnp.concatenate([got, halves[1]], 0)
    )
    places = devices * own
    slots_here = (device * own).astype(jnp.int32) + jnp.arange(own, dtype=jnp.int32)
    slot_of_mine = lax.dynamic_slice(cache_slot, (device * own,), (own,))
    request_of_mine = jnp.argmax(cache_slot[None, :] == slots_here[:, None], 1).astype(jnp.int32)
    digits = jnp.stack([decode_length // 256, decode_length % 256], 1).astype(BF16)
    tagged = jnp.concatenate([decode_tokens, jnp.pad(digits, ((0, 0), (0, 510)))], 1)
    tagged = tagged.reshape(own, SLAB, 128)
    tagged = place(tagged, slot_of_mine, places)

    split = half_q + half_kv
    first_weight = lax.all_gather(piece[:, :split], CHIPS, axis=0, tiled=True)

    here = {axis: (device >> shift) & 3 for axis, shift in (("y", 5), ("x", 2), ("z", 0))}
    back = 1 - 2 * ((device >> 4) & 1)
    came = {axis: [(at - back * k) & 3 for k in range(4)] for axis, at in here.items()}
    strip, tagged = lax.optimization_barrier((piece[:, split:], tagged))
    strips = [strip] + [send(strip, "z", k) for k in (1, 2, 3)]
    strips = interleave(here["z"].astype(jnp.int32)[None], strips)
    bn = half_q // 2
    stack = [strips[:, :, :bn], strips[:, :, bn:]]
    plan = (("y", 0, "x", 2), ("x", 1, "y", 0))
    parts = [
        jnp.zeros((4, 2, 4 * run, bn), BF16),
        jnp.zeros((2, 4, 4 * run, bn), BF16),
    ]
    for k in range(4):
        for i, (axis, dim, _, _) in enumerate(plan):
            stack[i] = send(stack[i], axis, RING) if k else stack[i]
            parts[i] = put(parts[i], stack[i], came[axis][k], dim)
    arrived = pick(exchange(tagged, devices), request_of_mine)
    arrived = arrived.reshape(own, SLAB * 128)
    own_tokens = jnp.pad(arrived[:, :width], ((0, EXTRA - own), (0, 0)))
    tags = arrived[:, width : width + 2].astype(jnp.int32)
    own_length = tags[:, 0] * 256 + tags[:, 1]

    offset = span_index[0] * rows
    span_positions = offset + jnp.arange(rows, dtype=jnp.int32)
    decode_positions = jnp.pad(own_length, (0, EXTRA - own))
    positions = jnp.concatenate(
        [span_positions, swap(span_positions), decode_positions, swap(decode_positions)]
    )
    quarter = hd // 4
    frequency = 10000.0 ** (-jnp.arange(quarter, dtype=F32) / quarter)
    angles = positions.astype(F32)[:, None] * frequency
    cos, sin = jnp.cos(angles), jnp.sin(angles)
    cos = jnp.concatenate([cos, cos], 1)
    sin = jnp.concatenate([-sin, sin], 1)
    cos = jnp.stack([cos, jnp.where(first_core, cos, 1.0)])
    sin = jnp.stack([sin, jnp.where(first_core, sin, 0.0)])

    order = arrival_order(run)
    both_spans = jnp.concatenate([span_tokens[0], swap(span_tokens[0])], 0)
    both_decodes = jnp.concatenate([own_tokens, swap(own_tokens)], 0)
    total = 2 * (rows + EXTRA)
    lhs = norm_ordered(both_spans, norm_gain, order, total, 128, 0)
    at = 2 * rows // (2 * EXTRA)
    lhs = norm_ordered(both_decodes, norm_gain, order, total, 2 * EXTRA, at, (lhs,))
    mine = [[part] for part in parts]
    theirs = [[swap(part)] for part in parts]
    for k in (1, 2, 3):
        if k == 2:
            parts, lhs, cos, sin = lax.optimization_barrier((parts, lhs, cos, sin))
        parts = [send(part, p[2], RING) for part, p in zip(parts, plan)]
        for i in range(2):
            mine[i].append(parts[i])
            if k < 3:
                theirs[i].append(swap(parts[i]))
    ours_c, other_c = project(4, 2, rows, lhs, first_weight, cos, sin, hd)
    theirs_c = swap(other_c)
    ours_ab, other_ab = project(0, 4, rows, lhs, first_weight, cos, sin, hd)
    theirs_ab = swap(other_ab)
    parts, ours_ab = lax.optimization_barrier((parts, ours_ab))
    for i in range(2):
        theirs[i].append(swap(parts[i]))

    key = jnp.where(first_core, ours_c[1], theirs_c[1])
    value = jnp.where(first_core, theirs_c[1], ours_c[1])
    keyval = jnp.concatenate([key, value], 1)
    decode_keyval = keyval[rows : rows + own]
    info = jnp.concatenate([own_length, request_of_mine, core[None]])
    quarters = (ours_ab, ours_c, theirs_ab, theirs_c)
    home = exchange(decode_attend(info, quarters, keyval, decode_cache, places), devices)
    att1 = span_attend(span_index, ours_ab, ours_c, key, value, rows, span_cache)
    att2 = span_attend(span_index, theirs_ab, theirs_c, key, value, rows, span_cache)
    home = pick(home, slot_of_mine).reshape(own, SLAB * 128)[:, :width]
    shifts = jnp.asarray([2] * 4 + [5] * 4 + [2] * 4 + [5] * 4, jnp.int32)
    steps = jnp.asarray([0, 1, 2, 3] * 2 + [0, -1, -2, -3] * 2, jnp.int32)
    came_from = (((device.astype(jnp.int32) >> shifts) & 3) - (1 - 2 * core) * steps) & 3
    span_output, decode_output = finish(
        jnp.concatenate([core[None], came_from]),
        att1,
        att2,
        jnp.pad(home, ((0, EXTRA - own), (0, 0))),
        span_tokens[0],
        jnp.pad(decode_tokens, ((0, EXTRA - own), (0, 0))),
        [c for half in (mine, theirs) for part in half for c in part],
    )
    return span_output[None], keyval[:rows][None], decode_output[:own], decode_keyval


def solution(mesh):
    both = P(AXES)
    return jax.shard_map(
        functools.partial(shards, mesh.size),
        mesh=Mesh(mesh.devices.reshape(4, 2, 4, 4), AXES),
        in_specs=(both, both, P(), both, both, both, both, both, both, both, P()),
        out_specs=(both, both, both, both),
        check_vma=False,
    )
```

time: 217 us -> 189 us (0.87)
  waiting for transfers between devices: 98.9 us -> 44.1 us
  starting transfers between devices: 19.7 us -> 57.5 us
  between operations: 25.4 us -> 15.2 us
  local copies, waits for them, and re-layouts: 11.3 us -> 18.3 us
  other arithmetic: 14.4 us -> 7.66 us
    all_gather x2 -> x1, waiting for transfers between devices: 85 us -> 0.01 us  [shards(): first_weight = lax.all_gather(piece[:, :split], CHIPS, axis=0, tiled=True)]
    ppermute x0 -> x30, waiting for transfers between devices: none -> 41.7 us  [the longest x15 39.9 us: send(): return lax.ppermute(v, AXES, list(zip(DEVICES.tolist(), to.tolist())))]
    ppermute x0 -> x30, starting transfers between devices: none -> 40.7 us  [the longest x15 32.1 us: send(): return lax.ppermute(v, AXES, list(zip(DEVICES.tolist(), to.tolist())))]
    all_to_all x2, waiting for transfers between devices: 13.9 us -> 2.34 us  [exchange(): lax.all_to_all(sent.reshape((devices, -1) + sent.shape[1:]), AXES, 0, 0)]
    dynamic_update_slice x0 -> x8, local copies, waits for them, and re-layouts: none -> 5.61 us  [put(): return lax.dynamic_update_slice(whole, jnp.expand_dims(piece, place), start)]
    select_n x2 -> x4, other arithmetic: 5.94 us -> 0.39 us  [the longest x1 0.21 us: shards(): cos = jnp.stack([cos, jnp.where(first_core, cos, 1.0)])]
    all_to_all x2, starting transfers between devices: 19.6 us -> 16.7 us  [exchange(): lax.all_to_all(sent.reshape((devices, -1) + sent.shape[1:]), AXES, 0, 0)]
    pallas_call x3 -> x9, Pallas kernels: 27.3 us -> 24.6 us  [the longest x1 10.1 us: finish(): pl.pallas_call(finish_body, grid_spec=pltpu.PrefetchScalarGridSpec(num_sc...]
  transfers between devices with their start and end apart: 4 -> 33, of which waited for: 3 -> 10; matrix products, arithmetic and copies ran while one was open for 8% -> 9% of each run, Pallas kernels for 16% -> 19%
where the time goes in v2:
time: 189 us; the launch traced here: 188 us
  starting transfers between devices  57.5 us (30%)
  Pallas kernels  45 us (24%)
  waiting for transfers between devices  44.1 us (23%)
  local copies, waits for them, and re-layouts  18.3 us (10%)
  between operations  15.2 us (8%)
  other arithmetic  7.66 us (4%)
    ppermute x15, waiting for transfers between devices, send(): return lax.ppermute(v, AXES, list(zip(DEVICES.tolist(), to.tolist())))  39.9 us
    ppermute x15, starting transfers between devices, send(): return lax.ppermute(v, AXES, list(zip(DEVICES.tolist(), to.tolist())))  32.1 us
    all_to_all x2, starting transfers between devices, exchange(): lax.all_to_all(sent.reshape((devices, -1) + sent.shape[1:]), AXES, 0, 0)  16.7 us
    pallas_call x2, Pallas kernels, span_attend(): pl.pallas_call(span_body, grid_spec=pltpu.PrefetchScalarGridSpec(num_scal...  16.5 us
    pallas_call x1, Pallas kernels, finish(): pl.pallas_call(finish_body, grid_spec=pltpu.PrefetchScalarGridSpec(num_sc...  10.1 us
    ppermute x15, starting transfers between devices, swap(): lax.ppermute(v, AXES, list(zip(DEVICES.tolist(), (DEVICES ^ 16).tolist())))  8.63 us
    pallas_call x2, Pallas kernels, project(): pl.pallas_call(functools.partial(project_body, rows), grid=(count,), in_s...  6.34 us
    unnamed x46, local copies, waits for them, and re-layouts  6.13 us
  transfers between devices with their start and end apart: 33, of which 10 were waited for; matrix products, arithmetic and copies ran while one was open for 9% of the time, Pallas kernels for 19%

profile of v2, /device:TPU:1, one launch (start us, length us, event | category | flops | bytes accessed | tf_op | source)
XLA Modules:
  0.0 187.7 jit_solution(15941915114168997506)
XLA Ops:
  7.3 0.9 fusion.13
  8.1 0.9 fusion.14
  9.0 0.7 fusion.15
  9.8 1.5 collective-permute-start
  11.3 1.0 collective-permute-done
  12.4 0.7 slice.87
  14.3 0.8 dynamic_slice.3.to_ref.came_ref
  15.1 0.7 convert_bitcast_fusion
  15.9 0.7 fusion.8
  16.6 1.7 place.1
  18.3 0.7 compare_reduce_fusion
  19.0 1.1 fusion.order_ref
  20.1 1.8 collective-permute-start.1
  21.9 3.3 %collective-permute-start.2 = (bf16[40,1280]{1,0:T(8,128)(2,1)S(1)}, bf16[40,1280]{1,0:T(8,128)(2,1)S(1)}, u32[]{:S(2)}, u32[]{:S(2)}) collective-permute-start(bf16[40,1280]{1,0:T(8,128)(2,1)S(1)} %slice.82.refs_0_), channel_id=1, source_target_pairs={{0,2},{1,3},{2,0},{3,1},{4,6},{5,7},{6,4},{7,5},{8,10},{9,11},{10,... | collective-permute-start | bytes 307208 | tf_op jit(solution)/shard_map/ppermute | solution.py:420
  25.2 0.7 collective-permute-start.3
  26.0 8.6 %all-to-all-start = ((bf16[128,2,24,128]{3,2,1,0:T(8,128)(2,1)}), bf16[128,2,24,128]{3,2,1,0:T(8,128)(2,1)}, u32[]{:S(2)}, u32[]{:S(2)}) async-start(bf16[128,2,24,128]{3,2,1,0:T(8,128)(2,1)} %bitcast.15), calls=%async_computation | async-start | bytes 3145728 | tf_op jit(solution)/shard_map/all_to_all | solution.py:405
  34.7 2.7 %collective-permute-start.8 = (bf16[2,80,640]{2,1,0:T(8,128)(2,1)S(1)}, bf16[2,80,640]{2,1,0:T(8,128)(2,1)S(1)}, u32[]{:S(2)}, u32[]{:S(2)}) collective-permute-start(bf16[2,80,640]{2,1,0:T(8,128)(2,1)S(1)} %get-tuple-element.40), channel_id=1, source_target_pairs={{0,4},{1,5},{2,6},{3,7},{4,8},{5,9},{6,10},{7,11},{8,12},{9,13},{1... | collective-permute-start | bytes 614408 | tf_op jit(solution)/shard_map/ppermute | solution.py:420
  37.4 2.5 %collective-permute-start.4 = (bf16[2,80,640]{2,1,0:T(8,128)(2,1)S(1)}, bf16[2,80,640]{2,1,0:T(8,128)(2,1)S(1)}, u32[]{:S(2)}, u32[]{:S(2)}) collective-permute-start(bf16[2,80,640]{2,1,0:T(8,128)(2,1)S(1)} %get-tuple-element.41), channel_id=1, source_target_pairs={{0,32},{1,33},{2,34},{3,35},{4,36},{5,37},{6,38},{7,39},{8,40},{9,... | collective-permute-start | bytes 614408 | tf_op jit(solution)/shard_map/ppermute | solution.py:420
  39.9 1.0 broadcast_in_dim.67
  40.9 0.7 bitcast_dynamic-update-slice_fusion.2
  41.6 1.0 broadcast_in_dim.61
  42.6 0.7 bitcast_dynamic-update-slice_fusion.7
  43.3 12.4 %collective-permute-done.8 = bf16[2,80,640]{2,1,0:T(8,128)(2,1)S(1)} collective-permute-done((bf16[2,80,640]{2,1,0:T(8,128)(2,1)S(1)}, bf16[2,80,640]{2,1,0:T(8,128)(2,1)S(1)}, u32[]{:S(2)}, u32[]{:S(2)}) %collective-permute-start.8) | collective-permute-done | bytes 204832 | tf_op jit(solution)/shard_map/ppermute | solution.py:420
  55.6 1.3 collective-permute-start.9
  56.9 2.6 %collective-permute-start.5 = (bf16[2,80,640]{2,1,0:T(8,128)(2,1)S(1)}, bf16[2,80,640]{2,1,0:T(8,128)(2,1)S(1)}, u32[]{:S(2)}, u32[]{:S(2)}) collective-permute-start(bf16[2,80,640]{2,1,0:T(8,128)(2,1)S(1)} %collective-permute-done.4), channel_id=1, source_target_pairs={{0,32},{1,33},{2,34},{3,35},{4,36},{5,37},{6,38},{7,39},{8,40},{9,... | collective-permute-start | bytes 614408 | tf_op jit(solution)/shard_map/ppermute | solution.py:420
  59.6 0.7 bitcast_dynamic-update-slice_fusion.1
  60.3 0.7 bitcast_dynamic-update-slice_fusion.6
  61.0 1.3 collective-permute-done.9
  62.3 1.5 collective-permute-start.10
  64.3 3.3 %collective-permute-start.6 = (bf16[2,80,640]{2,1,0:T(8,128)(2,1)S(1)}, bf16[2,80,640]{2,1,0:T(8,128)(2,1)S(1)}, u32[]{:S(2)}, u32[]{:S(2)}) collective-permute-start(bf16[2,80,640]{2,1,0:T(8,128)(2,1)S(1)} %collective-permute-done.5), channel_id=1, source_target_pairs={{0,32},{1,33},{2,34},{3,35},{4,36},{5,37},{6,38},{7,39},{8,40},{9,... | collective-permute-start | bytes 614408 | tf_op jit(solution)/shard_map/ppermute | solution.py:420
  67.6 0.7 bitcast_dynamic-update-slice_fusion
  68.3 0.7 bitcast_dynamic-update-slice_fusion.5
  69.0 0.7 bitcast_dynamic-update-slice_fusion.3.refs_4_
  69.7 2.6 %collective-permute-start.11 = (bf16[2,4,80,640]{3,2,1,0:T(8,128)(2,1)}, bf16[2,4,80,640]{3,2,1,0:T(8,128)(2,1)}, u32[]{:S(2)}, u32[]{:S(2)}) collective-permute-start(bf16[2,4,80,640]{3,2,1,0:T(8,128)(2,1)} %bitcast_dynamic-update-slice_fusion.3.refs_4_), channel_id=1, source_target_pairs={{0,32},{1,33},{2,34},{3,35},{4,36},{5,37},{6,38},{7,39},{8,40},{9,... | collective-permute-start | bytes 2457608 | tf_op jit(solution)/shard_map/ppermute | solution.py:420
  72.3 0.7 bitcast_dynamic-update-slice_fusion.4.refs_0_
  73.0 2.7 %collective-permute-start.7 = (bf16[4,2,80,640]{3,2,1,0:T(8,128)(2,1)}, bf16[4,2,80,640]{3,2,1,0:T(8,128)(2,1)}, u32[]{:S(2)}, u32[]{:S(2)}) collective-permute-start(bf16[4,2,80,640]{3,2,1,0:T(8,128)(2,1)} %bitcast_dynamic-update-slice_fusion.4.refs_0_), channel_id=1, source_target_pairs={{0,4},{1,5},{2,6},{3,7},{4,8},{5,9},{6,10},{7,11},{8,12},{9,13},{1... | collective-permute-start | bytes 2457608 | tf_op jit(solution)/shard_map/ppermute | solution.py:420
  75.8 4.1 %norm_ordered.2.refs_0_ = bf16[544,2560]{1,0:T(8,128)(2,1)S(1)} custom-call(bf16[512,2560]{1,0:T(8,128)(2,1)S(1)} %pad_maximum_fusion.x_ref, f32[1,2560]{1,0:T(1,128)S(1)} %broadcast_in_dim.72.gain_ref, bf16[640,640]{1,0:T(8,128)(2,1)S(1)} %copy-done.1), custom_call_target="tpu_custom_call" | custom-call | flops 1677721600 | bytes 5242880 | tf_op jit(solution)/shard_map/norm_ordered/pallas_call | solution.py:57
  79.9 1.3 pick.2
  81.4 0.8 collective-permute-start.15
  82.3 0.7 collective-permute-done.15
  83.1 1.0 fusion.4
  84.7 0.8 pad_maximum_fusion.1.cos_ref
  86.0 2.8 %collective-permute-done.11.refs_5_ = bf16[2,4,80,640]{3,2,1,0:T(8,128)(2,1)} collective-permute-done((bf16[2,4,80,640]{3,2,1,0:T(8,128)(2,1)}, bf16[2,4,80,640]{3,2,1,0:T(8,128)(2,1)}, u32[]{:S(2)}, u32[]{:S(2)}) %collective-permute-start.11) | collective-permute-done | bytes 819232 | tf_op jit(solution)/shard_map/ppermute | solution.py:420
  88.8 10.2 %collective-permute-done.7.refs_1_ = bf16[4,2,80,640]{3,2,1,0:T(8,128)(2,1)} collective-permute-done((bf16[4,2,80,640]{3,2,1,0:T(8,128)(2,1)}, bf16[4,2,80,640]{3,2,1,0:T(8,128)(2,1)}, u32[]{:S(2)}, u32[]{:S(2)}) %collective-permute-start.7) | collective-permute-done | bytes 819232 | tf_op jit(solution)/shard_map/ppermute | solution.py:420
  99.0 3.4 %collective-permute-start.16 = (bf16[4,2,80,640]{3,2,1,0:T(8,128)(2,1)}, bf16[4,2,80,640]{3,2,1,0:T(8,128)(2,1)}, u32[]{:S(2)}, u32[]{:S(2)}) collective-permute-start(bf16[4,2,80,640]{3,2,1,0:T(8,128)(2,1)} %collective-permute-done.7.refs_1_), channel_id=1, source_target_pairs={{0,4},{1,5},{2,6},{3,7},{4,8},{5,9},{6,10},{7,11},{8,12},{9,13},{1... | collective-permute-start | bytes 2457608 | tf_op jit(solution)/shard_map/ppermute | solution.py:420
  102.4 12.7 %collective-permute-done.16.refs_2_ = bf16[4,2,80,640]{3,2,1,0:T(8,128)(2,1)} collective-permute-done((bf16[4,2,80,640]{3,2,1,0:T(8,128)(2,1)}, bf16[4,2,80,640]{3,2,1,0:T(8,128)(2,1)}, u32[]{:S(2)}, u32[]{:S(2)}) %collective-permute-start.16) | collective-permute-done | bytes 819232 | tf_op jit(solution)/shard_map/ppermute | solution.py:420
  115.1 3.4 %collective-permute-start.17 = (bf16[4,2,80,640]{3,2,1,0:T(8,128)(2,1)}, bf16[4,2,80,640]{3,2,1,0:T(8,128)(2,1)}, u32[]{:S(2)}, u32[]{:S(2)}) collective-permute-start(bf16[4,2,80,640]{3,2,1,0:T(8,128)(2,1)} %collective-permute-done.16.refs_2_), channel_id=1, source_target_pairs={{0,4},{1,5},{2,6},{3,7},{4,8},{5,9},{6,10},{7,11},{8,12},{9,13},{1... | collective-permute-start | bytes 2457608 | tf_op jit(solution)/shard_map/ppermute | solution.py:420
  118.8 3.2 %copy-done = bf16[2560,1536]{1,0:T(8,128)(2,1)S(1)} copy-done((bf16[2560,1536]{1,0:T(8,128)(2,1)S(1)}, bf16[2560,1536]{1,0:T(8,128)(2,1)}, u32[]{:S(2)}) %copy-start) | copy-done | bytes 7864344
  122.0 1.1 copy-done.3
  123.1 2.1 %project.3 = (bf16[2,272,256]{2,1,0:T(8,128)(2,1)S(1)}, bf16[2,272,256]{2,1,0:T(8,128)(2,1)S(1)}) custom-call(bf16[544,2560]{1,0:T(8,128)(2,1)S(1)} %norm_ordered.3.x_ref, bf16[2560,1536]{1,0:T(8,128)(2,1)S(1)} %copy-done, f32[2,544,128]{2,1,0:T(8,128)S(1)} %copy-done.3, f32[2,544,128]{2,1,0:T(8,128)S(1)} %pad_maximum_fusion.2.sin_ref), custom_call_target="tpu_custom_call" | custom-call | flops 1426063360 | bytes 2621440 | tf_op jit(solution)/shard_map/project/pallas_call | solution.py:97
  125.2 1.7 collective-permute-start.20
  126.9 4.2 %project.2 = (bf16[4,272,256]{2,1,0:T(8,128)(2,1)S(1)}, bf16[4,272,256]{2,1,0:T(8,128)(2,1)S(1)}) custom-call(bf16[544,2560]{1,0:T(8,128)(2,1)S(1)} %norm_ordered.3.x_ref, bf16[2560,1536]{1,0:T(8,128)(2,1)S(1)} %copy-done, f32[2,544,128]{2,1,0:T(8,128)S(1)} %copy-done.3, f32[2,544,128]{2,1,0:T(8,128)S(1)} %pad_maximum_fusion.2.sin_ref), custom_call_target="tpu_custom_call" | custom-call | flops 2852126720 | bytes 5242880 | tf_op jit(solution)/shard_map/project/pallas_call | solution.py:97
  131.8 1.2 collective-permute-start.22
  133.2 3.9 %decode_attend.1 = bf16[256,24,128]{2,1,0:T(8,128)(2,1)} custom-call(s32[5]{0:T(128)S(1)} %pad_add_fusion.1.info_ref, bf16[4,272,256]{2,1,0:T(8,128)(2,1)S(1)} %get-tuple-element.30.ab_ref.oab_ref, bf16[2,272,256]{2,1,0:T(8,128)(2,1)S(1)} %get-tuple-element.31.c_ref.oc_ref, bf16[4,272,256]{2,1,0:T(8,128)(2,1)S(1)} %collective-permute-done.21.ab_ref.tab_ref, ...), custom_call_target="tpu_custom_call" | custom-call | flops 67108864 | bytes 4194304 | tf_op jit(solution)/shard_map/decode_attend/pallas_call | solution.py:163
  137.2 8.2 %all-to-all-start.1 = ((bf16[128,2,24,128]{3,2,1,0:T(8,128)(2,1)}), bf16[128,2,24,128]{3,2,1,0:T(8,128)(2,1)S(1)}, u32[]{:S(2)}, u32[]{:S(2)}) async-start(bf16[128,2,24,128]{3,2,1,0:T(8,128)(2,1)} %bitcast.26), calls=%async_computation.1 | async-start | bytes 3145728 | tf_op jit(solution)/shard_map/all_to_all | solution.py:405
  145.4 1.1 collective-permute-start.23
  148.3 0.7 fusion.2
  149.0 1.6 copy-done.13
  150.6 8.2 %span_attend.2.att1_ref = bf16[256,1280]{1,0:T(8,128)(2,1)S(1)} custom-call(s32[1]{0:T(128)S(6)} %copy.50.index_ref, bf16[4,272,256]{2,1,0:T(8,128)(2,1)S(1)} %copy-done.10, bf16[2,272,256]{2,1,0:T(8,128)(2,1)S(1)} %copy-done.6, bf16[272,256]{1,0:T(8,128)(2,1)S(1)} %get-tuple-element.39.k_ref, bf16[272,256]{1,0:T(8,128)(2,1)S(1)} %get-tuple-element.38.v_ref, ...), custom_call_target="tpu_custom_call" | custom-call | flops 3019898880 | bytes 2097152 | tf_op jit(solution)/shard_map/span_attend/pallas_call | solution.py:296
  158.9 8.2 %span_attend.3.att2_ref = bf16[256,1280]{1,0:T(8,128)(2,1)S(1)} custom-call(s32[1]{0:T(128)S(6)} %copy.50.index_ref, bf16[4,272,256]{2,1,0:T(8,128)(2,1)S(1)} %copy-done.12, bf16[2,272,256]{2,1,0:T(8,128)(2,1)S(1)} %copy-done.8, bf16[272,256]{1,0:T(8,128)(2,1)S(1)} %get-tuple-element.39.k_ref, bf16[272,256]{1,0:T(8,128)(2,1)S(1)} %get-tuple-element.38.v_ref, ...), custom_call_target="tpu_custom_call" | custom-call | flops 3019898880 | bytes 2097152 | tf_op jit(solution)/shard_map/span_attend/pallas_call | solution.py:296
  167.1 2.3 %all-to-all-done.1 = bf16[128,2,24,128]{3,2,1,0:T(8,128)(2,1)S(1)} async-done(((bf16[128,2,24,128]{3,2,1,0:T(8,128)(2,1)}), bf16[128,2,24,128]{3,2,1,0:T(8,128)(2,1)S(1)}, u32[]{:S(2)}, u32[]{:S(2)}) %all-to-all-start.1) | async-done | bytes 1572896 | tf_op jit(solution)/shard_map/all_to_all | solution.py:405
  169.5 0.6 pick.3
  170.2 10.1 %finish.1 = (bf16[256,2560]{1,0:T(8,128)(2,1)}, bf16[16,2560]{1,0:T(8,128)(2,1)S(1)}) custom-call(s32[17]{0:T(128)S(1)} %pad_add_fusion.info_ref, bf16[256,1280]{1,0:T(8,128)(2,1)S(1)} %span_attend.2.att1_ref, bf16[256,1280]{1,0:T(8,128)(2,1)S(1)} %span_attend.3.att2_ref, bf16[16,2560]{1,0:T(8,128)(2,1)S(1)} %pad.21.datt_ref, bf16[256,2560]{1,0:T(8,128)(2,1)} %bitcast.69, ...), custom_call_target="tpu_custom_call" | custom-call | flops 3355443200 | bytes 13107200 | tf_op jit(solution)/shard_map/finish/pallas_call | solution.py:372
  180.3 0.6 slice.80
  (113 shorter events, 6.0 us)
Async XLA Ops:
  7.2 11.9 %copy-start.17 = (s32[640]{0:T(1024)S(1)}, s32[640]{0:T(1024)}, u32[]{:S(2)}) copy-start(s32[640]{0:T(1024)} %constant.88.clone) | copy-start | bytes 7684
  7.2 11.1 %copy-start.18 = (s32[256]{0:T(256)S(1)}, s32[256]{0:T(256)}, u32[]{:S(2)}) copy-start(s32[256]{0:T(256)} %param.24) | copy-start | bytes 3076
  7.2 9.4 %copy-start.16 = (f32[2560]{0:T(1024)S(1)}, f32[2560]{0:T(1024)}, u32[]{:S(2)}) copy-start(f32[2560]{0:T(1024)} %param.16) | copy-start | bytes 30724
  7.2 111.6 %all-gather.2.cloned.1.call-start = ((), (), s32[]{:S(2)}) async-start(), calls=%async_computation.2 | async-start | bytes 7987200 | tf_op jit(solution)/shard_map/all_gather | solution.py:484
  9.8 2.5 %collective-permute-start = (bf16[20,2816]{1,0:T(8,128)(2,1)S(1)}, bf16[20,2816]{1,0:T(8,128)(2,1)S(1)}, u32[]{:S(2)}, u32[]{:S(2)}) collective-permute-start(bf16[20,2816]{1,0:T(8,128)(2,1)S(1)} %maximum_select_fusion.3), channel_id=1, source_target_pairs={{0,16},{1,17},{2,18},{3,19},{4,20},{5,21},{6,22},{7,23},{8,24},{9,... | collective-permute-start | bytes 337928 | tf_op jit(solution)/shard_map/ppermute | solution.py:424
  13.7 68.6 %collective-permute-start.14 = (s32[256]{0:T(256)S(1)}, s32[256]{0:T(256)S(1)}, u32[]{:S(2)}, u32[]{:S(2)}) collective-permute-start(s32[256]{0:T(256)S(1)} %iota_add_fusion), channel_id=1, source_target_pairs={{0,16},{1,17},{2,18},{3,19},{4,20},{5,21},{6,22},{7,23},{8,24},{9,... | collective-permute-start | bytes 3080 | tf_op jit(solution)/shard_map/ppermute | solution.py:424
  14.2 61.5 %collective-permute-start.13 = (bf16[256,2560]{1,0:T(8,128)(2,1)}, bf16[256,2560]{1,0:T(8,128)(2,1)S(1)}, u32[]{:S(2)}, u32[]{:S(2)}) collective-permute-start(bf16[256,2560]{1,0:T(8,128)(2,1)} %bitcast.68), channel_id=1, source_target_pairs={{0,16},{1,17},{2,18},{3,19},{4,20},{5,21},{6,22},{7,23},{8,24},{9,... | collective-permute-start | bytes 3932168 | tf_op jit(solution)/shard_map/ppermute | solution.py:424
  20.1 14.4 %collective-permute-start.1 = (bf16[40,1280]{1,0:T(8,128)(2,1)S(1)}, bf16[40,1280]{1,0:T(8,128)(2,1)S(1)}, u32[]{:S(2)}, u32[]{:S(2)}) collective-permute-start(bf16[40,1280]{1,0:T(8,128)(2,1)S(1)} %slice.82.refs_0_), channel_id=1, source_target_pairs={{0,1},{1,2},{2,3},{3,0},{4,5},{5,6},{6,7},{7,4},{8,9},{9,10},{10,1... | collective-permute-start | bytes 307208 | tf_op jit(solution)/shard_map/ppermute | solution.py:420
  21.9 12.6 %collective-permute-start.2 = (bf16[40,1280]{1,0:T(8,128)(2,1)S(1)}, bf16[40,1280]{1,0:T(8,128)(2,1)S(1)}, u32[]{:S(2)}, u32[]{:S(2)}) collective-permute-start(bf16[40,1280]{1,0:T(8,128)(2,1)S(1)} %slice.82.refs_0_), channel_id=1, source_target_pairs={{0,2},{1,3},{2,0},{3,1},{4,6},{5,7},{6,4},{7,5},{8,10},{9,11},{10,... | collective-permute-start | bytes 307208 | tf_op jit(solution)/shard_map/ppermute | solution.py:420
  25.2 9.3 %collective-permute-start.3 = (bf16[40,1280]{1,0:T(8,128)(2,1)S(1)}, bf16[40,1280]{1,0:T(8,128)(2,1)S(1)}, u32[]{:S(2)}, u32[]{:S(2)}) collective-permute-start(bf16[40,1280]{1,0:T(8,128)(2,1)S(1)} %slice.82.refs_0_), channel_id=1, source_target_pairs={{0,3},{1,0},{2,1},{3,2},{4,7},{5,4},{6,5},{7,6},{8,11},{9,8},{10,9... | collective-permute-start | bytes 307208 | tf_op jit(solution)/shard_map/ppermute | solution.py:420
  26.0 54.0 %all-to-all-start = ((bf16[128,2,24,128]{3,2,1,0:T(8,128)(2,1)}), bf16[128,2,24,128]{3,2,1,0:T(8,128)(2,1)}, u32[]{:S(2)}, u32[]{:S(2)}) async-start(bf16[128,2,24,128]{3,2,1,0:T(8,128)(2,1)} %bitcast.15), calls=%async_computation | async-start | bytes 3145728 | tf_op jit(solution)/shard_map/all_to_all | solution.py:405
  34.7 20.9 %collective-permute-start.8 = (bf16[2,80,640]{2,1,0:T(8,128)(2,1)S(1)}, bf16[2,80,640]{2,1,0:T(8,128)(2,1)S(1)}, u32[]{:S(2)}, u32[]{:S(2)}) collective-permute-start(bf16[2,80,640]{2,1,0:T(8,128)(2,1)S(1)} %get-tuple-element.40), channel_id=1, source_target_pairs={{0,4},{1,5},{2,6},{3,7},{4,8},{5,9},{6,10},{7,11},{8,12},{9,13},{1... | collective-permute-start | bytes 614408 | tf_op jit(solution)/shard_map/ppermute | solution.py:420
  37.4 19.5 %collective-permute-start.4 = (bf16[2,80,640]{2,1,0:T(8,128)(2,1)S(1)}, bf16[2,80,640]{2,1,0:T(8,128)(2,1)S(1)}, u32[]{:S(2)}, u32[]{:S(2)}) collective-permute-start(bf16[2,80,640]{2,1,0:T(8,128)(2,1)S(1)} %get-tuple-element.41), channel_id=1, source_target_pairs={{0,32},{1,33},{2,34},{3,35},{4,36},{5,37},{6,38},{7,39},{8,40},{9,... | collective-permute-start | bytes 614408 | tf_op jit(solution)/shard_map/ppermute | solution.py:420
  40.9 34.8 %copy-start.14 = (bf16[1,256,2560]{2,1,0:T(8,128)(2,1)S(1)}, bf16[1,256,2560]{2,1,0:T(8,128)(2,1)}, u32[]{:S(2)}) copy-start(bf16[1,256,2560]{2,1,0:T(8,128)(2,1)} %param.14) | copy-start | bytes 3932164
  55.6 6.7 %collective-permute-start.9 = (bf16[2,80,640]{2,1,0:T(8,128)(2,1)S(1)}, bf16[2,80,640]{2,1,0:T(8,128)(2,1)S(1)}, u32[]{:S(2)}, u32[]{:S(2)}) collective-permute-start(bf16[2,80,640]{2,1,0:T(8,128)(2,1)S(1)} %collective-permute-done.8), channel_id=1, source_target_pairs={{0,4},{1,5},{2,6},{3,7},{4,8},{5,9},{6,10},{7,11},{8,12},{9,13},{1... | collective-permute-start | bytes 614408 | tf_op jit(solution)/shard_map/ppermute | solution.py:420
  56.9 7.3 %collective-permute-start.5 = (bf16[2,80,640]{2,1,0:T(8,128)(2,1)S(1)}, bf16[2,80,640]{2,1,0:T(8,128)(2,1)S(1)}, u32[]{:S(2)}, u32[]{:S(2)}) collective-permute-start(bf16[2,80,640]{2,1,0:T(8,128)(2,1)S(1)} %collective-permute-done.4), channel_id=1, source_target_pairs={{0,32},{1,33},{2,34},{3,35},{4,36},{5,37},{6,38},{7,39},{8,40},{9,... | collective-permute-start | bytes 614408 | tf_op jit(solution)/shard_map/ppermute | solution.py:420
  62.3 6.7 %collective-permute-start.10 = (bf16[2,80,640]{2,1,0:T(8,128)(2,1)S(1)}, bf16[2,80,640]{2,1,0:T(8,128)(2,1)S(1)}, u32[]{:S(2)}, u32[]{:S(2)}) collective-permute-start(bf16[2,80,640]{2,1,0:T(8,128)(2,1)S(1)} %collective-permute-done.9), channel_id=1, source_target_pairs={{0,4},{1,5},{2,6},{3,7},{4,8},{5,9},{6,10},{7,11},{8,12},{9,13},{1... | collective-permute-start | bytes 614408 | tf_op jit(solution)/shard_map/ppermute | solution.py:420
  64.3 8.0 %collective-permute-start.6 = (bf16[2,80,640]{2,1,0:T(8,128)(2,1)S(1)}, bf16[2,80,640]{2,1,0:T(8,128)(2,1)S(1)}, u32[]{:S(2)}, u32[]{:S(2)}) collective-permute-start(bf16[2,80,640]{2,1,0:T(8,128)(2,1)S(1)} %collective-permute-done.5), channel_id=1, source_target_pairs={{0,32},{1,33},{2,34},{3,35},{4,36},{5,37},{6,38},{7,39},{8,40},{9,... | collective-permute-start | bytes 614408 | tf_op jit(solution)/shard_map/ppermute | solution.py:420
  69.7 19.1 %collective-permute-start.11 = (bf16[2,4,80,640]{3,2,1,0:T(8,128)(2,1)}, bf16[2,4,80,640]{3,2,1,0:T(8,128)(2,1)}, u32[]{:S(2)}, u32[]{:S(2)}) collective-permute-start(bf16[2,4,80,640]{3,2,1,0:T(8,128)(2,1)} %bitcast_dynamic-update-slice_fusion.3.refs_4_), channel_id=1, source_target_pairs={{0,32},{1,33},{2,34},{3,35},{4,36},{5,37},{6,38},{7,39},{8,40},{9,... | collective-permute-start | bytes 2457608 | tf_op jit(solution)/shard_map/ppermute | solution.py:420
  73.0 2.9 %copy-start.1 = (bf16[640,640]{1,0:T(8,128)(2,1)S(1)}, bf16[640,640]{1,0:T(8,128)(2,1)}, u32[]{:S(2)}) copy-start(bf16[640,640]{1,0:T(8,128)(2,1)} %fusion.order_ref) | copy-start | bytes 2457604
  73.0 26.0 %collective-permute-start.7 = (bf16[4,2,80,640]{3,2,1,0:T(8,128)(2,1)}, bf16[4,2,80,640]{3,2,1,0:T(8,128)(2,1)}, u32[]{:S(2)}, u32[]{:S(2)}) collective-permute-start(bf16[4,2,80,640]{3,2,1,0:T(8,128)(2,1)} %bitcast_dynamic-update-slice_fusion.4.refs_0_), channel_id=1, source_target_pairs={{0,4},{1,5},{2,6},{3,7},{4,8},{5,9},{6,10},{7,11},{8,12},{9,13},{1... | collective-permute-start | bytes 2457608 | tf_op jit(solution)/shard_map/ppermute | solution.py:420
  81.4 1.6 collective-permute-start.15
  82.2 3.3 %collective-permute-start.12 = (bf16[16,2560]{1,0:T(8,128)(2,1)S(1)}, bf16[16,2560]{1,0:T(8,128)(2,1)S(1)}, u32[]{:S(2)}, u32[]{:S(2)}) collective-permute-start(bf16[16,2560]{1,0:T(8,128)(2,1)S(1)} %pad.19), channel_id=1, source_target_pairs={{0,16},{1,17},{2,18},{3,19},{4,20},{5,21},{6,22},{7,23},{8,24},{9,... | collective-permute-start | bytes 245768 | tf_op jit(solution)/shard_map/ppermute | solution.py:424
  84.4 1.2 copy-start.2
  99.0 16.1 %collective-permute-start.16 = (bf16[4,2,80,640]{3,2,1,0:T(8,128)(2,1)}, bf16[4,2,80,640]{3,2,1,0:T(8,128)(2,1)}, u32[]{:S(2)}, u32[]{:S(2)}) collective-permute-start(bf16[4,2,80,640]{3,2,1,0:T(8,128)(2,1)} %collective-permute-done.7.refs_1_), channel_id=1, source_target_pairs={{0,4},{1,5},{2,6},{3,7},{4,8},{5,9},{6,10},{7,11},{8,12},{9,13},{1... | collective-permute-start | bytes 2457608 | tf_op jit(solution)/shard_map/ppermute | solution.py:420
  102.4 16.1 %collective-permute-start.18 = (bf16[2,4,80,640]{3,2,1,0:T(8,128)(2,1)}, bf16[2,4,80,640]{3,2,1,0:T(8,128)(2,1)}, u32[]{:S(2)}, u32[]{:S(2)}) collective-permute-start(bf16[2,4,80,640]{3,2,1,0:T(8,128)(2,1)} %collective-permute-done.11.refs_5_), channel_id=1, source_target_pairs={{0,32},{1,33},{2,34},{3,35},{4,36},{5,37},{6,38},{7,39},{8,40},{9,... | collective-permute-start | bytes 2457608 | tf_op jit(solution)/shard_map/ppermute | solution.py:420
  115.1 16.7 %collective-permute-start.17 = (bf16[4,2,80,640]{3,2,1,0:T(8,128)(2,1)}, bf16[4,2,80,640]{3,2,1,0:T(8,128)(2,1)}, u32[]{:S(2)}, u32[]{:S(2)}) collective-permute-start(bf16[4,2,80,640]{3,2,1,0:T(8,128)(2,1)} %collective-permute-done.16.refs_2_), channel_id=1, source_target_pairs={{0,4},{1,5},{2,6},{3,7},{4,8},{5,9},{6,10},{7,11},{8,12},{9,13},{1... | collective-permute-start | bytes 2457608 | tf_op jit(solution)/shard_map/ppermute | solution.py:420
  118.5 14.5 %collective-permute-start.19 = (bf16[2,4,80,640]{3,2,1,0:T(8,128)(2,1)}, bf16[2,4,80,640]{3,2,1,0:T(8,128)(2,1)}, u32[]{:S(2)}, u32[]{:S(2)}) collective-permute-start(bf16[2,4,80,640]{3,2,1,0:T(8,128)(2,1)} %collective-permute-done.18.refs_6_), channel_id=1, source_target_pairs={{0,32},{1,33},{2,34},{3,35},{4,36},{5,37},{6,38},{7,39},{8,40},{9,... | collective-permute-start | bytes 2457608 | tf_op jit(solution)/shard_map/ppermute | solution.py:420
  118.8 3.2 %copy-start = (bf16[2560,1536]{1,0:T(8,128)(2,1)S(1)}, bf16[2560,1536]{1,0:T(8,128)(2,1)}, u32[]{:S(2)}) copy-start(bf16[2560,1536]{1,0:T(8,128)(2,1)} %all-gather.2.cloned.1.call-done.w_ref) | copy-start | bytes 23592964
  122.0 1.1 copy-start.3
  125.2 8.0 %copy-start.5 = (bf16[2,272,256]{2,1,0:T(8,128)(2,1)}, bf16[2,272,256]{2,1,0:T(8,128)(2,1)S(1)}, u32[]{:S(2)}) copy-start(bf16[2,272,256]{2,1,0:T(8,128)(2,1)S(1)} %get-tuple-element.31.c_ref.oc_ref) | copy-start | bytes 835588
  125.2 7.8 %collective-permute-start.20 = (bf16[2,272,256]{2,1,0:T(8,128)(2,1)S(1)}, bf16[2,272,256]{2,1,0:T(8,128)(2,1)S(1)}, u32[]{:S(2)}, u32[]{:S(2)}) collective-permute-start(bf16[2,272,256]{2,1,0:T(8,128)(2,1)S(1)} %get-tuple-element.32), channel_id=1, source_target_pairs={{0,16},{1,17},{2,18},{3,19},{4,20},{5,21},{6,22},{7,23},{8,24},{9,... | collective-permute-start | bytes 835592 | tf_op jit(solution)/shard_map/ppermute | solution.py:424
  126.9 6.3 %copy-start.4 = (bf16[2,2048,512]{2,1,0:T(8,128)(2,1)S(1)}, bf16[2,2048,512]{2,1,0:T(8,128)(2,1)}, u32[]{:S(2)}) copy-start(bf16[2,2048,512]{2,1,0:T(8,128)(2,1)} %cache_ref.5) | copy-start | bytes 12582916
  131.2 6.0 %copy-start.9 = (bf16[4,272,256]{2,1,0:T(8,128)(2,1)}, bf16[4,272,256]{2,1,0:T(8,128)(2,1)S(1)}, u32[]{:S(2)}) copy-start(bf16[4,272,256]{2,1,0:T(8,128)(2,1)S(1)} %get-tuple-element.30.ab_ref.oab_ref) | copy-start | bytes 1671172
  131.2 2.0 %collective-permute-start.21 = (bf16[4,272,256]{2,1,0:T(8,128)(2,1)S(1)}, bf16[4,272,256]{2,1,0:T(8,128)(2,1)S(1)}, u32[]{:S(2)}, u32[]{:S(2)}) collective-permute-start(bf16[4,272,256]{2,1,0:T(8,128)(2,1)S(1)} %get-tuple-element.33), channel_id=1, source_target_pairs={{0,16},{1,17},{2,18},{3,19},{4,20},{5,21},{6,22},{7,23},{8,24},{9,... | collective-permute-start | bytes 1671176 | tf_op jit(solution)/shard_map/ppermute | solution.py:424
  131.3 15.4 %collective-permute-start.26 = (bf16[2,4,80,640]{3,2,1,0:T(8,128)(2,1)}, bf16[2,4,80,640]{3,2,1,0:T(8,128)(2,1)}, u32[]{:S(2)}, u32[]{:S(2)}) collective-permute-start(bf16[2,4,80,640]{3,2,1,0:T(8,128)(2,1)} %bitcast_dynamic-update-slice_fusion.3.refs_4_), channel_id=1, source_target_pairs={{0,16},{1,17},{2,18},{3,19},{4,20},{5,21},{6,22},{7,23},{8,24},{9,... | collective-permute-start | bytes 2457608 | tf_op jit(solution)/shard_map/ppermute | solution.py:424
  131.8 15.3 %collective-permute-start.22 = (bf16[4,2,80,640]{3,2,1,0:T(8,128)(2,1)}, bf16[4,2,80,640]{3,2,1,0:T(8,128)(2,1)}, u32[]{:S(2)}, u32[]{:S(2)}) collective-permute-start(bf16[4,2,80,640]{3,2,1,0:T(8,128)(2,1)} %bitcast_dynamic-update-slice_fusion.4.refs_0_), channel_id=1, source_target_pairs={{0,16},{1,17},{2,18},{3,19},{4,20},{5,21},{6,22},{7,23},{8,24},{9,... | collective-permute-start | bytes 2457608 | tf_op jit(solution)/shard_map/ppermute | solution.py:424
  133.0 14.2 %collective-permute-start.27 = (bf16[2,4,80,640]{3,2,1,0:T(8,128)(2,1)}, bf16[2,4,80,640]{3,2,1,0:T(8,128)(2,1)}, u32[]{:S(2)}, u32[]{:S(2)}) collective-permute-start(bf16[2,4,80,640]{3,2,1,0:T(8,128)(2,1)} %collective-permute-done.11.refs_5_), channel_id=1, source_target_pairs={{0,16},{1,17},{2,18},{3,19},{4,20},{5,21},{6,22},{7,23},{8,24},{9,... | collective-permute-start | bytes 2457608 | tf_op jit(solution)/shard_map/ppermute | solution.py:424
  133.0 4.2 %copy-start.7 = (bf16[2,272,256]{2,1,0:T(8,128)(2,1)}, bf16[2,272,256]{2,1,0:T(8,128)(2,1)S(1)}, u32[]{:S(2)}) copy-start(bf16[2,272,256]{2,1,0:T(8,128)(2,1)S(1)} %collective-permute-done.20.c_ref.tc_ref) | copy-start | bytes 835588
  133.2 4.0 %copy-start.11 = (bf16[4,272,256]{2,1,0:T(8,128)(2,1)}, bf16[4,272,256]{2,1,0:T(8,128)(2,1)S(1)}, u32[]{:S(2)}) copy-start(bf16[4,272,256]{2,1,0:T(8,128)(2,1)S(1)} %collective-permute-done.21.ab_ref.tab_ref) | copy-start | bytes 1671172
  137.2 8.2 %copy-start.19 = (s32[16]{0:T(128)S(1)}, s32[16]{0:T(128)}, u32[]{:S(2)}) copy-start(s32[16]{0:T(128)} %constant.89.clone) | copy-start | bytes 196
  137.2 8.2 %copy-start.20 = (s32[16]{0:T(128)S(1)}, s32[16]{0:T(128)}, u32[]{:S(2)}) copy-start(s32[16]{0:T(128)} %constant.90.clone) | copy-start | bytes 196
  137.2 10.5 %copy-start.15 = (bf16[2,2560]{1,0:T(2,128)(2,1)S(1)}, bf16[2,2560]{1,0:T(2,128)(2,1)}, u32[]{:S(2)}) copy-start(bf16[2,2560]{1,0:T(2,128)(2,1)} %param.15) | copy-start | bytes 30724
  137.2 11.8 %copy-start.6 = (bf16[2,272,256]{2,1,0:T(8,128)(2,1)S(1)}, bf16[2,272,256]{2,1,0:T(8,128)(2,1)}, u32[]{:S(2)}) copy-start(bf16[2,272,256]{2,1,0:T(8,128)(2,1)} %copy-done.5) | copy-start | bytes 835588
  137.2 11.8 %copy-start.10 = (bf16[4,272,256]{2,1,0:T(8,128)(2,1)S(1)}, bf16[4,272,256]{2,1,0:T(8,128)(2,1)}, u32[]{:S(2)}) copy-start(bf16[4,272,256]{2,1,0:T(8,128)(2,1)} %copy-done.9) | copy-start | bytes 1671172
  137.2 32.2 %all-to-all-start.1 = ((bf16[128,2,24,128]{3,2,1,0:T(8,128)(2,1)}), bf16[128,2,24,128]{3,2,1,0:T(8,128)(2,1)S(1)}, u32[]{:S(2)}, u32[]{:S(2)}) async-start(bf16[128,2,24,128]{3,2,1,0:T(8,128)(2,1)} %bitcast.26), calls=%async_computation.1 | async-start | bytes 3145728 | tf_op jit(solution)/shard_map/all_to_all | solution.py:405
  145.4 24.7 %collective-permute-start.23 = (bf16[4,2,80,640]{3,2,1,0:T(8,128)(2,1)}, bf16[4,2,80,640]{3,2,1,0:T(8,128)(2,1)}, u32[]{:S(2)}, u32[]{:S(2)}) collective-permute-start(bf16[4,2,80,640]{3,2,1,0:T(8,128)(2,1)} %collective-permute-done.7.refs_1_), channel_id=1, source_target_pairs={{0,16},{1,17},{2,18},{3,19},{4,20},{5,21},{6,22},{7,23},{8,24},{9,... | collective-permute-start | bytes 2457608 | tf_op jit(solution)/shard_map/ppermute | solution.py:424
  146.6 23.5 %collective-permute-start.24 = (bf16[4,2,80,640]{3,2,1,0:T(8,128)(2,1)}, bf16[4,2,80,640]{3,2,1,0:T(8,128)(2,1)}, u32[]{:S(2)}, u32[]{:S(2)}) collective-permute-start(bf16[4,2,80,640]{3,2,1,0:T(8,128)(2,1)} %collective-permute-done.16.refs_2_), channel_id=1, source_target_pairs={{0,16},{1,17},{2,18},{3,19},{4,20},{5,21},{6,22},{7,23},{8,24},{9,... | collective-permute-start | bytes 2457608 | tf_op jit(solution)/shard_map/ppermute | solution.py:424
  146.7 23.5 %collective-permute-start.28 = (bf16[2,4,80,640]{3,2,1,0:T(8,128)(2,1)}, bf16[2,4,80,640]{3,2,1,0:T(8,128)(2,1)}, u32[]{:S(2)}, u32[]{:S(2)}) collective-permute-start(bf16[2,4,80,640]{3,2,1,0:T(8,128)(2,1)} %collective-permute-done.18.refs_6_), channel_id=1, source_target_pairs={{0,16},{1,17},{2,18},{3,19},{4,20},{5,21},{6,22},{7,23},{8,24},{9,... | collective-permute-start | bytes 2457608 | tf_op jit(solution)/shard_map/ppermute | solution.py:424
  147.1 23.0 %collective-permute-start.25 = (bf16[4,2,80,640]{3,2,1,0:T(8,128)(2,1)}, bf16[4,2,80,640]{3,2,1,0:T(8,128)(2,1)}, u32[]{:S(2)}, u32[]{:S(2)}) collective-permute-start(bf16[4,2,80,640]{3,2,1,0:T(8,128)(2,1)} %collective-permute-done.17.refs_3_), channel_id=1, source_target_pairs={{0,16},{1,17},{2,18},{3,19},{4,20},{5,21},{6,22},{7,23},{8,24},{9,... | collective-permute-start | bytes 2457608 | tf_op jit(solution)/shard_map/ppermute | solution.py:424
  147.2 23.0 %collective-permute-start.29 = (bf16[2,4,80,640]{3,2,1,0:T(8,128)(2,1)}, bf16[2,4,80,640]{3,2,1,0:T(8,128)(2,1)}, u32[]{:S(2)}, u32[]{:S(2)}) collective-permute-start(bf16[2,4,80,640]{3,2,1,0:T(8,128)(2,1)} %collective-permute-done.19.refs_7_), channel_id=1, source_target_pairs={{0,16},{1,17},{2,18},{3,19},{4,20},{5,21},{6,22},{7,23},{8,24},{9,... | collective-permute-start | bytes 2457608 | tf_op jit(solution)/shard_map/ppermute | solution.py:424
  149.0 1.6 copy-start.13
  150.6 8.2 %copy-start.8 = (bf16[2,272,256]{2,1,0:T(8,128)(2,1)S(1)}, bf16[2,272,256]{2,1,0:T(8,128)(2,1)}, u32[]{:S(2)}) copy-start(bf16[2,272,256]{2,1,0:T(8,128)(2,1)} %copy-done.7) | copy-start | bytes 835588
  150.6 8.2 %copy-start.12 = (bf16[4,272,256]{2,1,0:T(8,128)(2,1)S(1)}, bf16[4,272,256]{2,1,0:T(8,128)(2,1)}, u32[]{:S(2)}) copy-start(bf16[4,272,256]{2,1,0:T(8,128)(2,1)} %copy-done.11) | copy-start | bytes 1671172
Sparse Core Ops, SparseCore 0:
  13.2 98.0 all-gather.1

commit v3 on v2

--- a/solution.py
+++ b/solution.py
@@ -211,27 +211,46 @@
     )(z, *pieces)
 
 
-def place_body(to_ref, rows_ref, out_ref):
+def place_body(slot_ref, here_ref, rows_ref, out_ref):
+    here = here_ref[0]
     for i in range(rows_ref.shape[0]):
-        out_ref[to_ref[i]] = rows_ref[i]
-
-
-def place(rows, to, places):
+        core, z, each = i // 8, i // 2 % 4, i % 2
+        source = (here & 0b1101100) | (core * 16 + z)
+        slot = slot_ref[source * 2 + each]
+        to = slot >> 1
+
+        @pl.when((to & 0b0010011) == (here & 0b0010011))
+        def _():
+            chip = ((to >> 5) << 2) | ((to >> 2) & 3)
+            out_ref[chip * 2 + (slot & 1)] = rows_ref[i]
+
+
+def place(slots, here, rows):
+    smem = pl.BlockSpec(memory_space=pltpu.SMEM)
+    vmem = pl.BlockSpec(memory_space=pltpu.VMEM)
     return pl.pallas_call(
         place_body,
-        in_specs=[pl.BlockSpec(memory_space=pltpu.SMEM), pl.BlockSpec(memory_space=pltpu.VMEM)],
-        out_specs=pl.BlockSpec(memory_space=pltpu.VMEM),
-        out_shape=jax.ShapeDtypeStruct((places,) + rows.shape[1:], BF16),
+        in_specs=[smem, smem, vmem],
+        out_specs=vmem,
+        out_shape=jax.ShapeDtypeStruct((32,) + rows.shape[1:], BF16),
         compiler_params=params(8),
         name="place",
-    )(to, rows)
+    )(slots, here, rows)
 
 
 def pick_body(came_ref, slab_ref, out_ref):
     out_ref[...] = slab_ref[...]
 
 
-def pick(arrived, came_from):
+def by_device(came):
+    return came >> 1
+
+
+def by_chip(came):
+    return ((came >> 6) << 2) | ((came >> 3) & 3)
+
+
+def pick(arrived, came_from, where):
     slab = arrived.shape[1:]
     return pl.pallas_call(
         pick_body,
@@ -239,7 +258,7 @@
             num_scalar_prefetch=1,
             grid=(2,),
             in_specs=[
-                pl.BlockSpec((1,) + slab, lambda i, s: (lax.shift_right_logical(s[i], 1) * 2 + i, 0, 0))
+                pl.BlockSpec((1,) + slab, lambda i, s: (where(s[i]) * 2 + i, 0, 0))
             ],
             out_specs=pl.BlockSpec((1,) + slab, lambda i, s: (i, 0, 0)),
         ),
@@ -249,14 +268,18 @@
     )(came_from, arrived)
 
 
-def span_body(index_ref, ab_ref, c_ref, k_ref, v_ref, cache_ref, out_ref):
+def span_body(index_ref, ab1_ref, c1_ref, ab2_ref, c2_ref, k_ref, v_ref, cache_ref, out_ref):
     index = index_ref[0]
-    q = jnp.where(pl.program_id(0) < pl.num_programs(0) - 1, ab_ref[0], c_ref[0])
-    rows, hd = q.shape
+    last = pl.program_id(0) == pl.num_programs(0) - 1
+    rows, hd = k_ref.shape
+    q = jnp.concatenate(
+        [jnp.where(last, c1_ref[0], ab1_ref[0]), jnp.where(last, c2_ref[0], ab2_ref[0])], 0
+    )
+    both = 2 * rows
     blocks = cache_ref.shape[1] // rows
     wrapped = index >= blocks
-    row = lax.broadcasted_iota(jnp.int32, (rows, rows), 0)
-    col = lax.broadcasted_iota(jnp.int32, (rows, rows), 1)
+    row = lax.rem(lax.broadcasted_iota(jnp.int32, (both, rows), 0), rows)
+    col = lax.broadcasted_iota(jnp.int32, (both, rows), 1)
     own = col <= row
     starts, scores, shifts = [], [], []
     top = None
@@ -276,8 +299,8 @@
         top = peak if top is None else jnp.maximum(top, peak)
     scale = LOG2E * hd**-0.5
     base = top * scale
-    total = jnp.zeros((rows, 1), F32)
-    mixed = jnp.zeros((rows, hd), F32)
+    total = jnp.zeros((both, 1), F32)
+    mixed = jnp.zeros((both, hd), F32)
     for rel in range(blocks):
         terms = jnp.exp2(scores[rel] * scale - (base - shifts[rel]))
         total += jnp.sum(terms, 1, keepdims=True)
@@ -287,42 +310,43 @@
             mixed += dot(jnp.where(own, 0.0, terms).astype(BF16), old_values)
         else:
             mixed += dot(terms.astype(BF16), old_values)
-    out_ref[...] = (mixed / total).astype(BF16)
-
-
-def span_attend(index, ab, c, key, value, rows, cache):
-    heads, hd = ab.shape[0] + 1, ab.shape[2]
+    made = (mixed / total).astype(BF16)
+    out_ref[0] = made[:rows]
+    out_ref[1] = made[rows:]
+
+
+def span_attend(index, ours, theirs, key, value, rows, cache):
+    half, hd = ours[0].shape[0] + 1, ours[0].shape[2]
+    heads = 2 * half
     window = cache.shape[1]
+    many = pl.BlockSpec((1, rows, hd), lambda h, s: (jnp.minimum(h, half - 2), 0, 0))
+    single = pl.BlockSpec((1, rows, hd), lambda h, s: (0, 0, 0))
+    pair = pl.BlockSpec((rows, hd), lambda h, s: (0, 0))
     return pl.pallas_call(
         span_body,
         grid_spec=pltpu.PrefetchScalarGridSpec(
             num_scalar_prefetch=1,
-            grid=(heads,),
-            in_specs=[
-                pl.BlockSpec((1, rows, hd), lambda h, s: (jnp.minimum(h, heads - 2), 0, 0)),
-                pl.BlockSpec((1, rows, hd), lambda h, s: (0, 0, 0)),
-                pl.BlockSpec((rows, hd), lambda h, s: (0, 0)),
-                pl.BlockSpec((rows, hd), lambda h, s: (0, 0)),
-                pl.BlockSpec((1, window, 2 * hd), lambda h, s: (0, 0, 0)),
-            ],
-            out_specs=pl.BlockSpec((rows, hd), lambda h, s: (0, h)),
-        ),
-        out_shape=jax.ShapeDtypeStruct((rows, heads * hd), BF16),
-        compiler_params=params(32, "arbitrary"),
+            grid=(half,),
+            in_specs=[many, single, many, single, pair, pair]
+            + [pl.BlockSpec((1, window, 2 * hd), lambda h, s: (0, 0, 0))],
+            out_specs=pl.BlockSpec((2, rows, hd), lambda h, s: (0, 0, h)),
+        ),
+        out_shape=jax.ShapeDtypeStruct((2, rows, half * hd), BF16),
+        compiler_params=params(36, "arbitrary"),
         cost_estimate=pl.CostEstimate(
             flops=4 * heads * rows * hd * (window + rows),
             bytes_accessed=4 * hd * window,
             transcendentals=heads * rows * window,
         ),
         name="span_attend",
-    )(index, ab, c, key, value, cache)
+    )(index, *ours, *theirs, key, value, cache)
 
 
 def finish_body(
-    info_ref, att1_ref, att2_ref, datt_ref, x_ref, dx_ref, *refs
+    info_ref, att_ref, datt_ref, x_ref, dx_ref, *refs
 ):
     chunks, (out_ref, dout_ref, lhs, w, sem) = refs[:16], refs[16:]
-    rows, k = att1_ref.shape
+    rows, k = att_ref.shape[1:]
     step = pl.program_id(0)
     core = info_ref[0]
 
@@ -340,8 +364,8 @@
         for quarter in range(4):
             for copy in copies(quarter):
                 copy.start()
-        lhs[core, :rows] = att1_ref[...]
-        lhs[1 - core, :rows] = att2_ref[...]
+        lhs[core, :rows] = att_ref[0]
+        lhs[1 - core, :rows] = att_ref[1]
         lhs[0, rows:] = datt_ref[:, :k]
         lhs[1, rows:] = datt_ref[:, k:]
 
@@ -361,7 +385,7 @@
     dout_ref[...] = (dx_ref[...].astype(F32) + total[rows:]).astype(BF16)
 
 
-def finish(info, att1, att2, datt, x, dx, chunks):
+def finish(info, att, datt, x, dx, chunks):
     rows, n = x.shape
     drows = dx.shape[0]
     run, bn = chunks[0].shape[2:]
@@ -375,8 +399,7 @@
             num_scalar_prefetch=1,
             grid=(4,),
             in_specs=[
-                pl.BlockSpec(att1.shape, lambda i, s: (0, 0)),
-                pl.BlockSpec(att2.shape, lambda i, s: (0, 0)),
+                pl.BlockSpec(att.shape, lambda i, s: (0, 0, 0)),
                 pl.BlockSpec(datt.shape, lambda i, s: (0, 0)),
                 pl.BlockSpec((rows, bn), column),
                 pl.BlockSpec((drows, bn), column),
@@ -393,16 +416,17 @@
             jax.ShapeDtypeStruct((rows, n), BF16),
             jax.ShapeDtypeStruct((drows, n), BF16),
         ],
-        compiler_params=params(48, "arbitrary"),
+        compiler_params=params(60, "arbitrary"),
         cost_estimate=pl.CostEstimate(
             flops=2 * rows * n * n, bytes_accessed=2 * n * n, transcendentals=0
         ),
         name="finish",
-    )(info, att1, att2, datt, x, dx, *chunks)
-
-
-def exchange(sent, devices):
-    got = lax.all_to_all(sent.reshape((devices, -1) + sent.shape[1:]), AXES, 0, 0)
+    )(info, att, datt, x, dx, *chunks)
+
+
+def exchange(sent, axes):
+    members = lax.axis_size(axes)
+    got = lax.all_to_all(sent.reshape((members, -1) + sent.shape[1:]), axes, 0, 0)
     return got.reshape(sent.shape)
 
 
@@ -478,16 +502,17 @@
     digits = jnp.stack([decode_length // 256, decode_length % 256], 1).astype(BF16)
     tagged = jnp.concatenate([decode_tokens, jnp.pad(digits, ((0, 0), (0, 510)))], 1)
     tagged = tagged.reshape(own, SLAB, 128)
-    tagged = place(tagged, slot_of_mine, places)
-
+    tagged = jnp.broadcast_to(tagged, (8,) + tagged.shape).reshape(8 * own, SLAB, 128)
     split = half_q + half_kv
     first_weight = lax.all_gather(piece[:, :split], CHIPS, axis=0, tiled=True)
 
     here = {axis: (device >> shift) & 3 for axis, shift in (("y", 5), ("x", 2), ("z", 0))}
     back = 1 - 2 * ((device >> 4) & 1)
     came = {axis: [(at - back * k) & 3 for k in range(4)] for axis, at in here.items()}
-    strip, tagged = lax.optimization_barrier((piece[:, split:], tagged))
+    strip = piece[:, split:]
     strips = [strip] + [send(strip, "z", k) for k in (1, 2, 3)]
+    tagged, _ = lax.optimization_barrier((tagged, strips))
+    tagged = place(cache_slot, device.astype(jnp.int32)[None], exchange(tagged, ("c", "z")))
     strips = interleave(here["z"].astype(jnp.int32)[None], strips)
     bn = half_q // 2
     stack = [strips[:, :, :bn], strips[:, :, bn:]]
@@ -500,7 +525,7 @@
         for i, (axis, dim, _, _) in enumerate(plan):
             stack[i] = send(stack[i], axis, RING) if k else stack[i]
             parts[i] = put(parts[i], stack[i], came[axis][k], dim)
-    arrived = pick(exchange(tagged, devices), request_of_mine)
+    arrived = pick(exchange(tagged, ("y", "x")), request_of_mine, by_chip)
     arrived = arrived.reshape(own, SLAB * 128)
     own_tokens = jnp.pad(arrived[:, :width], ((0, EXTRA - own), (0, 0)))
     tags = arrived[:, width : width + 2].astype(jnp.int32)
@@ -530,42 +555,56 @@
     lhs = norm_ordered(both_decodes, norm_gain, order, total, 2 * EXTRA, at, (lhs,))
     mine = [[part] for part in parts]
     theirs = [[swap(part)] for part in parts]
-    for k in (1, 2, 3):
-        if k == 2:
-            parts, lhs, cos, sin = lax.optimization_barrier((parts, lhs, cos, sin))
+    def ring_step(parts):
         parts = [send(part, p[2], RING) for part, p in zip(parts, plan)]
         for i in range(2):
             mine[i].append(parts[i])
-            if k < 3:
-                theirs[i].append(swap(parts[i]))
+        return parts
+
+    def swap_last(after):
+        parts, _ = lax.optimization_barrier(([m[-1] for m in mine], after))
+        for i in range(2):
+            theirs[i].append(swap(parts[i]))
+
+    parts = ring_step(parts)
+    swap_last(())
+    shifts = jnp.asarray([2] * 4 + [5] * 4 + [2] * 4 + [5] * 4, jnp.int32)
+    steps = jnp.asarray([0, 1, 2, 3] * 2 + [0, -1, -2, -3] * 2, jnp.int32)
+    came_from = (((device.astype(jnp.int32) >> shifts) & 3) - (1 - 2 * core) * steps) & 3
+    finish_info = jnp.concatenate([core[None], came_from])
+    decode_rows = jnp.pad(decode_tokens, ((0, EXTRA - own), (0, 0)))
+    info = jnp.concatenate([own_length, request_of_mine, core[None]])
+    parts, lhs, cos, sin, finish_info, decode_rows, info = lax.optimization_barrier(
+        (parts, lhs, cos, sin, finish_info, decode_rows, info)
+    )
+    ring_step(parts)
+    first_weight = pltpu.with_memory_space_constraint(first_weight, pltpu.HBM)
     ours_c, other_c = project(4, 2, rows, lhs, first_weight, cos, sin, hd)
     theirs_c = swap(other_c)
     ours_ab, other_ab = project(0, 4, rows, lhs, first_weight, cos, sin, hd)
     theirs_ab = swap(other_ab)
-    parts, ours_ab = lax.optimization_barrier((parts, ours_ab))
-    for i in range(2):
-        theirs[i].append(swap(parts[i]))
+    swap_last(ours_ab)
+    parts, _ = lax.optimization_barrier(([m[-1] for m in mine], ours_ab))
+    ring_step(parts)
 
     key = jnp.where(first_core, ours_c[1], theirs_c[1])
     value = jnp.where(first_core, theirs_c[1], ours_c[1])
     keyval = jnp.concatenate([key, value], 1)
     decode_keyval = keyval[rows : rows + own]
-    info = jnp.concatenate([own_length, request_of_mine, core[None]])
     quarters = (ours_ab, ours_c, theirs_ab, theirs_c)
-    home = exchange(decode_attend(info, quarters, keyval, decode_cache, places), devices)
-    att1 = span_attend(span_index, ours_ab, ours_c, key, value, rows, span_cache)
-    att2 = span_attend(span_index, theirs_ab, theirs_c, key, value, rows, span_cache)
-    home = pick(home, slot_of_mine).reshape(own, SLAB * 128)[:, :width]
-    shifts = jnp.asarray([2] * 4 + [5] * 4 + [2] * 4 + [5] * 4, jnp.int32)
-    steps = jnp.asarray([0, 1, 2, 3] * 2 + [0, -1, -2, -3] * 2, jnp.int32)
-    came_from = (((device.astype(jnp.int32) >> shifts) & 3) - (1 - 2 * core) * steps) & 3
+    routed = decode_attend(info, quarters, keyval, decode_cache, places)
+    home = exchange(routed, AXES)
+    swap_last(routed)
+    att = span_attend(
+        span_index, (ours_ab, ours_c), (theirs_ab, theirs_c), key, value, rows, span_cache
+    )
+    home = pick(home, slot_of_mine, by_device).reshape(own, SLAB * 128)[:, :width]
     span_output, decode_output = finish(
-        jnp.concatenate([core[None], came_from]),
-        att1,
-        att2,
+        finish_info,
+        att,
         jnp.pad(home, ((0, EXTRA - own), (0, 0))),
         span_tokens[0],
-        jnp.pad(decode_tokens, ((0, EXTRA - own), (0, 0))),
+        decode_rows,
         [c for half in (mine, theirs) for part in half for c in part],
     )
     return span_output[None], keyval[:rows][None], decode_output[:own], decode_keyval

time: 189 us -> 179 us (0.947)
  waiting for transfers between devices: 44.1 us -> 32.4 us
  starting transfers between devices: 57.5 us -> 51.4 us
  local copies, waits for them, and re-layouts: 18.3 us -> 23.2 us
  other arithmetic: 7.66 us -> 10.3 us
    ppermute x15, waiting for transfers between devices: 39.9 us -> 24.8 us  [send(): return lax.ppermute(v, AXES, list(zip(DEVICES.tolist(), to.tolist())))]
    ppermute x15, starting transfers between devices: 32.1 us -> 27 us  [send(): return lax.ppermute(v, AXES, list(zip(DEVICES.tolist(), to.tolist())))]
    all_to_all x2 -> x3, waiting for transfers between devices: 2.34 us -> 5.86 us  [exchange(): lax.all_to_all(sent.reshape((members, -1) + sent.shape[1:]), axes, 0, 0)]
    dynamic_update_slice x8, local copies, waits for them, and re-layouts: 5.61 us -> 8.36 us  [put(): return lax.dynamic_update_slice(whole, jnp.expand_dims(piece, place), start)]
    pallas_call x2, Pallas kernels: 6.34 us -> 9.03 us  [project(): pl.pallas_call(functools.partial(project_body, rows), grid=(count,), in_s...]
    pallas_call x2 -> x1, Pallas kernels: 16.5 us -> 14.4 us  [span_attend(): pl.pallas_call(span_body, grid_spec=pltpu.PrefetchScalarGridSpec(num_scal...]
    all_to_all x2 -> x3, starting transfers between devices: 16.7 us -> 15.4 us  [exchange(): lax.all_to_all(sent.reshape((members, -1) + sent.shape[1:]), axes, 0, 0)]
    unnamed x46 -> x30, local copies, waits for them, and re-layouts: 6.13 us -> 4.88 us
  transfers between devices with their start and end apart: 33 -> 34, of which waited for: 10 -> 9; matrix products, arithmetic and copies ran while one was open for 9% -> 14% of each run, Pallas kernels for 19% -> 19%
where the time goes in v3:
time: 179 us; the launch traced here: 178 us
  starting transfers between devices  51.4 us (29%)
  Pallas kernels  45.3 us (25%)
  waiting for transfers between devices  32.4 us (18%)
  local copies, waits for them, and re-layouts  23.2 us (13%)
  between operations  15.1 us (8%)
  other arithmetic  10.3 us (6%)
    ppermute x15, starting transfers between devices, send(): return lax.ppermute(v, AXES, list(zip(DEVICES.tolist(), to.tolist())))  27 us
    ppermute x15, waiting for transfers between devices, send(): return lax.ppermute(v, AXES, list(zip(DEVICES.tolist(), to.tolist())))  24.8 us
    all_to_all x3, starting transfers between devices, exchange(): lax.all_to_all(sent.reshape((members, -1) + sent.shape[1:]), axes, 0, 0)  15.4 us
    pallas_call x1, Pallas kernels, span_attend(): pl.pallas_call(span_body, grid_spec=pltpu.PrefetchScalarGridSpec(num_scal...  14.4 us
    pallas_call x1, Pallas kernels, finish(): pl.pallas_call(finish_body, grid_spec=pltpu.PrefetchScalarGridSpec(num_sc...  10.7 us
    pallas_call x2, Pallas kernels, project(): pl.pallas_call(functools.partial(project_body, rows), grid=(count,), in_s...  9.03 us
    ppermute x15, starting transfers between devices, swap(): lax.ppermute(v, AXES, list(zip(DEVICES.tolist(), (DEVICES ^ 16).tolist())))  8.96 us
    dynamic_update_slice x8, local copies, waits for them, and re-layouts, put(): return lax.dynamic_update_slice(whole, jnp.expand_dims(piece, place), start)  8.36 us
  transfers between devices with their start and end apart: 34, of which 9 were waited for; matrix products, arithmetic and copies ran while one was open for 14% of the time, Pallas kernels for 19%

profile of v3, /device:TPU:1, one launch (start us, length us, event | category | flops | bytes accessed | tf_op | source)
XLA Modules:
  0.0 177.7 jit_solution(5472067125044901788)
XLA Ops:
  7.2 0.9 fusion.14
  8.1 0.7 fusion.15
  8.8 0.9 fusion.13
  9.8 1.5 collective-permute-start
  11.3 1.0 collective-permute-done
  15.2 0.7 fusion.8
  15.9 0.7 broadcast_in_dim.79.gain_ref
  16.6 1.4 pad.21.dx_ref
  18.0 0.7 subtract_and_fusion
  18.7 1.4 compare_reduce_fusion
  20.0 1.8 %fusion.order_ref = bf16[640,640]{1,0:T(8,128)(2,1)} fusion(s32[640]{0:T(1024)} %constant.88.clone), kind=kLoop, calls=%fused_computation.2 | loop fusion | flops 819200 | bytes 821760 | tf_op jit(solution)/shard_map/convert_element_type | solution.py:34
  21.8 1.8 %collective-permute-start.1 = (bf16[40,1280]{1,0:T(8,128)(2,1)S(1)}, bf16[40,1280]{1,0:T(8,128)(2,1)S(1)}, u32[]{:S(2)}, u32[]{:S(2)}) collective-permute-start(bf16[40,1280]{1,0:T(8,128)(2,1)S(1)} %slice.82.refs_0_), channel_id=1, source_target_pairs={{0,1},{1,2},{2,3},{3,0},{4,5},{5,6},{6,7},{7,4},{8,9},{9,10},{10,1... | collective-permute-start | bytes 307208 | tf_op jit(solution)/shard_map/ppermute | solution.py:444
  23.6 3.3 %collective-permute-start.2 = (bf16[40,1280]{1,0:T(8,128)(2,1)S(1)}, bf16[40,1280]{1,0:T(8,128)(2,1)S(1)}, u32[]{:S(2)}, u32[]{:S(2)}) collective-permute-start(bf16[40,1280]{1,0:T(8,128)(2,1)S(1)} %slice.82.refs_0_), channel_id=1, source_target_pairs={{0,2},{1,3},{2,0},{3,1},{4,6},{5,7},{6,4},{7,5},{8,10},{9,11},{10,... | collective-permute-start | bytes 307208 | tf_op jit(solution)/shard_map/ppermute | solution.py:444
  26.9 0.7 collective-permute-start.3
  28.7 3.5 %collective-permute-done.2.refs_2_ = bf16[40,1280]{1,0:T(8,128)(2,1)S(1)} collective-permute-done((bf16[40,1280]{1,0:T(8,128)(2,1)S(1)}, bf16[40,1280]{1,0:T(8,128)(2,1)S(1)}, u32[]{:S(2)}, u32[]{:S(2)}) %collective-permute-start.2) | collective-permute-done | bytes 102432 | tf_op jit(solution)/shard_map/ppermute | solution.py:444
  32.4 2.8 %collective-permute-start.4 = (bf16[2,80,640]{2,1,0:T(8,128)(2,1)S(1)}, bf16[2,80,640]{2,1,0:T(8,128)(2,1)}, u32[]{:S(2)}, u32[]{:S(2)}) collective-permute-start(bf16[2,80,640]{2,1,0:T(8,128)(2,1)S(1)} %get-tuple-element.51), channel_id=1, source_target_pairs={{0,32},{1,33},{2,34},{3,35},{4,36},{5,37},{6,38},{7,39},{8,40},{9,... | collective-permute-start | bytes 614408 | tf_op jit(solution)/shard_map/ppermute | solution.py:444
  35.2 2.5 %collective-permute-start.8 = (bf16[2,80,640]{2,1,0:T(8,128)(2,1)S(1)}, bf16[2,80,640]{2,1,0:T(8,128)(2,1)}, u32[]{:S(2)}, u32[]{:S(2)}) collective-permute-start(bf16[2,80,640]{2,1,0:T(8,128)(2,1)S(1)} %get-tuple-element.50), channel_id=1, source_target_pairs={{0,4},{1,5},{2,6},{3,7},{4,8},{5,9},{6,10},{7,11},{8,12},{9,13},{1... | collective-permute-start | bytes 614408 | tf_op jit(solution)/shard_map/ppermute | solution.py:444
  38.3 3.8 %all-to-all-start = ((bf16[8,2,24,128]{3,2,1,0:T(8,128)(2,1)}), bf16[8,2,24,128]{3,2,1,0:T(8,128)(2,1)S(1)}, u32[]{:S(2)}, u32[]{:S(2)}) async-start(bf16[8,2,24,128]{3,2,1,0:T(8,128)(2,1)} %bitcast.16), calls=%async_computation | async-start | bytes 196608 | tf_op jit(solution)/shard_map/all_to_all | solution.py:429
  42.1 1.0 broadcast_in_dim.66
  43.1 0.7 bitcast_dynamic-update-slice_fusion.7
  43.8 1.0 broadcast_in_dim.72
  44.8 0.7 bitcast_dynamic-update-slice_fusion.2
  45.5 1.7 all-to-all-done
  47.1 1.4 place.1
  48.5 5.2 %all-to-all-start.1 = ((bf16[16,2,24,128]{3,2,1,0:T(8,128)(2,1)}), bf16[16,2,24,128]{3,2,1,0:T(8,128)(2,1)S(1)}, u32[]{:S(2)}, u32[]{:S(2)}) async-start(bf16[16,2,24,128]{3,2,1,0:T(8,128)(2,1)} %bitcast.18), calls=%async_computation.1 | async-start | bytes 393216 | tf_op jit(solution)/shard_map/all_to_all | solution.py:429
  53.7 2.6 %collective-permute-start.5 = (bf16[2,80,640]{2,1,0:T(8,128)(2,1)}, bf16[2,80,640]{2,1,0:T(8,128)(2,1)}, u32[]{:S(2)}, u32[]{:S(2)}) collective-permute-start(bf16[2,80,640]{2,1,0:T(8,128)(2,1)} %collective-permute-done.4), channel_id=1, source_target_pairs={{0,32},{1,33},{2,34},{3,35},{4,36},{5,37},{6,38},{7,39},{8,40},{9,... | collective-permute-start | bytes 614408 | tf_op jit(solution)/shard_map/ppermute | solution.py:444
  56.4 2.4 %collective-permute-start.9 = (bf16[2,80,640]{2,1,0:T(8,128)(2,1)}, bf16[2,80,640]{2,1,0:T(8,128)(2,1)S(1)}, u32[]{:S(2)}, u32[]{:S(2)}) collective-permute-start(bf16[2,80,640]{2,1,0:T(8,128)(2,1)} %collective-permute-done.8), channel_id=1, source_target_pairs={{0,4},{1,5},{2,6},{3,7},{4,8},{5,9},{6,10},{7,11},{8,12},{9,13},{1... | collective-permute-start | bytes 614408 | tf_op jit(solution)/shard_map/ppermute | solution.py:444
  58.8 1.6 bitcast_dynamic-update-slice_fusion.6
  60.4 1.6 bitcast_dynamic-update-slice_fusion.1
  62.0 0.8 all-to-all-done.1
  63.8 1.2 collective-permute-start.15
  65.1 0.7 collective-permute-done.15
  65.9 1.0 fusion.4
  67.5 0.8 pad_maximum_fusion.2.sin_ref
  68.3 0.7 collective-permute-start.6
  69.0 1.3 collective-permute-start.10
  70.3 1.6 bitcast_dynamic-update-slice_fusion.5
  72.0 0.7 bitcast_dynamic-update-slice_fusion
  72.7 5.0 %collective-permute-done.6 = bf16[2,80,640]{2,1,0:T(8,128)(2,1)S(1)} collective-permute-done((bf16[2,80,640]{2,1,0:T(8,128)(2,1)}, bf16[2,80,640]{2,1,0:T(8,128)(2,1)S(1)}, u32[]{:S(2)}, u32[]{:S(2)}) %collective-permute-start.6) | collective-permute-done | bytes 204832 | tf_op jit(solution)/shard_map/ppermute | solution.py:444
  77.7 0.7 bitcast_dynamic-update-slice_fusion.4.refs_0_
  78.4 0.7 bitcast_dynamic-update-slice_fusion.3.refs_4_
  79.1 2.6 %collective-permute-start.11 = (bf16[2,4,80,640]{3,2,1,0:T(8,128)(2,1)}, bf16[2,4,80,640]{3,2,1,0:T(8,128)(2,1)}, u32[]{:S(2)}, u32[]{:S(2)}) collective-permute-start(bf16[2,4,80,640]{3,2,1,0:T(8,128)(2,1)} %bitcast_dynamic-update-slice_fusion.3.refs_4_), channel_id=1, source_target_pairs={{0,32},{1,33},{2,34},{3,35},{4,36},{5,37},{6,38},{7,39},{8,40},{9,... | collective-permute-start | bytes 2457608 | tf_op jit(solution)/shard_map/ppermute | solution.py:444
  82.0 1.0 copy-done
  82.9 4.0 %norm_ordered.2.refs_0_ = bf16[544,2560]{1,0:T(8,128)(2,1)S(1)} custom-call(bf16[512,2560]{1,0:T(8,128)(2,1)S(1)} %pad_maximum_fusion.x_ref, f32[1,2560]{1,0:T(1,128)S(1)} %broadcast_in_dim.79.gain_ref, bf16[640,640]{1,0:T(8,128)(2,1)S(1)} %copy-done), custom_call_target="tpu_custom_call" | custom-call | flops 1677721600 | bytes 5242880 | tf_op jit(solution)/shard_map/norm_ordered/pallas_call | solution.py:57
  87.4 15.7 %collective-permute-done.7.refs_1_ = bf16[4,2,80,640]{3,2,1,0:T(8,128)(2,1)} collective-permute-done((bf16[4,2,80,640]{3,2,1,0:T(8,128)(2,1)}, bf16[4,2,80,640]{3,2,1,0:T(8,128)(2,1)}, u32[]{:S(2)}, u32[]{:S(2)}) %collective-permute-start.7) | collective-permute-done | bytes 819232 | tf_op jit(solution)/shard_map/ppermute | solution.py:444
  103.2 1.2 collective-permute-start.18
  104.4 2.3 %collective-permute-start.19 = (bf16[2,4,80,640]{3,2,1,0:T(8,128)(2,1)}, bf16[2,4,80,640]{3,2,1,0:T(8,128)(2,1)}, u32[]{:S(2)}, u32[]{:S(2)}) collective-permute-start(bf16[2,4,80,640]{3,2,1,0:T(8,128)(2,1)} %collective-permute-done.11.refs_5_), channel_id=1, source_target_pairs={{0,32},{1,33},{2,34},{3,35},{4,36},{5,37},{6,38},{7,39},{8,40},{9,... | collective-permute-start | bytes 2457608 | tf_op jit(solution)/shard_map/ppermute | solution.py:444
  106.7 1.1 copy-done.1
  107.7 5.6 %project.2 = (bf16[4,272,256]{2,1,0:T(8,128)(2,1)S(1)}, bf16[4,272,256]{2,1,0:T(8,128)(2,1)S(1)}) custom-call(bf16[544,2560]{1,0:T(8,128)(2,1)S(1)} %norm_ordered.3.x_ref, bf16[2560,1536]{1,0:T(8,128)(2,1)} %all-gather.2.cloned.1.call-done.w_ref, f32[2,544,128]{2,1,0:T(8,128)S(1)} %pad_maximum_fusion.1.cos_ref, f32[2,544,128]{2,1,0:T(8,128)S(1)} %copy-done.1), custom_call_target="tpu_custom_call" | custom-call | flops 2852126720 | bytes 5242880 | tf_op jit(solution)/shard_map/project/pallas_call | solution.py:97
  113.4 3.4 %project.3 = (bf16[2,272,256]{2,1,0:T(8,128)(2,1)S(1)}, bf16[2,272,256]{2,1,0:T(8,128)(2,1)S(1)}) custom-call(bf16[544,2560]{1,0:T(8,128)(2,1)S(1)} %norm_ordered.3.x_ref, bf16[2560,1536]{1,0:T(8,128)(2,1)} %all-gather.2.cloned.1.call-done.w_ref, f32[2,544,128]{2,1,0:T(8,128)S(1)} %pad_maximum_fusion.1.cos_ref, f32[2,544,128]{2,1,0:T(8,128)S(1)} %copy-done.1), custom_call_target="tpu_custom_call" | custom-call | flops 1426063360 | bytes 2621440 | tf_op jit(solution)/shard_map/project/pallas_call | solution.py:97
  117.5 1.1 collective-permute-start.26
  118.7 1.5 collective-permute-start.23
  120.1 1.5 collective-permute-start.20
  121.7 1.3 collective-permute-start.21
  123.0 3.9 %decode_attend.1 = bf16[256,24,128]{2,1,0:T(8,128)(2,1)} custom-call(s32[5]{0:T(128)S(1)} %pad_add_fusion.1.info_ref, bf16[4,272,256]{2,1,0:T(8,128)(2,1)S(1)} %get-tuple-element.32.ab1_ref.oab_ref, bf16[2,272,256]{2,1,0:T(8,128)(2,1)S(1)} %get-tuple-element.33.c1_ref.oc_ref, bf16[4,272,256]{2,1,0:T(8,128)(2,1)S(1)} %collective-permute-done.16.ab2_ref.tab_ref, ...), custom_call_target="tpu_custom_call" | custom-call | flops 67108864 | bytes 4194304 | tf_op jit(solution)/shard_map/decode_attend/pallas_call | solution.py:163
  126.9 6.4 %all-to-all-start.2 = ((bf16[128,2,24,128]{3,2,1,0:T(8,128)(2,1)}), bf16[128,2,24,128]{3,2,1,0:T(8,128)(2,1)S(1)}, u32[]{:S(2)}, u32[]{:S(2)}) async-start(bf16[128,2,24,128]{3,2,1,0:T(8,128)(2,1)} %bitcast.30), calls=%async_computation.2 | async-start | bytes 3145728 | tf_op jit(solution)/shard_map/all_to_all | solution.py:429
  133.4 1.1 collective-permute-start.27
  136.2 0.7 fusion.2
  136.9 1.6 copy-done.11
  138.5 14.4 %span_attend.1.att_ref = bf16[2,256,1280]{2,1,0:T(8,128)(2,1)S(1)} custom-call(s32[1]{0:T(128)S(6)} %copy.50.index_ref, bf16[4,272,256]{2,1,0:T(8,128)(2,1)S(1)} %copy-done.7, bf16[2,272,256]{2,1,0:T(8,128)(2,1)S(1)} %copy-done.5, bf16[4,272,256]{2,1,0:T(8,128)(2,1)S(1)} %copy-done.9, bf16[2,272,256]{2,1,0:T(8,128)(2,1)S(1)} %collective-permute-done.17.c2_ref.tc_ref, ...), custom_call_target="tpu_custom_call" | custom-call | flops 6039797760 | bytes 2097152 | tf_op jit(solution)/shard_map/span_attend/pallas_call | solution.py:325
  153.0 1.1 copy-done.3
  154.0 3.4 %all-to-all-done.2 = bf16[128,2,24,128]{3,2,1,0:T(8,128)(2,1)S(1)} async-done(((bf16[128,2,24,128]{3,2,1,0:T(8,128)(2,1)}), bf16[128,2,24,128]{3,2,1,0:T(8,128)(2,1)S(1)}, u32[]{:S(2)}, u32[]{:S(2)}) %all-to-all-start.2) | async-done | bytes 1572896 | tf_op jit(solution)/shard_map/all_to_all | solution.py:429
  158.7 10.7 %finish.1 = (bf16[256,2560]{1,0:T(8,128)(2,1)}, bf16[16,2560]{1,0:T(8,128)(2,1)}) custom-call(s32[17]{0:T(128)} %pad_add_fusion.info_ref, bf16[2,256,1280]{2,1,0:T(8,128)(2,1)} %copy-done.3, bf16[16,2560]{1,0:T(8,128)(2,1)} %pad.22.datt_ref, bf16[256,2560]{1,0:T(8,128)(2,1)} %bitcast.74, bf16[16,2560]{1,0:T(8,128)(2,1)} %pad.21.dx_ref, ...), custom_call_target="tpu_custom_call" | custom-call | flops 3355443200 | bytes 13107200 | tf_op jit(solution)/shard_map/finish/pallas_call | solution.py:396
  169.5 1.4 slice.80
  (99 shorter events, 10.2 us)
Async XLA Ops:
  7.2 99.5 %all-gather.2.cloned.1.call-start = ((), (), s32[]{:S(2)}) async-start(), calls=%async_computation.3 | async-start | bytes 7987200 | tf_op jit(solution)/shard_map/all_gather | solution.py:507
  9.8 2.5 %collective-permute-start = (bf16[20,2816]{1,0:T(8,128)(2,1)S(1)}, bf16[20,2816]{1,0:T(8,128)(2,1)S(1)}, u32[]{:S(2)}, u32[]{:S(2)}) collective-permute-start(bf16[20,2816]{1,0:T(8,128)(2,1)S(1)} %maximum_select_fusion.3), channel_id=1, source_target_pairs={{0,16},{1,17},{2,18},{3,19},{4,20},{5,21},{6,22},{7,23},{8,24},{9,... | collective-permute-start | bytes 337928 | tf_op jit(solution)/shard_map/ppermute | solution.py:448
  13.0 68.7 %collective-permute-start.13 = (bf16[256,2560]{1,0:T(8,128)(2,1)}, bf16[256,2560]{1,0:T(8,128)(2,1)S(1)}, u32[]{:S(2)}, u32[]{:S(2)}) collective-permute-start(bf16[256,2560]{1,0:T(8,128)(2,1)} %bitcast.73), channel_id=1, source_target_pairs={{0,16},{1,17},{2,18},{3,19},{4,20},{5,21},{6,22},{7,23},{8,24},{9,... | collective-permute-start | bytes 3932168 | tf_op jit(solution)/shard_map/ppermute | solution.py:448
  14.1 50.9 %collective-permute-start.14 = (s32[256]{0:T(256)S(1)}, s32[256]{0:T(256)S(1)}, u32[]{:S(2)}, u32[]{:S(2)}) collective-permute-start(s32[256]{0:T(256)S(1)} %iota_add_fusion), channel_id=1, source_target_pairs={{0,16},{1,17},{2,18},{3,19},{4,20},{5,21},{6,22},{7,23},{8,24},{9,... | collective-permute-start | bytes 3080 | tf_op jit(solution)/shard_map/ppermute | solution.py:448
  20.0 27.1 %copy-start.10 = (s32[256]{0:T(256)S(1)}, s32[256]{0:T(256)}, u32[]{:S(2)}) copy-start(s32[256]{0:T(256)} %slot_ref.1) | copy-start | bytes 3076
  21.8 6.9 %collective-permute-start.1 = (bf16[40,1280]{1,0:T(8,128)(2,1)S(1)}, bf16[40,1280]{1,0:T(8,128)(2,1)S(1)}, u32[]{:S(2)}, u32[]{:S(2)}) collective-permute-start(bf16[40,1280]{1,0:T(8,128)(2,1)S(1)} %slice.82.refs_0_), channel_id=1, source_target_pairs={{0,1},{1,2},{2,3},{3,0},{4,5},{5,6},{6,7},{7,4},{8,9},{9,10},{10,1... | collective-permute-start | bytes 307208 | tf_op jit(solution)/shard_map/ppermute | solution.py:444
  23.6 8.6 %collective-permute-start.2 = (bf16[40,1280]{1,0:T(8,128)(2,1)S(1)}, bf16[40,1280]{1,0:T(8,128)(2,1)S(1)}, u32[]{:S(2)}, u32[]{:S(2)}) collective-permute-start(bf16[40,1280]{1,0:T(8,128)(2,1)S(1)} %slice.82.refs_0_), channel_id=1, source_target_pairs={{0,2},{1,3},{2,0},{3,1},{4,6},{5,7},{6,4},{7,5},{8,10},{9,11},{10,... | collective-permute-start | bytes 307208 | tf_op jit(solution)/shard_map/ppermute | solution.py:444
  26.9 5.3 %collective-permute-start.3 = (bf16[40,1280]{1,0:T(8,128)(2,1)S(1)}, bf16[40,1280]{1,0:T(8,128)(2,1)S(1)}, u32[]{:S(2)}, u32[]{:S(2)}) collective-permute-start(bf16[40,1280]{1,0:T(8,128)(2,1)S(1)} %slice.82.refs_0_), channel_id=1, source_target_pairs={{0,3},{1,0},{2,1},{3,2},{4,7},{5,4},{6,5},{7,6},{8,11},{9,8},{10,9... | collective-permute-start | bytes 307208 | tf_op jit(solution)/shard_map/ppermute | solution.py:444
  32.4 21.4 %collective-permute-start.4 = (bf16[2,80,640]{2,1,0:T(8,128)(2,1)S(1)}, bf16[2,80,640]{2,1,0:T(8,128)(2,1)}, u32[]{:S(2)}, u32[]{:S(2)}) collective-permute-start(bf16[2,80,640]{2,1,0:T(8,128)(2,1)S(1)} %get-tuple-element.51), channel_id=1, source_target_pairs={{0,32},{1,33},{2,34},{3,35},{4,36},{5,37},{6,38},{7,39},{8,40},{9,... | collective-permute-start | bytes 614408 | tf_op jit(solution)/shard_map/ppermute | solution.py:444
  35.2 21.2 %collective-permute-start.8 = (bf16[2,80,640]{2,1,0:T(8,128)(2,1)S(1)}, bf16[2,80,640]{2,1,0:T(8,128)(2,1)}, u32[]{:S(2)}, u32[]{:S(2)}) collective-permute-start(bf16[2,80,640]{2,1,0:T(8,128)(2,1)S(1)} %get-tuple-element.50), channel_id=1, source_target_pairs={{0,4},{1,5},{2,6},{3,7},{4,8},{5,9},{6,10},{7,11},{8,12},{9,13},{1... | collective-permute-start | bytes 614408 | tf_op jit(solution)/shard_map/ppermute | solution.py:444
  38.3 8.9 %all-to-all-start = ((bf16[8,2,24,128]{3,2,1,0:T(8,128)(2,1)}), bf16[8,2,24,128]{3,2,1,0:T(8,128)(2,1)S(1)}, u32[]{:S(2)}, u32[]{:S(2)}) async-start(bf16[8,2,24,128]{3,2,1,0:T(8,128)(2,1)} %bitcast.16), calls=%async_computation | async-start | bytes 196608 | tf_op jit(solution)/shard_map/all_to_all | solution.py:429
  48.5 14.3 %all-to-all-start.1 = ((bf16[16,2,24,128]{3,2,1,0:T(8,128)(2,1)}), bf16[16,2,24,128]{3,2,1,0:T(8,128)(2,1)S(1)}, u32[]{:S(2)}, u32[]{:S(2)}) async-start(bf16[16,2,24,128]{3,2,1,0:T(8,128)(2,1)} %bitcast.18), calls=%async_computation.1 | async-start | bytes 393216 | tf_op jit(solution)/shard_map/all_to_all | solution.py:429
  53.7 14.6 %collective-permute-start.5 = (bf16[2,80,640]{2,1,0:T(8,128)(2,1)}, bf16[2,80,640]{2,1,0:T(8,128)(2,1)}, u32[]{:S(2)}, u32[]{:S(2)}) collective-permute-start(bf16[2,80,640]{2,1,0:T(8,128)(2,1)} %collective-permute-done.4), channel_id=1, source_target_pairs={{0,32},{1,33},{2,34},{3,35},{4,36},{5,37},{6,38},{7,39},{8,40},{9,... | collective-permute-start | bytes 614408 | tf_op jit(solution)/shard_map/ppermute | solution.py:444
  56.4 12.6 %collective-permute-start.9 = (bf16[2,80,640]{2,1,0:T(8,128)(2,1)}, bf16[2,80,640]{2,1,0:T(8,128)(2,1)S(1)}, u32[]{:S(2)}, u32[]{:S(2)}) collective-permute-start(bf16[2,80,640]{2,1,0:T(8,128)(2,1)} %collective-permute-done.8), channel_id=1, source_target_pairs={{0,4},{1,5},{2,6},{3,7},{4,8},{5,9},{6,10},{7,11},{8,12},{9,13},{1... | collective-permute-start | bytes 614408 | tf_op jit(solution)/shard_map/ppermute | solution.py:444
  63.8 2.0 %collective-permute-start.15 = (s32[16]{0:T(128)S(1)}, s32[16]{0:T(128)S(1)}, u32[]{:S(2)}, u32[]{:S(2)}) collective-permute-start(s32[16]{0:T(128)S(1)} %pad.20), channel_id=1, source_target_pairs={{0,16},{1,17},{2,18},{3,19},{4,20},{5,21},{6,22},{7,23},{8,24},{9,... | collective-permute-start | bytes 200 | tf_op jit(solution)/shard_map/ppermute | solution.py:448
  65.0 16.7 %collective-permute-start.12 = (bf16[16,2560]{1,0:T(8,128)(2,1)S(1)}, bf16[16,2560]{1,0:T(8,128)(2,1)S(1)}, u32[]{:S(2)}, u32[]{:S(2)}) collective-permute-start(bf16[16,2560]{1,0:T(8,128)(2,1)S(1)} %pad.19), channel_id=1, source_target_pairs={{0,16},{1,17},{2,18},{3,19},{4,20},{5,21},{6,22},{7,23},{8,24},{9,... | collective-permute-start | bytes 245768 | tf_op jit(solution)/shard_map/ppermute | solution.py:448
  67.2 14.6 %copy-start.12 = (bf16[1,256,2560]{2,1,0:T(8,128)(2,1)S(1)}, bf16[1,256,2560]{2,1,0:T(8,128)(2,1)}, u32[]{:S(2)}) copy-start(bf16[1,256,2560]{2,1,0:T(8,128)(2,1)} %param.14) | copy-start | bytes 3932164
  68.3 9.4 %collective-permute-start.6 = (bf16[2,80,640]{2,1,0:T(8,128)(2,1)}, bf16[2,80,640]{2,1,0:T(8,128)(2,1)S(1)}, u32[]{:S(2)}, u32[]{:S(2)}) collective-permute-start(bf16[2,80,640]{2,1,0:T(8,128)(2,1)} %collective-permute-done.5), channel_id=1, source_target_pairs={{0,32},{1,33},{2,34},{3,35},{4,36},{5,37},{6,38},{7,39},{8,40},{9,... | collective-permute-start | bytes 614408 | tf_op jit(solution)/shard_map/ppermute | solution.py:444
  69.0 9.4 %collective-permute-start.10 = (bf16[2,80,640]{2,1,0:T(8,128)(2,1)S(1)}, bf16[2,80,640]{2,1,0:T(8,128)(2,1)S(1)}, u32[]{:S(2)}, u32[]{:S(2)}) collective-permute-start(bf16[2,80,640]{2,1,0:T(8,128)(2,1)S(1)} %collective-permute-done.9), channel_id=1, source_target_pairs={{0,4},{1,5},{2,6},{3,7},{4,8},{5,9},{6,10},{7,11},{8,12},{9,13},{1... | collective-permute-start | bytes 614408 | tf_op jit(solution)/shard_map/ppermute | solution.py:444
  78.4 24.7 %collective-permute-start.7 = (bf16[4,2,80,640]{3,2,1,0:T(8,128)(2,1)}, bf16[4,2,80,640]{3,2,1,0:T(8,128)(2,1)}, u32[]{:S(2)}, u32[]{:S(2)}) collective-permute-start(bf16[4,2,80,640]{3,2,1,0:T(8,128)(2,1)} %bitcast_dynamic-update-slice_fusion.4.refs_0_), channel_id=1, source_target_pairs={{0,4},{1,5},{2,6},{3,7},{4,8},{5,9},{6,10},{7,11},{8,12},{9,13},{1... | collective-permute-start | bytes 2457608 | tf_op jit(solution)/shard_map/ppermute | solution.py:444
  79.1 24.1 %collective-permute-start.11 = (bf16[2,4,80,640]{3,2,1,0:T(8,128)(2,1)}, bf16[2,4,80,640]{3,2,1,0:T(8,128)(2,1)}, u32[]{:S(2)}, u32[]{:S(2)}) collective-permute-start(bf16[2,4,80,640]{3,2,1,0:T(8,128)(2,1)} %bitcast_dynamic-update-slice_fusion.3.refs_4_), channel_id=1, source_target_pairs={{0,32},{1,33},{2,34},{3,35},{4,36},{5,37},{6,38},{7,39},{8,40},{9,... | collective-permute-start | bytes 2457608 | tf_op jit(solution)/shard_map/ppermute | solution.py:444
  81.7 1.2 copy-start
  103.2 14.4 %collective-permute-start.18 = (bf16[4,2,80,640]{3,2,1,0:T(8,128)(2,1)}, bf16[4,2,80,640]{3,2,1,0:T(8,128)(2,1)}, u32[]{:S(2)}, u32[]{:S(2)}) collective-permute-start(bf16[4,2,80,640]{3,2,1,0:T(8,128)(2,1)} %collective-permute-done.7.refs_1_), channel_id=1, source_target_pairs={{0,4},{1,5},{2,6},{3,7},{4,8},{5,9},{6,10},{7,11},{8,12},{9,13},{1... | collective-permute-start | bytes 2457608 | tf_op jit(solution)/shard_map/ppermute | solution.py:444
  104.4 14.3 %collective-permute-start.19 = (bf16[2,4,80,640]{3,2,1,0:T(8,128)(2,1)}, bf16[2,4,80,640]{3,2,1,0:T(8,128)(2,1)}, u32[]{:S(2)}, u32[]{:S(2)}) collective-permute-start(bf16[2,4,80,640]{3,2,1,0:T(8,128)(2,1)} %collective-permute-done.11.refs_5_), channel_id=1, source_target_pairs={{0,32},{1,33},{2,34},{3,35},{4,36},{5,37},{6,38},{7,39},{8,40},{9,... | collective-permute-start | bytes 2457608 | tf_op jit(solution)/shard_map/ppermute | solution.py:444
  106.7 1.1 copy-start.1
  113.3 9.6 %copy-start.6 = (bf16[4,272,256]{2,1,0:T(8,128)(2,1)}, bf16[4,272,256]{2,1,0:T(8,128)(2,1)S(1)}, u32[]{:S(2)}) copy-start(bf16[4,272,256]{2,1,0:T(8,128)(2,1)S(1)} %get-tuple-element.32.ab1_ref.oab_ref) | copy-start | bytes 1671172
  113.3 8.3 %collective-permute-start.16 = (bf16[4,272,256]{2,1,0:T(8,128)(2,1)S(1)}, bf16[4,272,256]{2,1,0:T(8,128)(2,1)S(1)}, u32[]{:S(2)}, u32[]{:S(2)}) collective-permute-start(bf16[4,272,256]{2,1,0:T(8,128)(2,1)S(1)} %get-tuple-element.34), channel_id=1, source_target_pairs={{0,16},{1,17},{2,18},{3,19},{4,20},{5,21},{6,22},{7,23},{8,24},{9,... | collective-permute-start | bytes 1671176 | tf_op jit(solution)/shard_map/ppermute | solution.py:448
  113.4 9.5 %copy-start.2 = (bf16[2,2048,512]{2,1,0:T(8,128)(2,1)S(1)}, bf16[2,2048,512]{2,1,0:T(8,128)(2,1)}, u32[]{:S(2)}) copy-start(bf16[2,2048,512]{2,1,0:T(8,128)(2,1)} %cache_ref.3) | copy-start | bytes 12582916
  116.9 10.1 %copy-start.4 = (bf16[2,272,256]{2,1,0:T(8,128)(2,1)}, bf16[2,272,256]{2,1,0:T(8,128)(2,1)S(1)}, u32[]{:S(2)}) copy-start(bf16[2,272,256]{2,1,0:T(8,128)(2,1)S(1)} %get-tuple-element.33.c1_ref.oc_ref) | copy-start | bytes 835588
  116.9 3.3 %collective-permute-start.17 = (bf16[2,272,256]{2,1,0:T(8,128)(2,1)S(1)}, bf16[2,272,256]{2,1,0:T(8,128)(2,1)S(1)}, u32[]{:S(2)}, u32[]{:S(2)}) collective-permute-start(bf16[2,272,256]{2,1,0:T(8,128)(2,1)S(1)} %get-tuple-element.35), channel_id=1, source_target_pairs={{0,16},{1,17},{2,18},{3,19},{4,20},{5,21},{6,22},{7,23},{8,24},{9,... | collective-permute-start | bytes 835592 | tf_op jit(solution)/shard_map/ppermute | solution.py:448
  117.4 17.2 %collective-permute-start.22 = (bf16[4,2,80,640]{3,2,1,0:T(8,128)(2,1)}, bf16[4,2,80,640]{3,2,1,0:T(8,128)(2,1)}, u32[]{:S(2)}, u32[]{:S(2)}) collective-permute-start(bf16[4,2,80,640]{3,2,1,0:T(8,128)(2,1)} %bitcast_dynamic-update-slice_fusion.4.refs_0_), channel_id=1, source_target_pairs={{0,16},{1,17},{2,18},{3,19},{4,20},{5,21},{6,22},{7,23},{8,24},{9,... | collective-permute-start | bytes 2457608 | tf_op jit(solution)/shard_map/ppermute | solution.py:448
  117.5 17.5 %collective-permute-start.26 = (bf16[2,4,80,640]{3,2,1,0:T(8,128)(2,1)}, bf16[2,4,80,640]{3,2,1,0:T(8,128)(2,1)}, u32[]{:S(2)}, u32[]{:S(2)}) collective-permute-start(bf16[2,4,80,640]{3,2,1,0:T(8,128)(2,1)} %bitcast_dynamic-update-slice_fusion.3.refs_4_), channel_id=1, source_target_pairs={{0,16},{1,17},{2,18},{3,19},{4,20},{5,21},{6,22},{7,23},{8,24},{9,... | collective-permute-start | bytes 2457608 | tf_op jit(solution)/shard_map/ppermute | solution.py:448
  118.7 16.5 %collective-permute-start.23 = (bf16[4,2,80,640]{3,2,1,0:T(8,128)(2,1)}, bf16[4,2,80,640]{3,2,1,0:T(8,128)(2,1)}, u32[]{:S(2)}, u32[]{:S(2)}) collective-permute-start(bf16[4,2,80,640]{3,2,1,0:T(8,128)(2,1)} %collective-permute-done.7.refs_1_), channel_id=1, source_target_pairs={{0,16},{1,17},{2,18},{3,19},{4,20},{5,21},{6,22},{7,23},{8,24},{9,... | collective-permute-start | bytes 2457608 | tf_op jit(solution)/shard_map/ppermute | solution.py:448
  120.1 13.2 %collective-permute-start.20 = (bf16[4,2,80,640]{3,2,1,0:T(8,128)(2,1)}, bf16[4,2,80,640]{3,2,1,0:T(8,128)(2,1)}, u32[]{:S(2)}, u32[]{:S(2)}) collective-permute-start(bf16[4,2,80,640]{3,2,1,0:T(8,128)(2,1)} %collective-permute-done.18.refs_2_), channel_id=1, source_target_pairs={{0,4},{1,5},{2,6},{3,7},{4,8},{5,9},{6,10},{7,11},{8,12},{9,13},{1... | collective-permute-start | bytes 2457608 | tf_op jit(solution)/shard_map/ppermute | solution.py:444
  121.7 5.3 %copy-start.8 = (bf16[4,272,256]{2,1,0:T(8,128)(2,1)}, bf16[4,272,256]{2,1,0:T(8,128)(2,1)S(1)}, u32[]{:S(2)}) copy-start(bf16[4,272,256]{2,1,0:T(8,128)(2,1)S(1)} %collective-permute-done.16.ab2_ref.tab_ref) | copy-start | bytes 1671172
  121.7 12.8 %collective-permute-start.21 = (bf16[2,4,80,640]{3,2,1,0:T(8,128)(2,1)}, bf16[2,4,80,640]{3,2,1,0:T(8,128)(2,1)}, u32[]{:S(2)}, u32[]{:S(2)}) collective-permute-start(bf16[2,4,80,640]{3,2,1,0:T(8,128)(2,1)} %collective-permute-done.19.refs_6_), channel_id=1, source_target_pairs={{0,32},{1,33},{2,34},{3,35},{4,36},{5,37},{6,38},{7,39},{8,40},{9,... | collective-permute-start | bytes 2457608 | tf_op jit(solution)/shard_map/ppermute | solution.py:444
  126.9 10.0 %copy-start.7 = (bf16[4,272,256]{2,1,0:T(8,128)(2,1)S(1)}, bf16[4,272,256]{2,1,0:T(8,128)(2,1)}, u32[]{:S(2)}) copy-start(bf16[4,272,256]{2,1,0:T(8,128)(2,1)} %copy-done.6) | copy-start | bytes 1671172
  126.9 10.0 %copy-start.5 = (bf16[2,272,256]{2,1,0:T(8,128)(2,1)S(1)}, bf16[2,272,256]{2,1,0:T(8,128)(2,1)}, u32[]{:S(2)}) copy-start(bf16[2,272,256]{2,1,0:T(8,128)(2,1)} %copy-done.4) | copy-start | bytes 835588
  126.9 10.0 %copy-start.9 = (bf16[4,272,256]{2,1,0:T(8,128)(2,1)S(1)}, bf16[4,272,256]{2,1,0:T(8,128)(2,1)}, u32[]{:S(2)}) copy-start(bf16[4,272,256]{2,1,0:T(8,128)(2,1)} %copy-done.8) | copy-start | bytes 1671172
  126.9 30.5 %all-to-all-start.2 = ((bf16[128,2,24,128]{3,2,1,0:T(8,128)(2,1)}), bf16[128,2,24,128]{3,2,1,0:T(8,128)(2,1)S(1)}, u32[]{:S(2)}, u32[]{:S(2)}) async-start(bf16[128,2,24,128]{3,2,1,0:T(8,128)(2,1)} %bitcast.30), calls=%async_computation.2 | async-start | bytes 3145728 | tf_op jit(solution)/shard_map/all_to_all | solution.py:429
  133.4 25.3 %collective-permute-start.27 = (bf16[2,4,80,640]{3,2,1,0:T(8,128)(2,1)}, bf16[2,4,80,640]{3,2,1,0:T(8,128)(2,1)}, u32[]{:S(2)}, u32[]{:S(2)}) collective-permute-start(bf16[2,4,80,640]{3,2,1,0:T(8,128)(2,1)} %collective-permute-done.11.refs_5_), channel_id=1, source_target_pairs={{0,16},{1,17},{2,18},{3,19},{4,20},{5,21},{6,22},{7,23},{8,24},{9,... | collective-permute-start | bytes 2457608 | tf_op jit(solution)/shard_map/ppermute | solution.py:448
  134.5 24.2 %collective-permute-start.24 = (bf16[4,2,80,640]{3,2,1,0:T(8,128)(2,1)}, bf16[4,2,80,640]{3,2,1,0:T(8,128)(2,1)}, u32[]{:S(2)}, u32[]{:S(2)}) collective-permute-start(bf16[4,2,80,640]{3,2,1,0:T(8,128)(2,1)} %collective-permute-done.18.refs_2_), channel_id=1, source_target_pairs={{0,16},{1,17},{2,18},{3,19},{4,20},{5,21},{6,22},{7,23},{8,24},{9,... | collective-permute-start | bytes 2457608 | tf_op jit(solution)/shard_map/ppermute | solution.py:448
  134.6 24.1 %collective-permute-start.28 = (bf16[2,4,80,640]{3,2,1,0:T(8,128)(2,1)}, bf16[2,4,80,640]{3,2,1,0:T(8,128)(2,1)}, u32[]{:S(2)}, u32[]{:S(2)}) collective-permute-start(bf16[2,4,80,640]{3,2,1,0:T(8,128)(2,1)} %collective-permute-done.19.refs_6_), channel_id=1, source_target_pairs={{0,16},{1,17},{2,18},{3,19},{4,20},{5,21},{6,22},{7,23},{8,24},{9,... | collective-permute-start | bytes 2457608 | tf_op jit(solution)/shard_map/ppermute | solution.py:448
  135.0 23.7 %collective-permute-start.25 = (bf16[4,2,80,640]{3,2,1,0:T(8,128)(2,1)}, bf16[4,2,80,640]{3,2,1,0:T(8,128)(2,1)}, u32[]{:S(2)}, u32[]{:S(2)}) collective-permute-start(bf16[4,2,80,640]{3,2,1,0:T(8,128)(2,1)} %collective-permute-done.20.refs_3_), channel_id=1, source_target_pairs={{0,16},{1,17},{2,18},{3,19},{4,20},{5,21},{6,22},{7,23},{8,24},{9,... | collective-permute-start | bytes 2457608 | tf_op jit(solution)/shard_map/ppermute | solution.py:448
  135.1 23.6 %collective-permute-start.29 = (bf16[2,4,80,640]{3,2,1,0:T(8,128)(2,1)}, bf16[2,4,80,640]{3,2,1,0:T(8,128)(2,1)}, u32[]{:S(2)}, u32[]{:S(2)}) collective-permute-start(bf16[2,4,80,640]{3,2,1,0:T(8,128)(2,1)} %collective-permute-done.21.refs_7_), channel_id=1, source_target_pairs={{0,16},{1,17},{2,18},{3,19},{4,20},{5,21},{6,22},{7,23},{8,24},{9,... | collective-permute-start | bytes 2457608 | tf_op jit(solution)/shard_map/ppermute | solution.py:448
  136.9 1.6 copy-start.11
  153.0 1.1 copy-start.3
Sparse Core Ops, SparseCore 0:
  13.2 87.7 all-gather.1

commit v4 on v3

--- a/solution.py
+++ b/solution.py
@@ -382,7 +382,8 @@
         term = dot(lhs[half], right)
         total = term if total is None else total + term
     out_ref[...] = (x_ref[...].astype(F32) + total[:rows]).astype(BF16)
-    dout_ref[...] = (dx_ref[...].astype(F32) + total[rows:]).astype(BF16)
+    drows = dx_ref.shape[0]
+    dout_ref[...] = (dx_ref[...].astype(F32) + total[rows : rows + drows]).astype(BF16)
 
 
 def finish(info, att, datt, x, dx, chunks):
@@ -407,7 +408,7 @@
             + [pl.BlockSpec(memory_space=pl.ANY)] * 16,
             out_specs=[pl.BlockSpec((rows, bn), column), pl.BlockSpec((drows, bn), column)],
             scratch_shapes=[
-                pltpu.VMEM((2, rows + drows, n // 2), BF16),
+                pltpu.VMEM((2, rows + EXTRA, n // 2), BF16),
                 pltpu.VMEM((4, 4, 2, 4, run, bn), BF16),
                 pltpu.SemaphoreType.DMA((4, 4)),
             ],
@@ -416,7 +417,7 @@
             jax.ShapeDtypeStruct((rows, n), BF16),
             jax.ShapeDtypeStruct((drows, n), BF16),
         ],
-        compiler_params=params(60, "arbitrary"),
+        compiler_params=params(24, "arbitrary"),
         cost_estimate=pl.CostEstimate(
             flops=2 * rows * n * n, bytes_accessed=2 * n * n, transcendentals=0
         ),
@@ -572,13 +573,14 @@
     steps = jnp.asarray([0, 1, 2, 3] * 2 + [0, -1, -2, -3] * 2, jnp.int32)
     came_from = (((device.astype(jnp.int32) >> shifts) & 3) - (1 - 2 * core) * steps) & 3
     finish_info = jnp.concatenate([core[None], came_from])
-    decode_rows = jnp.pad(decode_tokens, ((0, EXTRA - own), (0, 0)))
     info = jnp.concatenate([own_length, request_of_mine, core[None]])
-    parts, lhs, cos, sin, finish_info, decode_rows, info = lax.optimization_barrier(
-        (parts, lhs, cos, sin, finish_info, decode_rows, info)
+    parts, lhs, cos, sin, finish_info, info = lax.optimization_barrier(
+        (parts, lhs, cos, sin, finish_info, info)
     )
     ring_step(parts)
-    first_weight = pltpu.with_memory_space_constraint(first_weight, pltpu.HBM)
+    first_weight, cos, sin = (
+        pltpu.with_memory_space_constraint(v, pltpu.HBM) for v in (first_weight, cos, sin)
+    )
     ours_c, other_c = project(4, 2, rows, lhs, first_weight, cos, sin, hd)
     theirs_c = swap(other_c)
     ours_ab, other_ab = project(0, 4, rows, lhs, first_weight, cos, sin, hd)
@@ -604,10 +606,10 @@
         att,
         jnp.pad(home, ((0, EXTRA - own), (0, 0))),
         span_tokens[0],
-        decode_rows,
+        decode_tokens,
         [c for half in (mine, theirs) for part in half for c in part],
     )
-    return span_output[None], keyval[:rows][None], decode_output[:own], decode_keyval
+    return span_output[None], keyval[:rows][None], decode_output, decode_keyval
 
 
 def solution(mesh):

time: 179 us -> 180 us (level)
  local copies, waits for them, and re-layouts: 23.2 us -> 28 us
    unnamed x30 -> x46, local copies, waits for them, and re-layouts: 4.88 us -> 12.9 us
    ppermute x15, starting transfers between devices: 8.96 us -> 11.9 us  [swap(): lax.ppermute(v, AXES, list(zip(DEVICES.tolist(), (DEVICES ^ 16).tolist())))]
    all_to_all x3, waiting for transfers between devices: 5.86 us -> 3.07 us  [exchange(): lax.all_to_all(sent.reshape((members, -1) + sent.shape[1:]), axes, 0, 0)]
    pallas_call x1, Pallas kernels: 10.7 us -> 8.72 us  [finish(): pl.pallas_call(finish_body, grid_spec=pltpu.PrefetchScalarGridSpec(num_sc...]
    ppermute x15, starting transfers between devices: 27 us -> 25.1 us  [send(): return lax.ppermute(v, AXES, list(zip(DEVICES.tolist(), to.tolist())))]
  transfers between devices with their start and end apart: 34 -> 34, of which waited for: 9 -> 9; matrix products, arithmetic and copies ran while one was open for 14% -> 13% of each run, Pallas kernels for 19% -> 19%
where the time goes in v4:
time: 180 us; the launch traced here: 179 us
  starting transfers between devices  50.8 us (28%)
  Pallas kernels  43.6 us (24%)
  waiting for transfers between devices  31.1 us (17%)
  local copies, waits for them, and re-layouts  28 us (16%)
  between operations  15.2 us (8%)
  other arithmetic  10.5 us (6%)
    ppermute x15, waiting for transfers between devices, send(): return lax.ppermute(v, AXES, list(zip(DEVICES.tolist(), to.tolist())))  26.3 us
    ppermute x15, starting transfers between devices, send(): return lax.ppermute(v, AXES, list(zip(DEVICES.tolist(), to.tolist())))  25.1 us
    pallas_call x1, Pallas kernels, span_attend(): pl.pallas_call(span_body, grid_spec=pltpu.PrefetchScalarGridSpec(num_scal...  14.4 us
    all_to_all x3, starting transfers between devices, exchange(): lax.all_to_all(sent.reshape((members, -1) + sent.shape[1:]), axes, 0, 0)  13.8 us
    unnamed x46, local copies, waits for them, and re-layouts  12.9 us
    ppermute x15, starting transfers between devices, swap(): lax.ppermute(v, AXES, list(zip(DEVICES.tolist(), (DEVICES ^ 16).tolist())))  11.9 us
    pallas_call x2, Pallas kernels, project(): pl.pallas_call(functools.partial(project_body, rows), grid=(count,), in_s...  9.4 us
    pallas_call x1, Pallas kernels, finish(): pl.pallas_call(finish_body, grid_spec=pltpu.PrefetchScalarGridSpec(num_sc...  8.72 us
  transfers between devices with their start and end apart: 34, of which 9 were waited for; matrix products, arithmetic and copies ran while one was open for 13% of the time, Pallas kernels for 19%

profile of v4, /device:TPU:1, one launch (start us, length us, event | category | flops | bytes accessed | tf_op | source)
XLA Modules:
  0.0 179.3 jit_solution(1369428721370842697)
XLA Ops:
  7.2 0.9 fusion.14
  8.1 0.7 fusion.15
  8.8 0.9 fusion.13
  9.8 1.5 collective-permute-start
  11.3 1.0 collective-permute-done
  15.2 0.7 fusion.8
  15.9 0.7 broadcast_in_dim.79.gain_ref
  17.3 1.4 compare_reduce_fusion
  18.7 1.8 %fusion.order_ref = bf16[640,640]{1,0:T(8,128)(2,1)} fusion(s32[640]{0:T(1024)} %constant.88.clone), kind=kLoop, calls=%fused_computation.2 | loop fusion | flops 819200 | bytes 821760 | tf_op jit(solution)/shard_map/convert_element_type | solution.py:34
  20.5 1.8 collective-permute-start.1
  22.3 3.3 %collective-permute-start.2 = (bf16[40,1280]{1,0:T(8,128)(2,1)S(1)}, bf16[40,1280]{1,0:T(8,128)(2,1)S(1)}, u32[]{:S(2)}, u32[]{:S(2)}) collective-permute-start(bf16[40,1280]{1,0:T(8,128)(2,1)S(1)} %slice.78.refs_0_), channel_id=1, source_target_pairs={{0,2},{1,3},{2,0},{3,1},{4,6},{5,7},{6,4},{7,5},{8,10},{9,11},{10,... | collective-permute-start | bytes 307208 | tf_op jit(solution)/shard_map/ppermute | solution.py:445
  25.6 0.7 collective-permute-start.3
  26.4 1.0 collective-permute-done.1.refs_1_
  27.4 3.1 %collective-permute-done.2.refs_2_ = bf16[40,1280]{1,0:T(8,128)(2,1)S(1)} collective-permute-done((bf16[40,1280]{1,0:T(8,128)(2,1)S(1)}, bf16[40,1280]{1,0:T(8,128)(2,1)S(1)}, u32[]{:S(2)}, u32[]{:S(2)}) %collective-permute-start.2) | collective-permute-done | bytes 102432 | tf_op jit(solution)/shard_map/ppermute | solution.py:445
  30.6 2.8 %collective-permute-start.4 = (bf16[2,80,640]{2,1,0:T(8,128)(2,1)S(1)}, bf16[2,80,640]{2,1,0:T(8,128)(2,1)}, u32[]{:S(2)}, u32[]{:S(2)}) collective-permute-start(bf16[2,80,640]{2,1,0:T(8,128)(2,1)S(1)} %get-tuple-element.49), channel_id=1, source_target_pairs={{0,32},{1,33},{2,34},{3,35},{4,36},{5,37},{6,38},{7,39},{8,40},{9,... | collective-permute-start | bytes 614408 | tf_op jit(solution)/shard_map/ppermute | solution.py:445
  33.4 2.5 %collective-permute-start.8 = (bf16[2,80,640]{2,1,0:T(8,128)(2,1)S(1)}, bf16[2,80,640]{2,1,0:T(8,128)(2,1)}, u32[]{:S(2)}, u32[]{:S(2)}) collective-permute-start(bf16[2,80,640]{2,1,0:T(8,128)(2,1)S(1)} %get-tuple-element.48), channel_id=1, source_target_pairs={{0,4},{1,5},{2,6},{3,7},{4,8},{5,9},{6,10},{7,11},{8,12},{9,13},{1... | collective-permute-start | bytes 614408 | tf_op jit(solution)/shard_map/ppermute | solution.py:445
  36.6 4.4 %all-to-all-start = ((bf16[8,2,24,128]{3,2,1,0:T(8,128)(2,1)}), bf16[8,2,24,128]{3,2,1,0:T(8,128)(2,1)S(1)}, u32[]{:S(2)}, u32[]{:S(2)}) async-start(bf16[8,2,24,128]{3,2,1,0:T(8,128)(2,1)} %bitcast.16), calls=%async_computation | async-start | bytes 196608 | tf_op jit(solution)/shard_map/all_to_all | solution.py:430
  41.0 1.0 broadcast_in_dim.66
  42.6 1.0 broadcast_in_dim.72
  44.3 1.7 all-to-all-done
  46.0 1.4 place.1
  47.4 4.7 %all-to-all-start.1 = ((bf16[16,2,24,128]{3,2,1,0:T(8,128)(2,1)}), bf16[16,2,24,128]{3,2,1,0:T(8,128)(2,1)S(1)}, u32[]{:S(2)}, u32[]{:S(2)}) async-start(bf16[16,2,24,128]{3,2,1,0:T(8,128)(2,1)} %bitcast.18), calls=%async_computation.1 | async-start | bytes 393216 | tf_op jit(solution)/shard_map/all_to_all | solution.py:430
  52.1 2.6 %collective-permute-start.5 = (bf16[2,80,640]{2,1,0:T(8,128)(2,1)}, bf16[2,80,640]{2,1,0:T(8,128)(2,1)}, u32[]{:S(2)}, u32[]{:S(2)}) collective-permute-start(bf16[2,80,640]{2,1,0:T(8,128)(2,1)} %collective-permute-done.4), channel_id=1, source_target_pairs={{0,32},{1,33},{2,34},{3,35},{4,36},{5,37},{6,38},{7,39},{8,40},{9,... | collective-permute-start | bytes 614408 | tf_op jit(solution)/shard_map/ppermute | solution.py:445
  54.7 2.4 %collective-permute-start.9 = (bf16[2,80,640]{2,1,0:T(8,128)(2,1)}, bf16[2,80,640]{2,1,0:T(8,128)(2,1)S(1)}, u32[]{:S(2)}, u32[]{:S(2)}) collective-permute-start(bf16[2,80,640]{2,1,0:T(8,128)(2,1)} %collective-permute-done.8), channel_id=1, source_target_pairs={{0,4},{1,5},{2,6},{3,7},{4,8},{5,9},{6,10},{7,11},{8,12},{9,13},{1... | collective-permute-start | bytes 614408 | tf_op jit(solution)/shard_map/ppermute | solution.py:445
  57.1 1.6 bitcast_dynamic-update-slice_fusion.6
  58.8 1.6 bitcast_dynamic-update-slice_fusion.1
  60.4 1.4 all-to-all-done.1
  62.7 1.4 collective-permute-start.15
  64.2 0.7 collective-permute-done.15
  65.0 1.0 fusion.4
  66.5 0.8 pad_maximum_fusion.1.cos_ref
  67.3 0.9 pad_maximum_fusion.2.sin_ref
  68.8 0.9 collective-permute-start.10
  69.7 1.7 bitcast_dynamic-update-slice_fusion.5
  72.1 4.8 %collective-permute-done.6 = bf16[2,80,640]{2,1,0:T(8,128)(2,1)S(1)} collective-permute-done((bf16[2,80,640]{2,1,0:T(8,128)(2,1)}, bf16[2,80,640]{2,1,0:T(8,128)(2,1)S(1)}, u32[]{:S(2)}, u32[]{:S(2)}) %collective-permute-start.6) | collective-permute-done | bytes 204832 | tf_op jit(solution)/shard_map/ppermute | solution.py:445
  78.7 2.1 %collective-permute-start.11 = (bf16[2,4,80,640]{3,2,1,0:T(8,128)(2,1)}, bf16[2,4,80,640]{3,2,1,0:T(8,128)(2,1)}, u32[]{:S(2)}, u32[]{:S(2)}) collective-permute-start(bf16[2,4,80,640]{3,2,1,0:T(8,128)(2,1)} %bitcast_dynamic-update-slice_fusion.3.refs_4_), channel_id=1, source_target_pairs={{0,32},{1,33},{2,34},{3,35},{4,36},{5,37},{6,38},{7,39},{8,40},{9,... | collective-permute-start | bytes 2457608 | tf_op jit(solution)/shard_map/ppermute | solution.py:445
  81.1 1.0 copy-done
  82.1 4.1 %norm_ordered.2.refs_0_ = bf16[544,2560]{1,0:T(8,128)(2,1)S(1)} custom-call(bf16[512,2560]{1,0:T(8,128)(2,1)S(1)} %pad_maximum_fusion.x_ref, f32[1,2560]{1,0:T(1,128)S(1)} %broadcast_in_dim.79.gain_ref, bf16[640,640]{1,0:T(8,128)(2,1)S(1)} %copy-done), custom_call_target="tpu_custom_call" | custom-call | flops 1677721600 | bytes 5242880 | tf_op jit(solution)/shard_map/norm_ordered/pallas_call | solution.py:57
  86.5 17.1 %collective-permute-done.7.refs_1_ = bf16[4,2,80,640]{3,2,1,0:T(8,128)(2,1)} collective-permute-done((bf16[4,2,80,640]{3,2,1,0:T(8,128)(2,1)}, bf16[4,2,80,640]{3,2,1,0:T(8,128)(2,1)}, u32[]{:S(2)}, u32[]{:S(2)}) %collective-permute-start.7) | collective-permute-done | bytes 819232 | tf_op jit(solution)/shard_map/ppermute | solution.py:445
  103.6 1.3 collective-permute-start.18
  105.0 0.9 collective-permute-start.19
  105.8 5.8 %project.2 = (bf16[4,272,256]{2,1,0:T(8,128)(2,1)S(1)}, bf16[4,272,256]{2,1,0:T(8,128)(2,1)S(1)}) custom-call(bf16[544,2560]{1,0:T(8,128)(2,1)S(1)} %norm_ordered.3.x_ref, bf16[2560,1536]{1,0:T(8,128)(2,1)} %all-gather.2.cloned.1.call-done.w_ref, f32[2,544,128]{2,1,0:T(8,128)} %pad_maximum_fusion.1.cos_ref, f32[2,544,128]{2,1,0:T(8,128)} %pad_maximum_fusion.2.sin_ref), custom_call_target="tpu_custom_call" | custom-call | flops 2852126720 | bytes 5242880 | tf_op jit(solution)/shard_map/project/pallas_call | solution.py:97
  111.7 0.8 collective-permute-start.16
  112.4 3.6 %project.3 = (bf16[2,272,256]{2,1,0:T(8,128)(2,1)S(1)}, bf16[2,272,256]{2,1,0:T(8,128)(2,1)S(1)}) custom-call(bf16[544,2560]{1,0:T(8,128)(2,1)S(1)} %norm_ordered.3.x_ref, bf16[2560,1536]{1,0:T(8,128)(2,1)} %all-gather.2.cloned.1.call-done.w_ref, f32[2,544,128]{2,1,0:T(8,128)} %pad_maximum_fusion.1.cos_ref, f32[2,544,128]{2,1,0:T(8,128)} %pad_maximum_fusion.2.sin_ref), custom_call_target="tpu_custom_call" | custom-call | flops 1426063360 | bytes 2621440 | tf_op jit(solution)/shard_map/project/pallas_call | solution.py:97
  116.6 2.6 %collective-permute-start.26 = (bf16[2,4,80,640]{3,2,1,0:T(8,128)(2,1)}, bf16[2,4,80,640]{3,2,1,0:T(8,128)(2,1)S(1)}, u32[]{:S(2)}, u32[]{:S(2)}) collective-permute-start(bf16[2,4,80,640]{3,2,1,0:T(8,128)(2,1)} %bitcast_dynamic-update-slice_fusion.3.refs_4_), channel_id=1, source_target_pairs={{0,16},{1,17},{2,18},{3,19},{4,20},{5,21},{6,22},{7,23},{8,24},{9,... | collective-permute-start | bytes 2457608 | tf_op jit(solution)/shard_map/ppermute | solution.py:449
  119.3 1.1 collective-permute-start.23
  120.4 1.8 %collective-permute-start.20 = (bf16[4,2,80,640]{3,2,1,0:T(8,128)(2,1)}, bf16[4,2,80,640]{3,2,1,0:T(8,128)(2,1)}, u32[]{:S(2)}, u32[]{:S(2)}) collective-permute-start(bf16[4,2,80,640]{3,2,1,0:T(8,128)(2,1)} %collective-permute-done.18.refs_2_), channel_id=1, source_target_pairs={{0,4},{1,5},{2,6},{3,7},{4,8},{5,9},{6,10},{7,11},{8,12},{9,13},{1... | collective-permute-start | bytes 2457608 | tf_op jit(solution)/shard_map/ppermute | solution.py:445
  122.3 1.3 collective-permute-start.21
  123.6 3.9 %decode_attend.1 = bf16[256,24,128]{2,1,0:T(8,128)(2,1)} custom-call(s32[5]{0:T(128)S(1)} %pad_add_fusion.1.info_ref, bf16[4,272,256]{2,1,0:T(8,128)(2,1)S(1)} %get-tuple-element.31.ab1_ref.oab_ref, bf16[2,272,256]{2,1,0:T(8,128)(2,1)S(1)} %get-tuple-element.32.c1_ref.oc_ref, bf16[4,272,256]{2,1,0:T(8,128)(2,1)S(1)} %collective-permute-done.16.ab2_ref.tab_ref, ...), custom_call_target="tpu_custom_call" | custom-call | flops 67108864 | bytes 4194304 | tf_op jit(solution)/shard_map/decode_attend/pallas_call | solution.py:163
  127.5 4.7 %all-to-all-start.2 = ((bf16[128,2,24,128]{3,2,1,0:T(8,128)(2,1)}), bf16[128,2,24,128]{3,2,1,0:T(8,128)(2,1)S(1)}, u32[]{:S(2)}, u32[]{:S(2)}) async-start(bf16[128,2,24,128]{3,2,1,0:T(8,128)(2,1)} %bitcast.30), calls=%async_computation.2 | async-start | bytes 3145728 | tf_op jit(solution)/shard_map/all_to_all | solution.py:430
  132.2 2.1 %collective-permute-start.27 = (bf16[2,4,80,640]{3,2,1,0:T(8,128)(2,1)}, bf16[2,4,80,640]{3,2,1,0:T(8,128)(2,1)}, u32[]{:S(2)}, u32[]{:S(2)}) collective-permute-start(bf16[2,4,80,640]{3,2,1,0:T(8,128)(2,1)} %collective-permute-done.11.refs_5_), channel_id=1, source_target_pairs={{0,16},{1,17},{2,18},{3,19},{4,20},{5,21},{6,22},{7,23},{8,24},{9,... | collective-permute-start | bytes 2457608 | tf_op jit(solution)/shard_map/ppermute | solution.py:449
  134.8 0.9 copy-done.8
  136.9 0.7 fusion.2
  137.6 1.0 copy-done.11
  138.6 1.0 copy-done.13
  139.6 1.1 copy-done.15
  140.6 1.1 copy-done.17
  141.7 1.6 copy-done.20
  143.3 14.4 %span_attend.1.att_ref = bf16[2,256,1280]{2,1,0:T(8,128)(2,1)S(1)} custom-call(s32[1]{0:T(128)S(6)} %copy.50.index_ref, bf16[4,272,256]{2,1,0:T(8,128)(2,1)S(1)} %copy-done.15, bf16[2,272,256]{2,1,0:T(8,128)(2,1)S(1)} %copy-done.11, bf16[4,272,256]{2,1,0:T(8,128)(2,1)S(1)} %copy-done.17, bf16[2,272,256]{2,1,0:T(8,128)(2,1)S(1)} %copy-done.13, ...), custom_call_target="tpu_custom_call" | custom-call | flops 6039797760 | bytes 2097152 | tf_op jit(solution)/shard_map/span_attend/pallas_call | solution.py:325
  157.7 1.0 copy-done.4
  160.1 1.3 copy-done.5
  161.4 1.1 copy-done.7
  162.5 1.1 copy-done.9
  163.7 8.7 %finish.1 = (bf16[256,2560]{1,0:T(8,128)(2,1)}, bf16[2,2560]{1,0:T(2,128)(2,1)}) custom-call(s32[17]{0:T(128)S(1)} %pad_add_fusion.info_ref, bf16[2,256,1280]{2,1,0:T(8,128)(2,1)S(1)} %copy-done.5, bf16[16,2560]{1,0:T(8,128)(2,1)S(1)} %pad.18.datt_ref, bf16[256,2560]{1,0:T(8,128)(2,1)S(1)} %bitcast.71, bf16[2,2560]{1,0:T(2,128)(2,1)S(1)} %copy-done.18, ...), custom_call_target="tpu_custom_call" | custom-call | flops 3355443200 | bytes 13107200 | tf_op jit(solution)/shard_map/finish/pallas_call | solution.py:397
  (113 shorter events, 14.0 us)
Async XLA Ops:
  7.2 98.7 %all-gather.2.cloned.1.call-start = ((), (), s32[]{:S(2)}) async-start(), calls=%async_computation.3 | async-start | bytes 7987200 | tf_op jit(solution)/shard_map/all_gather | solution.py:508
  9.8 2.5 %collective-permute-start = (bf16[20,2816]{1,0:T(8,128)(2,1)S(1)}, bf16[20,2816]{1,0:T(8,128)(2,1)S(1)}, u32[]{:S(2)}, u32[]{:S(2)}) collective-permute-start(bf16[20,2816]{1,0:T(8,128)(2,1)S(1)} %maximum_select_fusion.3), channel_id=1, source_target_pairs={{0,16},{1,17},{2,18},{3,19},{4,20},{5,21},{6,22},{7,23},{8,24},{9,... | collective-permute-start | bytes 337928 | tf_op jit(solution)/shard_map/ppermute | solution.py:449
  13.0 67.8 %collective-permute-start.13 = (bf16[256,2560]{1,0:T(8,128)(2,1)}, bf16[256,2560]{1,0:T(8,128)(2,1)S(1)}, u32[]{:S(2)}, u32[]{:S(2)}) collective-permute-start(bf16[256,2560]{1,0:T(8,128)(2,1)} %bitcast.69), channel_id=1, source_target_pairs={{0,16},{1,17},{2,18},{3,19},{4,20},{5,21},{6,22},{7,23},{8,24},{9,... | collective-permute-start | bytes 3932168 | tf_op jit(solution)/shard_map/ppermute | solution.py:449
  14.1 50.0 %collective-permute-start.14 = (s32[256]{0:T(256)S(1)}, s32[256]{0:T(256)S(1)}, u32[]{:S(2)}, u32[]{:S(2)}) collective-permute-start(s32[256]{0:T(256)S(1)} %iota_add_fusion), channel_id=1, source_target_pairs={{0,16},{1,17},{2,18},{3,19},{4,20},{5,21},{6,22},{7,23},{8,24},{9,... | collective-permute-start | bytes 3080 | tf_op jit(solution)/shard_map/ppermute | solution.py:449
  18.7 27.3 %copy-start.19 = (s32[256]{0:T(256)S(1)}, s32[256]{0:T(256)}, u32[]{:S(2)}) copy-start(s32[256]{0:T(256)} %slot_ref.1) | copy-start | bytes 3076
  20.5 6.9 %collective-permute-start.1 = (bf16[40,1280]{1,0:T(8,128)(2,1)S(1)}, bf16[40,1280]{1,0:T(8,128)(2,1)S(1)}, u32[]{:S(2)}, u32[]{:S(2)}) collective-permute-start(bf16[40,1280]{1,0:T(8,128)(2,1)S(1)} %slice.78.refs_0_), channel_id=1, source_target_pairs={{0,1},{1,2},{2,3},{3,0},{4,5},{5,6},{6,7},{7,4},{8,9},{9,10},{10,1... | collective-permute-start | bytes 307208 | tf_op jit(solution)/shard_map/ppermute | solution.py:445
  22.3 8.1 %collective-permute-start.2 = (bf16[40,1280]{1,0:T(8,128)(2,1)S(1)}, bf16[40,1280]{1,0:T(8,128)(2,1)S(1)}, u32[]{:S(2)}, u32[]{:S(2)}) collective-permute-start(bf16[40,1280]{1,0:T(8,128)(2,1)S(1)} %slice.78.refs_0_), channel_id=1, source_target_pairs={{0,2},{1,3},{2,0},{3,1},{4,6},{5,7},{6,4},{7,5},{8,10},{9,11},{10,... | collective-permute-start | bytes 307208 | tf_op jit(solution)/shard_map/ppermute | solution.py:445
  25.6 4.8 %collective-permute-start.3 = (bf16[40,1280]{1,0:T(8,128)(2,1)S(1)}, bf16[40,1280]{1,0:T(8,128)(2,1)S(1)}, u32[]{:S(2)}, u32[]{:S(2)}) collective-permute-start(bf16[40,1280]{1,0:T(8,128)(2,1)S(1)} %slice.78.refs_0_), channel_id=1, source_target_pairs={{0,3},{1,0},{2,1},{3,2},{4,7},{5,4},{6,5},{7,6},{8,11},{9,8},{10,9... | collective-permute-start | bytes 307208 | tf_op jit(solution)/shard_map/ppermute | solution.py:445
  30.6 21.5 %collective-permute-start.4 = (bf16[2,80,640]{2,1,0:T(8,128)(2,1)S(1)}, bf16[2,80,640]{2,1,0:T(8,128)(2,1)}, u32[]{:S(2)}, u32[]{:S(2)}) collective-permute-start(bf16[2,80,640]{2,1,0:T(8,128)(2,1)S(1)} %get-tuple-element.49), channel_id=1, source_target_pairs={{0,32},{1,33},{2,34},{3,35},{4,36},{5,37},{6,38},{7,39},{8,40},{9,... | collective-permute-start | bytes 614408 | tf_op jit(solution)/shard_map/ppermute | solution.py:445
  33.4 21.3 %collective-permute-start.8 = (bf16[2,80,640]{2,1,0:T(8,128)(2,1)S(1)}, bf16[2,80,640]{2,1,0:T(8,128)(2,1)}, u32[]{:S(2)}, u32[]{:S(2)}) collective-permute-start(bf16[2,80,640]{2,1,0:T(8,128)(2,1)S(1)} %get-tuple-element.48), channel_id=1, source_target_pairs={{0,4},{1,5},{2,6},{3,7},{4,8},{5,9},{6,10},{7,11},{8,12},{9,13},{1... | collective-permute-start | bytes 614408 | tf_op jit(solution)/shard_map/ppermute | solution.py:445
  36.6 9.4 %all-to-all-start = ((bf16[8,2,24,128]{3,2,1,0:T(8,128)(2,1)}), bf16[8,2,24,128]{3,2,1,0:T(8,128)(2,1)S(1)}, u32[]{:S(2)}, u32[]{:S(2)}) async-start(bf16[8,2,24,128]{3,2,1,0:T(8,128)(2,1)} %bitcast.16), calls=%async_computation | async-start | bytes 196608 | tf_op jit(solution)/shard_map/all_to_all | solution.py:430
  47.4 14.4 %all-to-all-start.1 = ((bf16[16,2,24,128]{3,2,1,0:T(8,128)(2,1)}), bf16[16,2,24,128]{3,2,1,0:T(8,128)(2,1)S(1)}, u32[]{:S(2)}, u32[]{:S(2)}) async-start(bf16[16,2,24,128]{3,2,1,0:T(8,128)(2,1)} %bitcast.18), calls=%async_computation.1 | async-start | bytes 393216 | tf_op jit(solution)/shard_map/all_to_all | solution.py:430
  52.1 16.1 %collective-permute-start.5 = (bf16[2,80,640]{2,1,0:T(8,128)(2,1)}, bf16[2,80,640]{2,1,0:T(8,128)(2,1)}, u32[]{:S(2)}, u32[]{:S(2)}) collective-permute-start(bf16[2,80,640]{2,1,0:T(8,128)(2,1)} %collective-permute-done.4), channel_id=1, source_target_pairs={{0,32},{1,33},{2,34},{3,35},{4,36},{5,37},{6,38},{7,39},{8,40},{9,... | collective-permute-start | bytes 614408 | tf_op jit(solution)/shard_map/ppermute | solution.py:445
  54.7 14.0 %collective-permute-start.9 = (bf16[2,80,640]{2,1,0:T(8,128)(2,1)}, bf16[2,80,640]{2,1,0:T(8,128)(2,1)S(1)}, u32[]{:S(2)}, u32[]{:S(2)}) collective-permute-start(bf16[2,80,640]{2,1,0:T(8,128)(2,1)} %collective-permute-done.8), channel_id=1, source_target_pairs={{0,4},{1,5},{2,6},{3,7},{4,8},{5,9},{6,10},{7,11},{8,12},{9,13},{1... | collective-permute-start | bytes 614408 | tf_op jit(solution)/shard_map/ppermute | solution.py:445
  62.7 2.2 %collective-permute-start.15 = (s32[16]{0:T(128)S(1)}, s32[16]{0:T(128)S(1)}, u32[]{:S(2)}, u32[]{:S(2)}) collective-permute-start(s32[16]{0:T(128)S(1)} %pad.17), channel_id=1, source_target_pairs={{0,16},{1,17},{2,18},{3,19},{4,20},{5,21},{6,22},{7,23},{8,24},{9,... | collective-permute-start | bytes 200 | tf_op jit(solution)/shard_map/ppermute | solution.py:449
  64.1 16.7 %collective-permute-start.12 = (bf16[16,2560]{1,0:T(8,128)(2,1)S(1)}, bf16[16,2560]{1,0:T(8,128)(2,1)S(1)}, u32[]{:S(2)}, u32[]{:S(2)}) collective-permute-start(bf16[16,2560]{1,0:T(8,128)(2,1)S(1)} %pad.16), channel_id=1, source_target_pairs={{0,16},{1,17},{2,18},{3,19},{4,20},{5,21},{6,22},{7,23},{8,24},{9,... | collective-permute-start | bytes 245768 | tf_op jit(solution)/shard_map/ppermute | solution.py:449
  66.3 14.6 %copy-start.1 = (bf16[1,256,2560]{2,1,0:T(8,128)(2,1)S(1)}, bf16[1,256,2560]{2,1,0:T(8,128)(2,1)}, u32[]{:S(2)}) copy-start(bf16[1,256,2560]{2,1,0:T(8,128)(2,1)} %param.14) | copy-start | bytes 3932164
  68.2 8.8 %collective-permute-start.6 = (bf16[2,80,640]{2,1,0:T(8,128)(2,1)}, bf16[2,80,640]{2,1,0:T(8,128)(2,1)S(1)}, u32[]{:S(2)}, u32[]{:S(2)}) collective-permute-start(bf16[2,80,640]{2,1,0:T(8,128)(2,1)} %collective-permute-done.5), channel_id=1, source_target_pairs={{0,32},{1,33},{2,34},{3,35},{4,36},{5,37},{6,38},{7,39},{8,40},{9,... | collective-permute-start | bytes 614408 | tf_op jit(solution)/shard_map/ppermute | solution.py:445
  68.8 9.2 %collective-permute-start.10 = (bf16[2,80,640]{2,1,0:T(8,128)(2,1)S(1)}, bf16[2,80,640]{2,1,0:T(8,128)(2,1)S(1)}, u32[]{:S(2)}, u32[]{:S(2)}) collective-permute-start(bf16[2,80,640]{2,1,0:T(8,128)(2,1)S(1)} %collective-permute-done.9), channel_id=1, source_target_pairs={{0,4},{1,5},{2,6},{3,7},{4,8},{5,9},{6,10},{7,11},{8,12},{9,13},{1... | collective-permute-start | bytes 614408 | tf_op jit(solution)/shard_map/ppermute | solution.py:445
  77.7 25.9 %collective-permute-start.7 = (bf16[4,2,80,640]{3,2,1,0:T(8,128)(2,1)}, bf16[4,2,80,640]{3,2,1,0:T(8,128)(2,1)}, u32[]{:S(2)}, u32[]{:S(2)}) collective-permute-start(bf16[4,2,80,640]{3,2,1,0:T(8,128)(2,1)} %bitcast_dynamic-update-slice_fusion.4.refs_0_), channel_id=1, source_target_pairs={{0,4},{1,5},{2,6},{3,7},{4,8},{5,9},{6,10},{7,11},{8,12},{9,13},{1... | collective-permute-start | bytes 2457608 | tf_op jit(solution)/shard_map/ppermute | solution.py:445
  78.7 24.9 %collective-permute-start.11 = (bf16[2,4,80,640]{3,2,1,0:T(8,128)(2,1)}, bf16[2,4,80,640]{3,2,1,0:T(8,128)(2,1)}, u32[]{:S(2)}, u32[]{:S(2)}) collective-permute-start(bf16[2,4,80,640]{3,2,1,0:T(8,128)(2,1)} %bitcast_dynamic-update-slice_fusion.3.refs_4_), channel_id=1, source_target_pairs={{0,32},{1,33},{2,34},{3,35},{4,36},{5,37},{6,38},{7,39},{8,40},{9,... | collective-permute-start | bytes 2457608 | tf_op jit(solution)/shard_map/ppermute | solution.py:445
  80.9 1.2 copy-start
  103.6 13.0 %collective-permute-start.18 = (bf16[4,2,80,640]{3,2,1,0:T(8,128)(2,1)}, bf16[4,2,80,640]{3,2,1,0:T(8,128)(2,1)}, u32[]{:S(2)}, u32[]{:S(2)}) collective-permute-start(bf16[4,2,80,640]{3,2,1,0:T(8,128)(2,1)} %collective-permute-done.7.refs_1_), channel_id=1, source_target_pairs={{0,4},{1,5},{2,6},{3,7},{4,8},{5,9},{6,10},{7,11},{8,12},{9,13},{1... | collective-permute-start | bytes 2457608 | tf_op jit(solution)/shard_map/ppermute | solution.py:445
  105.0 14.3 %collective-permute-start.19 = (bf16[2,4,80,640]{3,2,1,0:T(8,128)(2,1)}, bf16[2,4,80,640]{3,2,1,0:T(8,128)(2,1)}, u32[]{:S(2)}, u32[]{:S(2)}) collective-permute-start(bf16[2,4,80,640]{3,2,1,0:T(8,128)(2,1)} %collective-permute-done.11.refs_5_), channel_id=1, source_target_pairs={{0,32},{1,33},{2,34},{3,35},{4,36},{5,37},{6,38},{7,39},{8,40},{9,... | collective-permute-start | bytes 2457608 | tf_op jit(solution)/shard_map/ppermute | solution.py:445
  111.7 11.9 %copy-start.14 = (bf16[4,272,256]{2,1,0:T(8,128)(2,1)}, bf16[4,272,256]{2,1,0:T(8,128)(2,1)S(1)}, u32[]{:S(2)}) copy-start(bf16[4,272,256]{2,1,0:T(8,128)(2,1)S(1)} %get-tuple-element.31.ab1_ref.oab_ref) | copy-start | bytes 1671172
  111.7 10.6 %collective-permute-start.16 = (bf16[4,272,256]{2,1,0:T(8,128)(2,1)S(1)}, bf16[4,272,256]{2,1,0:T(8,128)(2,1)S(1)}, u32[]{:S(2)}, u32[]{:S(2)}) collective-permute-start(bf16[4,272,256]{2,1,0:T(8,128)(2,1)S(1)} %get-tuple-element.33), channel_id=1, source_target_pairs={{0,16},{1,17},{2,18},{3,19},{4,20},{5,21},{6,22},{7,23},{8,24},{9,... | collective-permute-start | bytes 1671176 | tf_op jit(solution)/shard_map/ppermute | solution.py:449
  112.4 11.1 %copy-start.3 = (bf16[2,2048,512]{2,1,0:T(8,128)(2,1)S(1)}, bf16[2,2048,512]{2,1,0:T(8,128)(2,1)}, u32[]{:S(2)}) copy-start(bf16[2,2048,512]{2,1,0:T(8,128)(2,1)} %cache_ref.3) | copy-start | bytes 12582916
  116.0 11.5 %copy-start.10 = (bf16[2,272,256]{2,1,0:T(8,128)(2,1)}, bf16[2,272,256]{2,1,0:T(8,128)(2,1)S(1)}, u32[]{:S(2)}) copy-start(bf16[2,272,256]{2,1,0:T(8,128)(2,1)S(1)} %get-tuple-element.32.c1_ref.oc_ref) | copy-start | bytes 835588
  116.0 4.3 %collective-permute-start.17 = (bf16[2,272,256]{2,1,0:T(8,128)(2,1)S(1)}, bf16[2,272,256]{2,1,0:T(8,128)(2,1)S(1)}, u32[]{:S(2)}, u32[]{:S(2)}) collective-permute-start(bf16[2,272,256]{2,1,0:T(8,128)(2,1)S(1)} %get-tuple-element.34), channel_id=1, source_target_pairs={{0,16},{1,17},{2,18},{3,19},{4,20},{5,21},{6,22},{7,23},{8,24},{9,... | collective-permute-start | bytes 835592 | tf_op jit(solution)/shard_map/ppermute | solution.py:449
  116.2 18.3 %collective-permute-start.22 = (bf16[4,2,80,640]{3,2,1,0:T(8,128)(2,1)}, bf16[4,2,80,640]{3,2,1,0:T(8,128)(2,1)S(1)}, u32[]{:S(2)}, u32[]{:S(2)}) collective-permute-start(bf16[4,2,80,640]{3,2,1,0:T(8,128)(2,1)} %bitcast_dynamic-update-slice_fusion.4.refs_0_), channel_id=1, source_target_pairs={{0,16},{1,17},{2,18},{3,19},{4,20},{5,21},{6,22},{7,23},{8,24},{9,... | collective-permute-start | bytes 2457608 | tf_op jit(solution)/shard_map/ppermute | solution.py:449
  116.6 18.2 %collective-permute-start.26 = (bf16[2,4,80,640]{3,2,1,0:T(8,128)(2,1)}, bf16[2,4,80,640]{3,2,1,0:T(8,128)(2,1)S(1)}, u32[]{:S(2)}, u32[]{:S(2)}) collective-permute-start(bf16[2,4,80,640]{3,2,1,0:T(8,128)(2,1)} %bitcast_dynamic-update-slice_fusion.3.refs_4_), channel_id=1, source_target_pairs={{0,16},{1,17},{2,18},{3,19},{4,20},{5,21},{6,22},{7,23},{8,24},{9,... | collective-permute-start | bytes 2457608 | tf_op jit(solution)/shard_map/ppermute | solution.py:449
  119.3 16.8 %collective-permute-start.23 = (bf16[4,2,80,640]{3,2,1,0:T(8,128)(2,1)}, bf16[4,2,80,640]{3,2,1,0:T(8,128)(2,1)}, u32[]{:S(2)}, u32[]{:S(2)}) collective-permute-start(bf16[4,2,80,640]{3,2,1,0:T(8,128)(2,1)} %collective-permute-done.7.refs_1_), channel_id=1, source_target_pairs={{0,16},{1,17},{2,18},{3,19},{4,20},{5,21},{6,22},{7,23},{8,24},{9,... | collective-permute-start | bytes 2457608 | tf_op jit(solution)/shard_map/ppermute | solution.py:449
  120.4 7.1 %copy-start.12 = (bf16[2,272,256]{2,1,0:T(8,128)(2,1)}, bf16[2,272,256]{2,1,0:T(8,128)(2,1)S(1)}, u32[]{:S(2)}) copy-start(bf16[2,272,256]{2,1,0:T(8,128)(2,1)S(1)} %collective-permute-done.17.c2_ref.tc_ref) | copy-start | bytes 835588
  120.4 11.8 %collective-permute-start.20 = (bf16[4,2,80,640]{3,2,1,0:T(8,128)(2,1)}, bf16[4,2,80,640]{3,2,1,0:T(8,128)(2,1)}, u32[]{:S(2)}, u32[]{:S(2)}) collective-permute-start(bf16[4,2,80,640]{3,2,1,0:T(8,128)(2,1)} %collective-permute-done.18.refs_2_), channel_id=1, source_target_pairs={{0,4},{1,5},{2,6},{3,7},{4,8},{5,9},{6,10},{7,11},{8,12},{9,13},{1... | collective-permute-start | bytes 2457608 | tf_op jit(solution)/shard_map/ppermute | solution.py:445
  122.3 5.3 %copy-start.16 = (bf16[4,272,256]{2,1,0:T(8,128)(2,1)}, bf16[4,272,256]{2,1,0:T(8,128)(2,1)S(1)}, u32[]{:S(2)}) copy-start(bf16[4,272,256]{2,1,0:T(8,128)(2,1)S(1)} %collective-permute-done.16.ab2_ref.tab_ref) | copy-start | bytes 1671172
  122.3 12.1 %collective-permute-start.21 = (bf16[2,4,80,640]{3,2,1,0:T(8,128)(2,1)}, bf16[2,4,80,640]{3,2,1,0:T(8,128)(2,1)}, u32[]{:S(2)}, u32[]{:S(2)}) collective-permute-start(bf16[2,4,80,640]{3,2,1,0:T(8,128)(2,1)} %collective-permute-done.19.refs_6_), channel_id=1, source_target_pairs={{0,32},{1,33},{2,34},{3,35},{4,36},{5,37},{6,38},{7,39},{8,40},{9,... | collective-permute-start | bytes 2457608 | tf_op jit(solution)/shard_map/ppermute | solution.py:445
  127.5 31.3 %all-to-all-start.2 = ((bf16[128,2,24,128]{3,2,1,0:T(8,128)(2,1)}), bf16[128,2,24,128]{3,2,1,0:T(8,128)(2,1)S(1)}, u32[]{:S(2)}, u32[]{:S(2)}) async-start(bf16[128,2,24,128]{3,2,1,0:T(8,128)(2,1)} %bitcast.30), calls=%async_computation.2 | async-start | bytes 3145728 | tf_op jit(solution)/shard_map/all_to_all | solution.py:430
  132.2 27.2 %collective-permute-start.27 = (bf16[2,4,80,640]{3,2,1,0:T(8,128)(2,1)}, bf16[2,4,80,640]{3,2,1,0:T(8,128)(2,1)}, u32[]{:S(2)}, u32[]{:S(2)}) collective-permute-start(bf16[2,4,80,640]{3,2,1,0:T(8,128)(2,1)} %collective-permute-done.11.refs_5_), channel_id=1, source_target_pairs={{0,16},{1,17},{2,18},{3,19},{4,20},{5,21},{6,22},{7,23},{8,24},{9,... | collective-permute-start | bytes 2457608 | tf_op jit(solution)/shard_map/ppermute | solution.py:449
  134.3 25.1 %collective-permute-start.24 = (bf16[4,2,80,640]{3,2,1,0:T(8,128)(2,1)}, bf16[4,2,80,640]{3,2,1,0:T(8,128)(2,1)}, u32[]{:S(2)}, u32[]{:S(2)}) collective-permute-start(bf16[4,2,80,640]{3,2,1,0:T(8,128)(2,1)} %collective-permute-done.18.refs_2_), channel_id=1, source_target_pairs={{0,16},{1,17},{2,18},{3,19},{4,20},{5,21},{6,22},{7,23},{8,24},{9,... | collective-permute-start | bytes 2457608 | tf_op jit(solution)/shard_map/ppermute | solution.py:449
  134.5 3.2 %copy-start.6 = (bf16[4,2,80,640]{3,2,1,0:T(8,128)(2,1)}, bf16[4,2,80,640]{3,2,1,0:T(8,128)(2,1)S(1)}, u32[]{:S(2)}) copy-start(bf16[4,2,80,640]{3,2,1,0:T(8,128)(2,1)S(1)} %collective-permute-done.22.refs_8_) | copy-start | bytes 2457604
  134.5 25.0 %collective-permute-start.28 = (bf16[2,4,80,640]{3,2,1,0:T(8,128)(2,1)}, bf16[2,4,80,640]{3,2,1,0:T(8,128)(2,1)}, u32[]{:S(2)}, u32[]{:S(2)}) collective-permute-start(bf16[2,4,80,640]{3,2,1,0:T(8,128)(2,1)} %collective-permute-done.19.refs_6_), channel_id=1, source_target_pairs={{0,16},{1,17},{2,18},{3,19},{4,20},{5,21},{6,22},{7,23},{8,24},{9,... | collective-permute-start | bytes 2457608 | tf_op jit(solution)/shard_map/ppermute | solution.py:449
  134.8 0.9 copy-start.8
  135.8 23.7 %collective-permute-start.25 = (bf16[4,2,80,640]{3,2,1,0:T(8,128)(2,1)}, bf16[4,2,80,640]{3,2,1,0:T(8,128)(2,1)}, u32[]{:S(2)}, u32[]{:S(2)}) collective-permute-start(bf16[4,2,80,640]{3,2,1,0:T(8,128)(2,1)} %collective-permute-done.20.refs_3_), channel_id=1, source_target_pairs={{0,16},{1,17},{2,18},{3,19},{4,20},{5,21},{6,22},{7,23},{8,24},{9,... | collective-permute-start | bytes 2457608 | tf_op jit(solution)/shard_map/ppermute | solution.py:449
  136.0 23.5 %collective-permute-start.29 = (bf16[2,4,80,640]{3,2,1,0:T(8,128)(2,1)}, bf16[2,4,80,640]{3,2,1,0:T(8,128)(2,1)}, u32[]{:S(2)}, u32[]{:S(2)}) collective-permute-start(bf16[2,4,80,640]{3,2,1,0:T(8,128)(2,1)} %collective-permute-done.21.refs_7_), channel_id=1, source_target_pairs={{0,16},{1,17},{2,18},{3,19},{4,20},{5,21},{6,22},{7,23},{8,24},{9,... | collective-permute-start | bytes 2457608 | tf_op jit(solution)/shard_map/ppermute | solution.py:449
  137.6 1.0 copy-start.11
  138.6 1.0 copy-start.13
  139.6 1.1 copy-start.15
  140.6 1.1 copy-start.17
  141.7 1.6 copy-start.20
  143.3 16.2 %copy-start.18 = (bf16[2,2560]{1,0:T(2,128)(2,1)S(1)}, bf16[2,2560]{1,0:T(2,128)(2,1)}, u32[]{:S(2)}) copy-start(bf16[2,2560]{1,0:T(2,128)(2,1)} %dx_ref.1) | copy-start | bytes 30724
  157.7 1.1 copy-start.4
  158.8 1.3 copy-start.2
  160.1 1.3 copy-start.5
  161.4 1.1 copy-start.7
  162.5 1.1 copy-start.9
Sparse Core Ops, SparseCore 0:
  13.1 89.1 all-gather.1

commit v5 on v4

--- a/solution.py
+++ b/solution.py
@@ -417,7 +417,7 @@
             jax.ShapeDtypeStruct((rows, n), BF16),
             jax.ShapeDtypeStruct((drows, n), BF16),
         ],
-        compiler_params=params(24, "arbitrary"),
+        compiler_params=params(60, "arbitrary"),
         cost_estimate=pl.CostEstimate(
             flops=2 * rows * n * n, bytes_accessed=2 * n * n, transcendentals=0
         ),

time: 180 us -> 176 us (0.978)
  local copies, waits for them, and re-layouts: 28 us -> 17.7 us
  waiting for transfers between devices: 31.1 us -> 35.5 us
  Pallas kernels: 43.6 us -> 45.7 us
    unnamed x46 -> x24, local copies, waits for them, and re-layouts: 12.9 us -> 4.81 us
    all_to_all x3, waiting for transfers between devices: 3.07 us -> 6.44 us  [exchange(): lax.all_to_all(sent.reshape((members, -1) + sent.shape[1:]), axes, 0, 0)]
    dynamic_update_slice x8, local copies, waits for them, and re-layouts: 8.5 us -> 5.65 us  [put(): return lax.dynamic_update_slice(whole, jnp.expand_dims(piece, place), start)]
    pallas_call x1, Pallas kernels: 8.72 us -> 10.8 us  [finish(): pl.pallas_call(finish_body, grid_spec=pltpu.PrefetchScalarGridSpec(num_sc...]
  transfers between devices with their start and end apart: 34 -> 34, of which waited for: 9 -> 10; matrix products, arithmetic and copies ran while one was open for 13% -> 12% of each run, Pallas kernels for 19% -> 20%
where the time goes in v5:
time: 176 us; the launch traced here: 175 us
  starting transfers between devices  50.1 us (28%)
  Pallas kernels  45.7 us (26%)
  waiting for transfers between devices  35.5 us (20%)
  local copies, waits for them, and re-layouts  17.7 us (10%)
  between operations  15.1 us (9%)
  other arithmetic  11.1 us (6%)
    ppermute x15, waiting for transfers between devices, send(): return lax.ppermute(v, AXES, list(zip(DEVICES.tolist(), to.tolist())))  27.3 us
    ppermute x15, starting transfers between devices, send(): return lax.ppermute(v, AXES, list(zip(DEVICES.tolist(), to.tolist())))  24.9 us
    pallas_call x1, Pallas kernels, span_attend(): pl.pallas_call(span_body, grid_spec=pltpu.PrefetchScalarGridSpec(num_scal...  14.4 us
    all_to_all x3, starting transfers between devices, exchange(): lax.all_to_all(sent.reshape((members, -1) + sent.shape[1:]), axes, 0, 0)  13.7 us
    ppermute x15, starting transfers between devices, swap(): lax.ppermute(v, AXES, list(zip(DEVICES.tolist(), (DEVICES ^ 16).tolist())))  11.5 us
    pallas_call x1, Pallas kernels, finish(): pl.pallas_call(finish_body, grid_spec=pltpu.PrefetchScalarGridSpec(num_sc...  10.8 us
    pallas_call x2, Pallas kernels, project(): pl.pallas_call(functools.partial(project_body, rows), grid=(count,), in_s...  9.4 us
    all_to_all x3, waiting for transfers between devices, exchange(): lax.all_to_all(sent.reshape((members, -1) + sent.shape[1:]), axes, 0, 0)  6.44 us
  transfers between devices with their start and end apart: 34, of which 10 were waited for; matrix products, arithmetic and copies ran while one was open for 12% of the time, Pallas kernels for 20%

profile of v5, /device:TPU:1, one launch (start us, length us, event | category | flops | bytes accessed | tf_op | source)
XLA Modules:
  0.0 175.2 jit_solution(12305044737275527777)
XLA Ops:
  7.2 0.9 fusion.14
  8.1 0.7 fusion.15
  8.8 0.9 fusion.13
  9.8 1.5 collective-permute-start
  11.3 1.0 collective-permute-done
  12.4 0.7 slice.83
  15.2 0.7 fusion.8
  15.9 0.7 broadcast_in_dim.79.gain_ref
  16.6 0.7 subtract_and_fusion
  17.3 1.4 compare_reduce_fusion
  18.7 1.8 %fusion.order_ref = bf16[640,640]{1,0:T(8,128)(2,1)} fusion(s32[640]{0:T(1024)} %constant.88.clone), kind=kLoop, calls=%fused_computation.2 | loop fusion | flops 819200 | bytes 821760 | tf_op jit(solution)/shard_map/convert_element_type | solution.py:34
  20.5 1.8 %collective-permute-start.1 = (bf16[40,1280]{1,0:T(8,128)(2,1)S(1)}, bf16[40,1280]{1,0:T(8,128)(2,1)S(1)}, u32[]{:S(2)}, u32[]{:S(2)}) collective-permute-start(bf16[40,1280]{1,0:T(8,128)(2,1)S(1)} %slice.78.refs_0_), channel_id=1, source_target_pairs={{0,1},{1,2},{2,3},{3,0},{4,5},{5,6},{6,7},{7,4},{8,9},{9,10},{10,1... | collective-permute-start | bytes 307208 | tf_op jit(solution)/shard_map/ppermute | solution.py:445
  22.3 3.3 %collective-permute-start.2 = (bf16[40,1280]{1,0:T(8,128)(2,1)S(1)}, bf16[40,1280]{1,0:T(8,128)(2,1)S(1)}, u32[]{:S(2)}, u32[]{:S(2)}) collective-permute-start(bf16[40,1280]{1,0:T(8,128)(2,1)S(1)} %slice.78.refs_0_), channel_id=1, source_target_pairs={{0,2},{1,3},{2,0},{3,1},{4,6},{5,7},{6,4},{7,5},{8,10},{9,11},{10,... | collective-permute-start | bytes 307208 | tf_op jit(solution)/shard_map/ppermute | solution.py:445
  25.6 0.7 collective-permute-start.3
  27.4 3.1 %collective-permute-done.2.refs_2_ = bf16[40,1280]{1,0:T(8,128)(2,1)S(1)} collective-permute-done((bf16[40,1280]{1,0:T(8,128)(2,1)S(1)}, bf16[40,1280]{1,0:T(8,128)(2,1)S(1)}, u32[]{:S(2)}, u32[]{:S(2)}) %collective-permute-start.2) | collective-permute-done | bytes 102432 | tf_op jit(solution)/shard_map/ppermute | solution.py:445
  30.6 2.8 %collective-permute-start.4 = (bf16[2,80,640]{2,1,0:T(8,128)(2,1)S(1)}, bf16[2,80,640]{2,1,0:T(8,128)(2,1)S(1)}, u32[]{:S(2)}, u32[]{:S(2)}) collective-permute-start(bf16[2,80,640]{2,1,0:T(8,128)(2,1)S(1)} %get-tuple-element.49), channel_id=1, source_target_pairs={{0,32},{1,33},{2,34},{3,35},{4,36},{5,37},{6,38},{7,39},{8,40},{9,... | collective-permute-start | bytes 614408 | tf_op jit(solution)/shard_map/ppermute | solution.py:445
  33.4 2.5 %collective-permute-start.8 = (bf16[2,80,640]{2,1,0:T(8,128)(2,1)S(1)}, bf16[2,80,640]{2,1,0:T(8,128)(2,1)S(1)}, u32[]{:S(2)}, u32[]{:S(2)}) collective-permute-start(bf16[2,80,640]{2,1,0:T(8,128)(2,1)S(1)} %get-tuple-element.48), channel_id=1, source_target_pairs={{0,4},{1,5},{2,6},{3,7},{4,8},{5,9},{6,10},{7,11},{8,12},{9,13},{1... | collective-permute-start | bytes 614408 | tf_op jit(solution)/shard_map/ppermute | solution.py:445
  36.6 4.4 %all-to-all-start = ((bf16[8,2,24,128]{3,2,1,0:T(8,128)(2,1)}), bf16[8,2,24,128]{3,2,1,0:T(8,128)(2,1)S(1)}, u32[]{:S(2)}, u32[]{:S(2)}) async-start(bf16[8,2,24,128]{3,2,1,0:T(8,128)(2,1)} %bitcast.16), calls=%async_computation | async-start | bytes 196608 | tf_op jit(solution)/shard_map/all_to_all | solution.py:430
  41.0 1.0 broadcast_in_dim.66
  42.0 0.7 bitcast_dynamic-update-slice_fusion.7
  42.7 1.0 broadcast_in_dim.72
  43.7 0.7 bitcast_dynamic-update-slice_fusion.2
  44.4 1.6 all-to-all-done
  46.0 1.4 place.1
  47.4 4.7 %all-to-all-start.1 = ((bf16[16,2,24,128]{3,2,1,0:T(8,128)(2,1)}), bf16[16,2,24,128]{3,2,1,0:T(8,128)(2,1)S(1)}, u32[]{:S(2)}, u32[]{:S(2)}) async-start(bf16[16,2,24,128]{3,2,1,0:T(8,128)(2,1)} %bitcast.18), calls=%async_computation.1 | async-start | bytes 393216 | tf_op jit(solution)/shard_map/all_to_all | solution.py:430
  52.1 2.6 %collective-permute-start.5 = (bf16[2,80,640]{2,1,0:T(8,128)(2,1)S(1)}, bf16[2,80,640]{2,1,0:T(8,128)(2,1)S(1)}, u32[]{:S(2)}, u32[]{:S(2)}) collective-permute-start(bf16[2,80,640]{2,1,0:T(8,128)(2,1)S(1)} %collective-permute-done.4), channel_id=1, source_target_pairs={{0,32},{1,33},{2,34},{3,35},{4,36},{5,37},{6,38},{7,39},{8,40},{9,... | collective-permute-start | bytes 614408 | tf_op jit(solution)/shard_map/ppermute | solution.py:445
  54.7 2.4 %collective-permute-start.9 = (bf16[2,80,640]{2,1,0:T(8,128)(2,1)S(1)}, bf16[2,80,640]{2,1,0:T(8,128)(2,1)S(1)}, u32[]{:S(2)}, u32[]{:S(2)}) collective-permute-start(bf16[2,80,640]{2,1,0:T(8,128)(2,1)S(1)} %collective-permute-done.8), channel_id=1, source_target_pairs={{0,4},{1,5},{2,6},{3,7},{4,8},{5,9},{6,10},{7,11},{8,12},{9,13},{1... | collective-permute-start | bytes 614408 | tf_op jit(solution)/shard_map/ppermute | solution.py:445
  57.1 0.7 bitcast_dynamic-update-slice_fusion.6
  57.8 0.7 bitcast_dynamic-update-slice_fusion.1
  58.5 3.2 %all-to-all-done.1 = bf16[16,2,24,128]{3,2,1,0:T(8,128)(2,1)S(1)} async-done(((bf16[16,2,24,128]{3,2,1,0:T(8,128)(2,1)}), bf16[16,2,24,128]{3,2,1,0:T(8,128)(2,1)S(1)}, u32[]{:S(2)}, u32[]{:S(2)}) %all-to-all-start.1) | async-done | bytes 196640 | tf_op jit(solution)/shard_map/all_to_all | solution.py:430
  62.7 1.4 collective-permute-start.15
  64.2 0.7 collective-permute-done.15
  65.0 1.0 fusion.4
  66.5 0.9 pad_maximum_fusion.1.cos_ref
  67.4 0.9 pad_maximum_fusion.2.sin_ref
  68.8 0.9 collective-permute-start.10
  69.7 0.7 bitcast_dynamic-update-slice_fusion.5
  70.4 0.7 bitcast_dynamic-update-slice_fusion
  71.2 5.1 %collective-permute-done.6 = bf16[2,80,640]{2,1,0:T(8,128)(2,1)S(1)} collective-permute-done((bf16[2,80,640]{2,1,0:T(8,128)(2,1)S(1)}, bf16[2,80,640]{2,1,0:T(8,128)(2,1)S(1)}, u32[]{:S(2)}, u32[]{:S(2)}) %collective-permute-start.6) | collective-permute-done | bytes 204832 | tf_op jit(solution)/shard_map/ppermute | solution.py:445
  76.3 0.7 bitcast_dynamic-update-slice_fusion.4.refs_0_
  77.0 1.0 collective-permute-done.10
  78.0 0.7 bitcast_dynamic-update-slice_fusion.3.refs_4_
  78.7 1.7 collective-permute-start.11
  80.6 0.9 copy-done
  81.6 4.1 %norm_ordered.2.refs_0_ = bf16[544,2560]{1,0:T(8,128)(2,1)S(1)} custom-call(bf16[512,2560]{1,0:T(8,128)(2,1)S(1)} %pad_maximum_fusion.x_ref, f32[1,2560]{1,0:T(1,128)S(1)} %broadcast_in_dim.79.gain_ref, bf16[640,640]{1,0:T(8,128)(2,1)S(1)} %copy-done), custom_call_target="tpu_custom_call" | custom-call | flops 1677721600 | bytes 5242880 | tf_op jit(solution)/shard_map/norm_ordered/pallas_call | solution.py:57
  86.1 17.6 %collective-permute-done.7.refs_1_ = bf16[4,2,80,640]{3,2,1,0:T(8,128)(2,1)} collective-permute-done((bf16[4,2,80,640]{3,2,1,0:T(8,128)(2,1)}, bf16[4,2,80,640]{3,2,1,0:T(8,128)(2,1)}, u32[]{:S(2)}, u32[]{:S(2)}) %collective-permute-start.7) | collective-permute-done | bytes 819232 | tf_op jit(solution)/shard_map/ppermute | solution.py:445
  103.7 1.4 collective-permute-start.18
  105.0 0.9 collective-permute-start.19
  105.9 5.8 %project.2 = (bf16[4,272,256]{2,1,0:T(8,128)(2,1)S(1)}, bf16[4,272,256]{2,1,0:T(8,128)(2,1)S(1)}) custom-call(bf16[544,2560]{1,0:T(8,128)(2,1)S(1)} %norm_ordered.3.x_ref, bf16[2560,1536]{1,0:T(8,128)(2,1)} %all-gather.2.cloned.1.call-done.w_ref, f32[2,544,128]{2,1,0:T(8,128)} %pad_maximum_fusion.1.cos_ref, f32[2,544,128]{2,1,0:T(8,128)} %pad_maximum_fusion.2.sin_ref), custom_call_target="tpu_custom_call" | custom-call | flops 2852126720 | bytes 5242880 | tf_op jit(solution)/shard_map/project/pallas_call | solution.py:97
  112.3 3.6 %project.3 = (bf16[2,272,256]{2,1,0:T(8,128)(2,1)S(1)}, bf16[2,272,256]{2,1,0:T(8,128)(2,1)S(1)}) custom-call(bf16[544,2560]{1,0:T(8,128)(2,1)S(1)} %norm_ordered.3.x_ref, bf16[2560,1536]{1,0:T(8,128)(2,1)} %all-gather.2.cloned.1.call-done.w_ref, f32[2,544,128]{2,1,0:T(8,128)} %pad_maximum_fusion.1.cos_ref, f32[2,544,128]{2,1,0:T(8,128)} %pad_maximum_fusion.2.sin_ref), custom_call_target="tpu_custom_call" | custom-call | flops 1426063360 | bytes 2621440 | tf_op jit(solution)/shard_map/project/pallas_call | solution.py:97
  116.5 2.9 %collective-permute-start.26 = (bf16[2,4,80,640]{3,2,1,0:T(8,128)(2,1)}, bf16[2,4,80,640]{3,2,1,0:T(8,128)(2,1)}, u32[]{:S(2)}, u32[]{:S(2)}) collective-permute-start(bf16[2,4,80,640]{3,2,1,0:T(8,128)(2,1)} %bitcast_dynamic-update-slice_fusion.3.refs_4_), channel_id=1, source_target_pairs={{0,16},{1,17},{2,18},{3,19},{4,20},{5,21},{6,22},{7,23},{8,24},{9,... | collective-permute-start | bytes 2457608 | tf_op jit(solution)/shard_map/ppermute | solution.py:449
  119.3 0.9 collective-permute-start.23
  120.2 2.1 %collective-permute-start.20 = (bf16[4,2,80,640]{3,2,1,0:T(8,128)(2,1)}, bf16[4,2,80,640]{3,2,1,0:T(8,128)(2,1)}, u32[]{:S(2)}, u32[]{:S(2)}) collective-permute-start(bf16[4,2,80,640]{3,2,1,0:T(8,128)(2,1)} %collective-permute-done.18.refs_2_), channel_id=1, source_target_pairs={{0,4},{1,5},{2,6},{3,7},{4,8},{5,9},{6,10},{7,11},{8,12},{9,13},{1... | collective-permute-start | bytes 2457608 | tf_op jit(solution)/shard_map/ppermute | solution.py:445
  122.3 1.3 collective-permute-start.21
  123.6 3.9 %decode_attend.1 = bf16[256,24,128]{2,1,0:T(8,128)(2,1)} custom-call(s32[5]{0:T(128)S(1)} %pad_add_fusion.1.info_ref, bf16[4,272,256]{2,1,0:T(8,128)(2,1)S(1)} %get-tuple-element.31.ab1_ref.oab_ref, bf16[2,272,256]{2,1,0:T(8,128)(2,1)S(1)} %get-tuple-element.32.c1_ref.oc_ref, bf16[4,272,256]{2,1,0:T(8,128)(2,1)S(1)} %collective-permute-done.16.ab2_ref.tab_ref, ...), custom_call_target="tpu_custom_call" | custom-call | flops 67108864 | bytes 4194304 | tf_op jit(solution)/shard_map/decode_attend/pallas_call | solution.py:163
  127.6 4.6 %all-to-all-start.2 = ((bf16[128,2,24,128]{3,2,1,0:T(8,128)(2,1)}), bf16[128,2,24,128]{3,2,1,0:T(8,128)(2,1)S(1)}, u32[]{:S(2)}, u32[]{:S(2)}) async-start(bf16[128,2,24,128]{3,2,1,0:T(8,128)(2,1)} %bitcast.30), calls=%async_computation.2 | async-start | bytes 3145728 | tf_op jit(solution)/shard_map/all_to_all | solution.py:430
  132.2 1.9 %collective-permute-start.27 = (bf16[2,4,80,640]{3,2,1,0:T(8,128)(2,1)}, bf16[2,4,80,640]{3,2,1,0:T(8,128)(2,1)}, u32[]{:S(2)}, u32[]{:S(2)}) collective-permute-start(bf16[2,4,80,640]{3,2,1,0:T(8,128)(2,1)} %collective-permute-done.11.refs_5_), channel_id=1, source_target_pairs={{0,16},{1,17},{2,18},{3,19},{4,20},{5,21},{6,22},{7,23},{8,24},{9,... | collective-permute-start | bytes 2457608 | tf_op jit(solution)/shard_map/ppermute | solution.py:449
  135.8 0.7 fusion.2
  136.5 1.1 copy-done.6
  137.6 1.6 copy-done.8
  139.2 14.4 %span_attend.1.att_ref = bf16[2,256,1280]{2,1,0:T(8,128)(2,1)S(1)} custom-call(s32[1]{0:T(128)S(6)} %copy.50.index_ref, bf16[4,272,256]{2,1,0:T(8,128)(2,1)S(1)} %copy-done.4, bf16[2,272,256]{2,1,0:T(8,128)(2,1)S(1)} %get-tuple-element.32.c1_ref.oc_ref, bf16[4,272,256]{2,1,0:T(8,128)(2,1)S(1)} %copy-done.6, ...), custom_call_target="tpu_custom_call" | custom-call | flops 6039797760 | bytes 2097152 | tf_op jit(solution)/shard_map/span_attend/pallas_call | solution.py:325
  153.6 1.1 copy-done.2
  154.7 1.6 all-to-all-done.2
  157.5 10.8 %finish.1 = (bf16[256,2560]{1,0:T(8,128)(2,1)}, bf16[2,2560]{1,0:T(2,128)(2,1)}) custom-call(s32[17]{0:T(128)} %pad_add_fusion.info_ref, bf16[2,256,1280]{2,1,0:T(8,128)(2,1)} %copy-done.2, bf16[16,2560]{1,0:T(8,128)(2,1)} %pad.18.datt_ref, bf16[256,2560]{1,0:T(8,128)(2,1)} %bitcast.74, bf16[2,2560]{1,0:T(2,128)(2,1)} %dx_ref.1, ...), custom_call_target="tpu_custom_call" | custom-call | flops 3355443200 | bytes 13107200 | tf_op jit(solution)/shard_map/finish/pallas_call | solution.py:397
  (91 shorter events, 10.4 us)
Async XLA Ops:
  7.2 98.7 %all-gather.2.cloned.1.call-start = ((), (), s32[]{:S(2)}) async-start(), calls=%async_computation.3 | async-start | bytes 7987200 | tf_op jit(solution)/shard_map/all_gather | solution.py:508
  9.8 2.5 %collective-permute-start = (bf16[20,2816]{1,0:T(8,128)(2,1)S(1)}, bf16[20,2816]{1,0:T(8,128)(2,1)S(1)}, u32[]{:S(2)}, u32[]{:S(2)}) collective-permute-start(bf16[20,2816]{1,0:T(8,128)(2,1)S(1)} %maximum_select_fusion.3), channel_id=1, source_target_pairs={{0,16},{1,17},{2,18},{3,19},{4,20},{5,21},{6,22},{7,23},{8,24},{9,... | collective-permute-start | bytes 337928 | tf_op jit(solution)/shard_map/ppermute | solution.py:449
  13.0 67.4 %collective-permute-start.13 = (bf16[256,2560]{1,0:T(8,128)(2,1)}, bf16[256,2560]{1,0:T(8,128)(2,1)S(1)}, u32[]{:S(2)}, u32[]{:S(2)}) collective-permute-start(bf16[256,2560]{1,0:T(8,128)(2,1)} %bitcast.73), channel_id=1, source_target_pairs={{0,16},{1,17},{2,18},{3,19},{4,20},{5,21},{6,22},{7,23},{8,24},{9,... | collective-permute-start | bytes 3932168 | tf_op jit(solution)/shard_map/ppermute | solution.py:449
  14.2 50.0 %collective-permute-start.14 = (s32[256]{0:T(256)S(1)}, s32[256]{0:T(256)S(1)}, u32[]{:S(2)}, u32[]{:S(2)}) collective-permute-start(s32[256]{0:T(256)S(1)} %iota_add_fusion), channel_id=1, source_target_pairs={{0,16},{1,17},{2,18},{3,19},{4,20},{5,21},{6,22},{7,23},{8,24},{9,... | collective-permute-start | bytes 3080 | tf_op jit(solution)/shard_map/ppermute | solution.py:449
  18.7 27.3 %copy-start.7 = (s32[256]{0:T(256)S(1)}, s32[256]{0:T(256)}, u32[]{:S(2)}) copy-start(s32[256]{0:T(256)} %slot_ref.1) | copy-start | bytes 3076
  20.5 6.9 %collective-permute-start.1 = (bf16[40,1280]{1,0:T(8,128)(2,1)S(1)}, bf16[40,1280]{1,0:T(8,128)(2,1)S(1)}, u32[]{:S(2)}, u32[]{:S(2)}) collective-permute-start(bf16[40,1280]{1,0:T(8,128)(2,1)S(1)} %slice.78.refs_0_), channel_id=1, source_target_pairs={{0,1},{1,2},{2,3},{3,0},{4,5},{5,6},{6,7},{7,4},{8,9},{9,10},{10,1... | collective-permute-start | bytes 307208 | tf_op jit(solution)/shard_map/ppermute | solution.py:445
  22.3 8.1 %collective-permute-start.2 = (bf16[40,1280]{1,0:T(8,128)(2,1)S(1)}, bf16[40,1280]{1,0:T(8,128)(2,1)S(1)}, u32[]{:S(2)}, u32[]{:S(2)}) collective-permute-start(bf16[40,1280]{1,0:T(8,128)(2,1)S(1)} %slice.78.refs_0_), channel_id=1, source_target_pairs={{0,2},{1,3},{2,0},{3,1},{4,6},{5,7},{6,4},{7,5},{8,10},{9,11},{10,... | collective-permute-start | bytes 307208 | tf_op jit(solution)/shard_map/ppermute | solution.py:445
  25.6 4.8 %collective-permute-start.3 = (bf16[40,1280]{1,0:T(8,128)(2,1)S(1)}, bf16[40,1280]{1,0:T(8,128)(2,1)S(1)}, u32[]{:S(2)}, u32[]{:S(2)}) collective-permute-start(bf16[40,1280]{1,0:T(8,128)(2,1)S(1)} %slice.78.refs_0_), channel_id=1, source_target_pairs={{0,3},{1,0},{2,1},{3,2},{4,7},{5,4},{6,5},{7,6},{8,11},{9,8},{10,9... | collective-permute-start | bytes 307208 | tf_op jit(solution)/shard_map/ppermute | solution.py:445
  30.6 21.5 %collective-permute-start.4 = (bf16[2,80,640]{2,1,0:T(8,128)(2,1)S(1)}, bf16[2,80,640]{2,1,0:T(8,128)(2,1)S(1)}, u32[]{:S(2)}, u32[]{:S(2)}) collective-permute-start(bf16[2,80,640]{2,1,0:T(8,128)(2,1)S(1)} %get-tuple-element.49), channel_id=1, source_target_pairs={{0,32},{1,33},{2,34},{3,35},{4,36},{5,37},{6,38},{7,39},{8,40},{9,... | collective-permute-start | bytes 614408 | tf_op jit(solution)/shard_map/ppermute | solution.py:445
  33.4 21.3 %collective-permute-start.8 = (bf16[2,80,640]{2,1,0:T(8,128)(2,1)S(1)}, bf16[2,80,640]{2,1,0:T(8,128)(2,1)S(1)}, u32[]{:S(2)}, u32[]{:S(2)}) collective-permute-start(bf16[2,80,640]{2,1,0:T(8,128)(2,1)S(1)} %get-tuple-element.48), channel_id=1, source_target_pairs={{0,4},{1,5},{2,6},{3,7},{4,8},{5,9},{6,10},{7,11},{8,12},{9,13},{1... | collective-permute-start | bytes 614408 | tf_op jit(solution)/shard_map/ppermute | solution.py:445
  36.6 9.4 %all-to-all-start = ((bf16[8,2,24,128]{3,2,1,0:T(8,128)(2,1)}), bf16[8,2,24,128]{3,2,1,0:T(8,128)(2,1)S(1)}, u32[]{:S(2)}, u32[]{:S(2)}) async-start(bf16[8,2,24,128]{3,2,1,0:T(8,128)(2,1)} %bitcast.16), calls=%async_computation | async-start | bytes 196608 | tf_op jit(solution)/shard_map/all_to_all | solution.py:430
  47.4 14.4 %all-to-all-start.1 = ((bf16[16,2,24,128]{3,2,1,0:T(8,128)(2,1)}), bf16[16,2,24,128]{3,2,1,0:T(8,128)(2,1)S(1)}, u32[]{:S(2)}, u32[]{:S(2)}) async-start(bf16[16,2,24,128]{3,2,1,0:T(8,128)(2,1)} %bitcast.18), calls=%async_computation.1 | async-start | bytes 393216 | tf_op jit(solution)/shard_map/all_to_all | solution.py:430
  52.1 16.2 %collective-permute-start.5 = (bf16[2,80,640]{2,1,0:T(8,128)(2,1)S(1)}, bf16[2,80,640]{2,1,0:T(8,128)(2,1)S(1)}, u32[]{:S(2)}, u32[]{:S(2)}) collective-permute-start(bf16[2,80,640]{2,1,0:T(8,128)(2,1)S(1)} %collective-permute-done.4), channel_id=1, source_target_pairs={{0,32},{1,33},{2,34},{3,35},{4,36},{5,37},{6,38},{7,39},{8,40},{9,... | collective-permute-start | bytes 614408 | tf_op jit(solution)/shard_map/ppermute | solution.py:445
  54.7 14.1 %collective-permute-start.9 = (bf16[2,80,640]{2,1,0:T(8,128)(2,1)S(1)}, bf16[2,80,640]{2,1,0:T(8,128)(2,1)S(1)}, u32[]{:S(2)}, u32[]{:S(2)}) collective-permute-start(bf16[2,80,640]{2,1,0:T(8,128)(2,1)S(1)} %collective-permute-done.8), channel_id=1, source_target_pairs={{0,4},{1,5},{2,6},{3,7},{4,8},{5,9},{6,10},{7,11},{8,12},{9,13},{1... | collective-permute-start | bytes 614408 | tf_op jit(solution)/shard_map/ppermute | solution.py:445
  62.7 2.2 %collective-permute-start.15 = (s32[16]{0:T(128)S(1)}, s32[16]{0:T(128)S(1)}, u32[]{:S(2)}, u32[]{:S(2)}) collective-permute-start(s32[16]{0:T(128)S(1)} %pad.17), channel_id=1, source_target_pairs={{0,16},{1,17},{2,18},{3,19},{4,20},{5,21},{6,22},{7,23},{8,24},{9,... | collective-permute-start | bytes 200 | tf_op jit(solution)/shard_map/ppermute | solution.py:449
  64.1 16.3 %collective-permute-start.12 = (bf16[16,2560]{1,0:T(8,128)(2,1)S(1)}, bf16[16,2560]{1,0:T(8,128)(2,1)S(1)}, u32[]{:S(2)}, u32[]{:S(2)}) collective-permute-start(bf16[16,2560]{1,0:T(8,128)(2,1)S(1)} %pad.16), channel_id=1, source_target_pairs={{0,16},{1,17},{2,18},{3,19},{4,20},{5,21},{6,22},{7,23},{8,24},{9,... | collective-permute-start | bytes 245768 | tf_op jit(solution)/shard_map/ppermute | solution.py:449
  66.3 14.2 %copy-start.9 = (bf16[1,256,2560]{2,1,0:T(8,128)(2,1)S(1)}, bf16[1,256,2560]{2,1,0:T(8,128)(2,1)}, u32[]{:S(2)}) copy-start(bf16[1,256,2560]{2,1,0:T(8,128)(2,1)} %param.14) | copy-start | bytes 3932164
  68.3 8.0 %collective-permute-start.6 = (bf16[2,80,640]{2,1,0:T(8,128)(2,1)S(1)}, bf16[2,80,640]{2,1,0:T(8,128)(2,1)S(1)}, u32[]{:S(2)}, u32[]{:S(2)}) collective-permute-start(bf16[2,80,640]{2,1,0:T(8,128)(2,1)S(1)} %collective-permute-done.5), channel_id=1, source_target_pairs={{0,32},{1,33},{2,34},{3,35},{4,36},{5,37},{6,38},{7,39},{8,40},{9,... | collective-permute-start | bytes 614408 | tf_op jit(solution)/shard_map/ppermute | solution.py:445
  68.8 9.2 %collective-permute-start.10 = (bf16[2,80,640]{2,1,0:T(8,128)(2,1)S(1)}, bf16[2,80,640]{2,1,0:T(8,128)(2,1)S(1)}, u32[]{:S(2)}, u32[]{:S(2)}) collective-permute-start(bf16[2,80,640]{2,1,0:T(8,128)(2,1)S(1)} %collective-permute-done.9), channel_id=1, source_target_pairs={{0,4},{1,5},{2,6},{3,7},{4,8},{5,9},{6,10},{7,11},{8,12},{9,13},{1... | collective-permute-start | bytes 614408 | tf_op jit(solution)/shard_map/ppermute | solution.py:445
  77.0 26.7 %collective-permute-start.7 = (bf16[4,2,80,640]{3,2,1,0:T(8,128)(2,1)}, bf16[4,2,80,640]{3,2,1,0:T(8,128)(2,1)}, u32[]{:S(2)}, u32[]{:S(2)}) collective-permute-start(bf16[4,2,80,640]{3,2,1,0:T(8,128)(2,1)} %bitcast_dynamic-update-slice_fusion.4.refs_0_), channel_id=1, source_target_pairs={{0,4},{1,5},{2,6},{3,7},{4,8},{5,9},{6,10},{7,11},{8,12},{9,13},{1... | collective-permute-start | bytes 2457608 | tf_op jit(solution)/shard_map/ppermute | solution.py:445
  78.7 25.0 %collective-permute-start.11 = (bf16[2,4,80,640]{3,2,1,0:T(8,128)(2,1)}, bf16[2,4,80,640]{3,2,1,0:T(8,128)(2,1)}, u32[]{:S(2)}, u32[]{:S(2)}) collective-permute-start(bf16[2,4,80,640]{3,2,1,0:T(8,128)(2,1)} %bitcast_dynamic-update-slice_fusion.3.refs_4_), channel_id=1, source_target_pairs={{0,32},{1,33},{2,34},{3,35},{4,36},{5,37},{6,38},{7,39},{8,40},{9,... | collective-permute-start | bytes 2457608 | tf_op jit(solution)/shard_map/ppermute | solution.py:445
  80.4 1.1 copy-start
  103.7 12.8 %collective-permute-start.18 = (bf16[4,2,80,640]{3,2,1,0:T(8,128)(2,1)}, bf16[4,2,80,640]{3,2,1,0:T(8,128)(2,1)}, u32[]{:S(2)}, u32[]{:S(2)}) collective-permute-start(bf16[4,2,80,640]{3,2,1,0:T(8,128)(2,1)} %collective-permute-done.7.refs_1_), channel_id=1, source_target_pairs={{0,4},{1,5},{2,6},{3,7},{4,8},{5,9},{6,10},{7,11},{8,12},{9,13},{1... | collective-permute-start | bytes 2457608 | tf_op jit(solution)/shard_map/ppermute | solution.py:445
  105.0 14.3 %collective-permute-start.19 = (bf16[2,4,80,640]{3,2,1,0:T(8,128)(2,1)}, bf16[2,4,80,640]{3,2,1,0:T(8,128)(2,1)}, u32[]{:S(2)}, u32[]{:S(2)}) collective-permute-start(bf16[2,4,80,640]{3,2,1,0:T(8,128)(2,1)} %collective-permute-done.11.refs_5_), channel_id=1, source_target_pairs={{0,32},{1,33},{2,34},{3,35},{4,36},{5,37},{6,38},{7,39},{8,40},{9,... | collective-permute-start | bytes 2457608 | tf_op jit(solution)/shard_map/ppermute | solution.py:445
  111.7 11.9 %copy-start.3 = (bf16[4,272,256]{2,1,0:T(8,128)(2,1)}, bf16[4,272,256]{2,1,0:T(8,128)(2,1)S(1)}, u32[]{:S(2)}) copy-start(bf16[4,272,256]{2,1,0:T(8,128)(2,1)S(1)} %get-tuple-element.31.ab1_ref.oab_ref) | copy-start | bytes 1671172
  111.7 10.6 %collective-permute-start.16 = (bf16[4,272,256]{2,1,0:T(8,128)(2,1)S(1)}, bf16[4,272,256]{2,1,0:T(8,128)(2,1)S(1)}, u32[]{:S(2)}, u32[]{:S(2)}) collective-permute-start(bf16[4,272,256]{2,1,0:T(8,128)(2,1)S(1)} %get-tuple-element.33), channel_id=1, source_target_pairs={{0,16},{1,17},{2,18},{3,19},{4,20},{5,21},{6,22},{7,23},{8,24},{9,... | collective-permute-start | bytes 1671176 | tf_op jit(solution)/shard_map/ppermute | solution.py:449
  112.3 11.3 %copy-start.1 = (bf16[2,2048,512]{2,1,0:T(8,128)(2,1)S(1)}, bf16[2,2048,512]{2,1,0:T(8,128)(2,1)}, u32[]{:S(2)}) copy-start(bf16[2,2048,512]{2,1,0:T(8,128)(2,1)} %cache_ref.3) | copy-start | bytes 12582916
  115.9 4.3 %collective-permute-start.17 = (bf16[2,272,256]{2,1,0:T(8,128)(2,1)S(1)}, bf16[2,272,256]{2,1,0:T(8,128)(2,1)S(1)}, u32[]{:S(2)}, u32[]{:S(2)}) collective-permute-start(bf16[2,272,256]{2,1,0:T(8,128)(2,1)S(1)} %get-tuple-element.34), channel_id=1, source_target_pairs={{0,16},{1,17},{2,18},{3,19},{4,20},{5,21},{6,22},{7,23},{8,24},{9,... | collective-permute-start | bytes 835592 | tf_op jit(solution)/shard_map/ppermute | solution.py:449
  116.0 18.2 %collective-permute-start.22 = (bf16[4,2,80,640]{3,2,1,0:T(8,128)(2,1)}, bf16[4,2,80,640]{3,2,1,0:T(8,128)(2,1)}, u32[]{:S(2)}, u32[]{:S(2)}) collective-permute-start(bf16[4,2,80,640]{3,2,1,0:T(8,128)(2,1)} %bitcast_dynamic-update-slice_fusion.4.refs_0_), channel_id=1, source_target_pairs={{0,16},{1,17},{2,18},{3,19},{4,20},{5,21},{6,22},{7,23},{8,24},{9,... | collective-permute-start | bytes 2457608 | tf_op jit(solution)/shard_map/ppermute | solution.py:449
  116.5 18.1 %collective-permute-start.26 = (bf16[2,4,80,640]{3,2,1,0:T(8,128)(2,1)}, bf16[2,4,80,640]{3,2,1,0:T(8,128)(2,1)}, u32[]{:S(2)}, u32[]{:S(2)}) collective-permute-start(bf16[2,4,80,640]{3,2,1,0:T(8,128)(2,1)} %bitcast_dynamic-update-slice_fusion.3.refs_4_), channel_id=1, source_target_pairs={{0,16},{1,17},{2,18},{3,19},{4,20},{5,21},{6,22},{7,23},{8,24},{9,... | collective-permute-start | bytes 2457608 | tf_op jit(solution)/shard_map/ppermute | solution.py:449
  119.3 15.4 %collective-permute-start.23 = (bf16[4,2,80,640]{3,2,1,0:T(8,128)(2,1)}, bf16[4,2,80,640]{3,2,1,0:T(8,128)(2,1)}, u32[]{:S(2)}, u32[]{:S(2)}) collective-permute-start(bf16[4,2,80,640]{3,2,1,0:T(8,128)(2,1)} %collective-permute-done.7.refs_1_), channel_id=1, source_target_pairs={{0,16},{1,17},{2,18},{3,19},{4,20},{5,21},{6,22},{7,23},{8,24},{9,... | collective-permute-start | bytes 2457608 | tf_op jit(solution)/shard_map/ppermute | solution.py:449
  120.2 12.0 %collective-permute-start.20 = (bf16[4,2,80,640]{3,2,1,0:T(8,128)(2,1)}, bf16[4,2,80,640]{3,2,1,0:T(8,128)(2,1)}, u32[]{:S(2)}, u32[]{:S(2)}) collective-permute-start(bf16[4,2,80,640]{3,2,1,0:T(8,128)(2,1)} %collective-permute-done.18.refs_2_), channel_id=1, source_target_pairs={{0,4},{1,5},{2,6},{3,7},{4,8},{5,9},{6,10},{7,11},{8,12},{9,13},{1... | collective-permute-start | bytes 2457608 | tf_op jit(solution)/shard_map/ppermute | solution.py:445
  122.3 5.3 %copy-start.5 = (bf16[4,272,256]{2,1,0:T(8,128)(2,1)}, bf16[4,272,256]{2,1,0:T(8,128)(2,1)S(1)}, u32[]{:S(2)}) copy-start(bf16[4,272,256]{2,1,0:T(8,128)(2,1)S(1)} %collective-permute-done.16.ab2_ref.tab_ref) | copy-start | bytes 1671172
  122.3 11.8 %collective-permute-start.21 = (bf16[2,4,80,640]{3,2,1,0:T(8,128)(2,1)}, bf16[2,4,80,640]{3,2,1,0:T(8,128)(2,1)}, u32[]{:S(2)}, u32[]{:S(2)}) collective-permute-start(bf16[2,4,80,640]{3,2,1,0:T(8,128)(2,1)} %collective-permute-done.19.refs_6_), channel_id=1, source_target_pairs={{0,32},{1,33},{2,34},{3,35},{4,36},{5,37},{6,38},{7,39},{8,40},{9,... | collective-permute-start | bytes 2457608 | tf_op jit(solution)/shard_map/ppermute | solution.py:445
  127.6 8.9 %copy-start.4 = (bf16[4,272,256]{2,1,0:T(8,128)(2,1)S(1)}, bf16[4,272,256]{2,1,0:T(8,128)(2,1)}, u32[]{:S(2)}) copy-start(bf16[4,272,256]{2,1,0:T(8,128)(2,1)} %copy-done.3) | copy-start | bytes 1671172
  127.6 28.6 %all-to-all-start.2 = ((bf16[128,2,24,128]{3,2,1,0:T(8,128)(2,1)}), bf16[128,2,24,128]{3,2,1,0:T(8,128)(2,1)S(1)}, u32[]{:S(2)}, u32[]{:S(2)}) async-start(bf16[128,2,24,128]{3,2,1,0:T(8,128)(2,1)} %bitcast.30), calls=%async_computation.2 | async-start | bytes 3145728 | tf_op jit(solution)/shard_map/all_to_all | solution.py:430
  132.2 25.3 %collective-permute-start.27 = (bf16[2,4,80,640]{3,2,1,0:T(8,128)(2,1)}, bf16[2,4,80,640]{3,2,1,0:T(8,128)(2,1)}, u32[]{:S(2)}, u32[]{:S(2)}) collective-permute-start(bf16[2,4,80,640]{3,2,1,0:T(8,128)(2,1)} %collective-permute-done.11.refs_5_), channel_id=1, source_target_pairs={{0,16},{1,17},{2,18},{3,19},{4,20},{5,21},{6,22},{7,23},{8,24},{9,... | collective-permute-start | bytes 2457608 | tf_op jit(solution)/shard_map/ppermute | solution.py:449
  134.1 23.4 %collective-permute-start.24 = (bf16[4,2,80,640]{3,2,1,0:T(8,128)(2,1)}, bf16[4,2,80,640]{3,2,1,0:T(8,128)(2,1)}, u32[]{:S(2)}, u32[]{:S(2)}) collective-permute-start(bf16[4,2,80,640]{3,2,1,0:T(8,128)(2,1)} %collective-permute-done.18.refs_2_), channel_id=1, source_target_pairs={{0,16},{1,17},{2,18},{3,19},{4,20},{5,21},{6,22},{7,23},{8,24},{9,... | collective-permute-start | bytes 2457608 | tf_op jit(solution)/shard_map/ppermute | solution.py:449
  134.2 23.3 %collective-permute-start.28 = (bf16[2,4,80,640]{3,2,1,0:T(8,128)(2,1)}, bf16[2,4,80,640]{3,2,1,0:T(8,128)(2,1)}, u32[]{:S(2)}, u32[]{:S(2)}) collective-permute-start(bf16[2,4,80,640]{3,2,1,0:T(8,128)(2,1)} %collective-permute-done.19.refs_6_), channel_id=1, source_target_pairs={{0,16},{1,17},{2,18},{3,19},{4,20},{5,21},{6,22},{7,23},{8,24},{9,... | collective-permute-start | bytes 2457608 | tf_op jit(solution)/shard_map/ppermute | solution.py:449
  134.6 22.9 %collective-permute-start.25 = (bf16[4,2,80,640]{3,2,1,0:T(8,128)(2,1)}, bf16[4,2,80,640]{3,2,1,0:T(8,128)(2,1)}, u32[]{:S(2)}, u32[]{:S(2)}) collective-permute-start(bf16[4,2,80,640]{3,2,1,0:T(8,128)(2,1)} %collective-permute-done.20.refs_3_), channel_id=1, source_target_pairs={{0,16},{1,17},{2,18},{3,19},{4,20},{5,21},{6,22},{7,23},{8,24},{9,... | collective-permute-start | bytes 2457608 | tf_op jit(solution)/shard_map/ppermute | solution.py:449
  134.7 22.8 %collective-permute-start.29 = (bf16[2,4,80,640]{3,2,1,0:T(8,128)(2,1)}, bf16[2,4,80,640]{3,2,1,0:T(8,128)(2,1)}, u32[]{:S(2)}, u32[]{:S(2)}) collective-permute-start(bf16[2,4,80,640]{3,2,1,0:T(8,128)(2,1)} %collective-permute-done.21.refs_7_), channel_id=1, source_target_pairs={{0,16},{1,17},{2,18},{3,19},{4,20},{5,21},{6,22},{7,23},{8,24},{9,... | collective-permute-start | bytes 2457608 | tf_op jit(solution)/shard_map/ppermute | solution.py:449
  136.5 1.1 copy-start.6
  137.6 1.6 copy-start.8
  153.6 1.1 copy-start.2
Sparse Core Ops, SparseCore 0:
  13.2 89.5 all-gather.1

commit v6 on v5

--- a/solution.py
+++ b/solution.py
@@ -585,9 +585,6 @@
     theirs_c = swap(other_c)
     ours_ab, other_ab = project(0, 4, rows, lhs, first_weight, cos, sin, hd)
     theirs_ab = swap(other_ab)
-    swap_last(ours_ab)
-    parts, _ = lax.optimization_barrier(([m[-1] for m in mine], ours_ab))
-    ring_step(parts)
 
     key = jnp.where(first_core, ours_c[1], theirs_c[1])
     value = jnp.where(first_core, theirs_c[1], ours_c[1])
@@ -597,9 +594,12 @@
     routed = decode_attend(info, quarters, keyval, decode_cache, places)
     home = exchange(routed, AXES)
     swap_last(routed)
+    parts, _ = lax.optimization_barrier(([m[-1] for m in mine], routed))
+    ring_step(parts)
     att = span_attend(
         span_index, (ours_ab, ours_c), (theirs_ab, theirs_c), key, value, rows, span_cache
     )
+    swap_last(att)
     home = pick(home, slot_of_mine, by_device).reshape(own, SLAB * 128)[:, :width]
     span_output, decode_output = finish(
         finish_info,

time: 176 us -> 177 us (level)
  starting transfers between devices: 50.1 us -> 47.9 us
  waiting for transfers between devices: 35.5 us -> 37.5 us
    ppermute x15, starting transfers between devices: 11.5 us -> 7.16 us  [swap(): lax.ppermute(v, AXES, list(zip(DEVICES.tolist(), (DEVICES ^ 16).tolist())))]
    ppermute x15, waiting for transfers between devices: 1.74 us -> 4.7 us  [swap(): lax.ppermute(v, AXES, list(zip(DEVICES.tolist(), (DEVICES ^ 16).tolist())))]
    ppermute x15, starting transfers between devices: 24.9 us -> 27.1 us  [send(): return lax.ppermute(v, AXES, list(zip(DEVICES.tolist(), to.tolist())))]
    unnamed x24 -> x26, local copies, waits for them, and re-layouts: 4.81 us -> 4.86 us
  transfers between devices with their start and end apart: 34 -> 34, of which waited for: 10 -> 13; matrix products, arithmetic and copies ran while one was open for 12% -> 12% of each run, Pallas kernels for 20% -> 20%
where the time goes in v6:
time: 177 us; the launch traced here: 176 us
  starting transfers between devices  47.9 us (27%)
  Pallas kernels  45.6 us (26%)
  waiting for transfers between devices  37.5 us (21%)
  local copies, waits for them, and re-layouts  18.8 us (11%)
  between operations  15.1 us (9%)
  other arithmetic  11.1 us (6%)
    ppermute x15, starting transfers between devices, send(): return lax.ppermute(v, AXES, list(zip(DEVICES.tolist(), to.tolist())))  27.1 us
    ppermute x15, waiting for transfers between devices, send(): return lax.ppermute(v, AXES, list(zip(DEVICES.tolist(), to.tolist())))  26.6 us
    pallas_call x1, Pallas kernels, span_attend(): pl.pallas_call(span_body, grid_spec=pltpu.PrefetchScalarGridSpec(num_scal...  14.4 us
    all_to_all x3, starting transfers between devices, exchange(): lax.all_to_all(sent.reshape((members, -1) + sent.shape[1:]), axes, 0, 0)  13.6 us
    pallas_call x1, Pallas kernels, finish(): pl.pallas_call(finish_body, grid_spec=pltpu.PrefetchScalarGridSpec(num_sc...  10.7 us
    pallas_call x2, Pallas kernels, project(): pl.pallas_call(functools.partial(project_body, rows), grid=(count,), in_s...  9.4 us
    ppermute x15, starting transfers between devices, swap(): lax.ppermute(v, AXES, list(zip(DEVICES.tolist(), (DEVICES ^ 16).tolist())))  7.16 us
    dynamic_update_slice x8, local copies, waits for them, and re-layouts, put(): return lax.dynamic_update_slice(whole, jnp.expand_dims(piece, place), start)  6.64 us
  transfers between devices with their start and end apart: 34, of which 13 were waited for; matrix products, arithmetic and copies ran while one was open for 12% of the time, Pallas kernels for 20%

profile of v6, /device:TPU:1, one launch (start us, length us, event | category | flops | bytes accessed | tf_op | source)
XLA Modules:
  0.0 176.1 jit_solution(6930006377333921948)
XLA Ops:
  7.2 0.9 fusion.14
  8.1 0.7 fusion.15
  8.8 0.9 fusion.13
  9.8 1.5 collective-permute-start
  11.3 1.0 collective-permute-done
  15.2 0.7 fusion.8
  15.9 0.7 broadcast_in_dim.79.gain_ref
  16.6 0.7 subtract_and_fusion
  17.3 1.4 compare_reduce_fusion
  18.7 1.8 %fusion.order_ref = bf16[640,640]{1,0:T(8,128)(2,1)} fusion(s32[640]{0:T(1024)} %constant.88.clone), kind=kLoop, calls=%fused_computation.2 | loop fusion | flops 819200 | bytes 821760 | tf_op jit(solution)/shard_map/convert_element_type | solution.py:34
  20.5 1.8 %collective-permute-start.1 = (bf16[40,1280]{1,0:T(8,128)(2,1)S(1)}, bf16[40,1280]{1,0:T(8,128)(2,1)S(1)}, u32[]{:S(2)}, u32[]{:S(2)}) collective-permute-start(bf16[40,1280]{1,0:T(8,128)(2,1)S(1)} %slice.78.refs_0_), channel_id=1, source_target_pairs={{0,1},{1,2},{2,3},{3,0},{4,5},{5,6},{6,7},{7,4},{8,9},{9,10},{10,1... | collective-permute-start | bytes 307208 | tf_op jit(solution)/shard_map/ppermute | solution.py:445
  22.3 3.3 %collective-permute-start.2 = (bf16[40,1280]{1,0:T(8,128)(2,1)S(1)}, bf16[40,1280]{1,0:T(8,128)(2,1)S(1)}, u32[]{:S(2)}, u32[]{:S(2)}) collective-permute-start(bf16[40,1280]{1,0:T(8,128)(2,1)S(1)} %slice.78.refs_0_), channel_id=1, source_target_pairs={{0,2},{1,3},{2,0},{3,1},{4,6},{5,7},{6,4},{7,5},{8,10},{9,11},{10,... | collective-permute-start | bytes 307208 | tf_op jit(solution)/shard_map/ppermute | solution.py:445
  25.6 0.7 collective-permute-start.3
  27.4 3.1 %collective-permute-done.2.refs_2_ = bf16[40,1280]{1,0:T(8,128)(2,1)S(1)} collective-permute-done((bf16[40,1280]{1,0:T(8,128)(2,1)S(1)}, bf16[40,1280]{1,0:T(8,128)(2,1)S(1)}, u32[]{:S(2)}, u32[]{:S(2)}) %collective-permute-start.2) | collective-permute-done | bytes 102432 | tf_op jit(solution)/shard_map/ppermute | solution.py:445
  30.6 2.8 %collective-permute-start.4 = (bf16[2,80,640]{2,1,0:T(8,128)(2,1)S(1)}, bf16[2,80,640]{2,1,0:T(8,128)(2,1)S(1)}, u32[]{:S(2)}, u32[]{:S(2)}) collective-permute-start(bf16[2,80,640]{2,1,0:T(8,128)(2,1)S(1)} %get-tuple-element.49), channel_id=1, source_target_pairs={{0,32},{1,33},{2,34},{3,35},{4,36},{5,37},{6,38},{7,39},{8,40},{9,... | collective-permute-start | bytes 614408 | tf_op jit(solution)/shard_map/ppermute | solution.py:445
  33.4 2.5 %collective-permute-start.8 = (bf16[2,80,640]{2,1,0:T(8,128)(2,1)S(1)}, bf16[2,80,640]{2,1,0:T(8,128)(2,1)S(1)}, u32[]{:S(2)}, u32[]{:S(2)}) collective-permute-start(bf16[2,80,640]{2,1,0:T(8,128)(2,1)S(1)} %get-tuple-element.48), channel_id=1, source_target_pairs={{0,4},{1,5},{2,6},{3,7},{4,8},{5,9},{6,10},{7,11},{8,12},{9,13},{1... | collective-permute-start | bytes 614408 | tf_op jit(solution)/shard_map/ppermute | solution.py:445
  36.6 4.4 %all-to-all-start = ((bf16[8,2,24,128]{3,2,1,0:T(8,128)(2,1)}), bf16[8,2,24,128]{3,2,1,0:T(8,128)(2,1)S(1)}, u32[]{:S(2)}, u32[]{:S(2)}) async-start(bf16[8,2,24,128]{3,2,1,0:T(8,128)(2,1)} %bitcast.16), calls=%async_computation | async-start | bytes 196608 | tf_op jit(solution)/shard_map/all_to_all | solution.py:430
  41.0 1.0 broadcast_in_dim.66
  42.0 0.7 bitcast_dynamic-update-slice_fusion.7
  42.7 1.0 broadcast_in_dim.72
  43.7 0.7 bitcast_dynamic-update-slice_fusion.2
  44.4 1.6 all-to-all-done
  46.0 1.4 place.1
  47.4 4.7 %all-to-all-start.1 = ((bf16[16,2,24,128]{3,2,1,0:T(8,128)(2,1)}), bf16[16,2,24,128]{3,2,1,0:T(8,128)(2,1)S(1)}, u32[]{:S(2)}, u32[]{:S(2)}) async-start(bf16[16,2,24,128]{3,2,1,0:T(8,128)(2,1)} %bitcast.18), calls=%async_computation.1 | async-start | bytes 393216 | tf_op jit(solution)/shard_map/all_to_all | solution.py:430
  52.1 2.6 %collective-permute-start.5 = (bf16[2,80,640]{2,1,0:T(8,128)(2,1)S(1)}, bf16[2,80,640]{2,1,0:T(8,128)(2,1)}, u32[]{:S(2)}, u32[]{:S(2)}) collective-permute-start(bf16[2,80,640]{2,1,0:T(8,128)(2,1)S(1)} %collective-permute-done.4), channel_id=1, source_target_pairs={{0,32},{1,33},{2,34},{3,35},{4,36},{5,37},{6,38},{7,39},{8,40},{9,... | collective-permute-start | bytes 614408 | tf_op jit(solution)/shard_map/ppermute | solution.py:445
  54.7 2.4 %collective-permute-start.9 = (bf16[2,80,640]{2,1,0:T(8,128)(2,1)S(1)}, bf16[2,80,640]{2,1,0:T(8,128)(2,1)S(1)}, u32[]{:S(2)}, u32[]{:S(2)}) collective-permute-start(bf16[2,80,640]{2,1,0:T(8,128)(2,1)S(1)} %collective-permute-done.8), channel_id=1, source_target_pairs={{0,4},{1,5},{2,6},{3,7},{4,8},{5,9},{6,10},{7,11},{8,12},{9,13},{1... | collective-permute-start | bytes 614408 | tf_op jit(solution)/shard_map/ppermute | solution.py:445
  57.1 0.7 bitcast_dynamic-update-slice_fusion.6
  57.8 0.7 bitcast_dynamic-update-slice_fusion.1
  58.5 3.3 %all-to-all-done.1 = bf16[16,2,24,128]{3,2,1,0:T(8,128)(2,1)S(1)} async-done(((bf16[16,2,24,128]{3,2,1,0:T(8,128)(2,1)}), bf16[16,2,24,128]{3,2,1,0:T(8,128)(2,1)S(1)}, u32[]{:S(2)}, u32[]{:S(2)}) %all-to-all-start.1) | async-done | bytes 196640 | tf_op jit(solution)/shard_map/all_to_all | solution.py:430
  62.7 1.4 collective-permute-start.15
  64.2 0.7 collective-permute-done.15
  65.0 1.0 fusion.4
  66.5 0.8 pad_maximum_fusion.1.cos_ref
  67.4 0.9 pad_maximum_fusion.2.sin_ref
  68.8 0.9 collective-permute-start.10
  69.7 1.7 bitcast_dynamic-update-slice_fusion.5
  71.4 0.7 bitcast_dynamic-update-slice_fusion
  72.1 4.7 %collective-permute-done.6 = bf16[2,80,640]{2,1,0:T(8,128)(2,1)S(1)} collective-permute-done((bf16[2,80,640]{2,1,0:T(8,128)(2,1)}, bf16[2,80,640]{2,1,0:T(8,128)(2,1)S(1)}, u32[]{:S(2)}, u32[]{:S(2)}) %collective-permute-start.6) | collective-permute-done | bytes 204832 | tf_op jit(solution)/shard_map/ppermute | solution.py:445
  76.8 0.7 bitcast_dynamic-update-slice_fusion.4.refs_0_
  77.9 0.7 bitcast_dynamic-update-slice_fusion.3.refs_4_
  78.6 2.3 %collective-permute-start.11 = (bf16[2,4,80,640]{3,2,1,0:T(8,128)(2,1)}, bf16[2,4,80,640]{3,2,1,0:T(8,128)(2,1)}, u32[]{:S(2)}, u32[]{:S(2)}) collective-permute-start(bf16[2,4,80,640]{3,2,1,0:T(8,128)(2,1)} %bitcast_dynamic-update-slice_fusion.3.refs_4_), channel_id=1, source_target_pairs={{0,32},{1,33},{2,34},{3,35},{4,36},{5,37},{6,38},{7,39},{8,40},{9,... | collective-permute-start | bytes 2457608 | tf_op jit(solution)/shard_map/ppermute | solution.py:445
  81.1 1.0 copy-done
  82.1 4.1 %norm_ordered.2.refs_0_ = bf16[544,2560]{1,0:T(8,128)(2,1)S(1)} custom-call(bf16[512,2560]{1,0:T(8,128)(2,1)S(1)} %pad_maximum_fusion.x_ref, f32[1,2560]{1,0:T(1,128)S(1)} %broadcast_in_dim.79.gain_ref, bf16[640,640]{1,0:T(8,128)(2,1)S(1)} %copy-done), custom_call_target="tpu_custom_call" | custom-call | flops 1677721600 | bytes 5242880 | tf_op jit(solution)/shard_map/norm_ordered/pallas_call | solution.py:57
  86.6 17.0 %collective-permute-done.7.refs_1_ = bf16[4,2,80,640]{3,2,1,0:T(8,128)(2,1)} collective-permute-done((bf16[4,2,80,640]{3,2,1,0:T(8,128)(2,1)}, bf16[4,2,80,640]{3,2,1,0:T(8,128)(2,1)}, u32[]{:S(2)}, u32[]{:S(2)}) %collective-permute-start.7) | collective-permute-done | bytes 819232 | tf_op jit(solution)/shard_map/ppermute | solution.py:445
  103.6 1.4 collective-permute-start.18
  105.0 0.8 collective-permute-start.19
  105.8 3.4 %project.3 = (bf16[2,272,256]{2,1,0:T(8,128)(2,1)S(1)}, bf16[2,272,256]{2,1,0:T(8,128)(2,1)S(1)}) custom-call(bf16[544,2560]{1,0:T(8,128)(2,1)S(1)} %norm_ordered.3.x_ref, bf16[2560,1536]{1,0:T(8,128)(2,1)} %all-gather.2.cloned.1.call-done.w_ref, f32[2,544,128]{2,1,0:T(8,128)} %pad_maximum_fusion.1.cos_ref, f32[2,544,128]{2,1,0:T(8,128)} %pad_maximum_fusion.2.sin_ref), custom_call_target="tpu_custom_call" | custom-call | flops 1426063360 | bytes 2621440 | tf_op jit(solution)/shard_map/project/pallas_call | solution.py:97
  109.3 0.8 collective-permute-start.17
  110.1 6.0 %project.2 = (bf16[4,272,256]{2,1,0:T(8,128)(2,1)S(1)}, bf16[4,272,256]{2,1,0:T(8,128)(2,1)S(1)}) custom-call(bf16[544,2560]{1,0:T(8,128)(2,1)S(1)} %norm_ordered.3.x_ref, bf16[2560,1536]{1,0:T(8,128)(2,1)} %all-gather.2.cloned.1.call-done.w_ref, f32[2,544,128]{2,1,0:T(8,128)} %pad_maximum_fusion.1.cos_ref, f32[2,544,128]{2,1,0:T(8,128)} %pad_maximum_fusion.2.sin_ref), custom_call_target="tpu_custom_call" | custom-call | flops 2852126720 | bytes 5242880 | tf_op jit(solution)/shard_map/project/pallas_call | solution.py:97
  116.2 1.9 %collective-permute-done.16.ab2_ref.tab_ref = bf16[4,272,256]{2,1,0:T(8,128)(2,1)S(1)} collective-permute-done((bf16[4,272,256]{2,1,0:T(8,128)(2,1)S(1)}, bf16[4,272,256]{2,1,0:T(8,128)(2,1)S(1)}, u32[]{:S(2)}, u32[]{:S(2)}) %collective-permute-start.16) | collective-permute-done | bytes 557088 | tf_op jit(solution)/shard_map/ppermute | solution.py:449
  118.1 3.9 %decode_attend.1 = bf16[256,24,128]{2,1,0:T(8,128)(2,1)} custom-call(s32[5]{0:T(128)S(1)} %pad_add_fusion.1.info_ref, bf16[4,272,256]{2,1,0:T(8,128)(2,1)S(1)} %get-tuple-element.31.ab1_ref.oab_ref, bf16[2,272,256]{2,1,0:T(8,128)(2,1)S(1)} %get-tuple-element.32.c1_ref.oc_ref, bf16[4,272,256]{2,1,0:T(8,128)(2,1)S(1)} %collective-permute-done.16.ab2_ref.tab_ref, ...), custom_call_target="tpu_custom_call" | custom-call | flops 67108864 | bytes 4194304 | tf_op jit(solution)/shard_map/decode_attend/pallas_call | solution.py:163
  122.1 2.5 %collective-permute-start.20 = (bf16[4,2,80,640]{3,2,1,0:T(8,128)(2,1)}, bf16[4,2,80,640]{3,2,1,0:T(8,128)(2,1)}, u32[]{:S(2)}, u32[]{:S(2)}) collective-permute-start(bf16[4,2,80,640]{3,2,1,0:T(8,128)(2,1)} %collective-permute-done.18.refs_2_), channel_id=1, source_target_pairs={{0,4},{1,5},{2,6},{3,7},{4,8},{5,9},{6,10},{7,11},{8,12},{9,13},{1... | collective-permute-start | bytes 2457608 | tf_op jit(solution)/shard_map/ppermute | solution.py:445
  124.6 2.4 %collective-permute-start.21 = (bf16[2,4,80,640]{3,2,1,0:T(8,128)(2,1)}, bf16[2,4,80,640]{3,2,1,0:T(8,128)(2,1)}, u32[]{:S(2)}, u32[]{:S(2)}) collective-permute-start(bf16[2,4,80,640]{3,2,1,0:T(8,128)(2,1)} %collective-permute-done.19.refs_6_), channel_id=1, source_target_pairs={{0,32},{1,33},{2,34},{3,35},{4,36},{5,37},{6,38},{7,39},{8,40},{9,... | collective-permute-start | bytes 2457608 | tf_op jit(solution)/shard_map/ppermute | solution.py:445
  127.5 4.5 %all-to-all-start.2 = ((bf16[128,2,24,128]{3,2,1,0:T(8,128)(2,1)}), bf16[128,2,24,128]{3,2,1,0:T(8,128)(2,1)S(1)}, u32[]{:S(2)}, u32[]{:S(2)}) async-start(bf16[128,2,24,128]{3,2,1,0:T(8,128)(2,1)} %bitcast.30), calls=%async_computation.2 | async-start | bytes 3145728 | tf_op jit(solution)/shard_map/all_to_all | solution.py:430
  132.0 1.0 copy-done.6
  133.0 1.6 copy-done.8
  134.6 14.4 %span_attend.1.att_ref = bf16[2,256,1280]{2,1,0:T(8,128)(2,1)S(1)} custom-call(s32[1]{0:T(128)S(6)} %copy.50.index_ref, bf16[4,272,256]{2,1,0:T(8,128)(2,1)S(1)} %copy-done.4, bf16[2,272,256]{2,1,0:T(8,128)(2,1)S(1)} %get-tuple-element.32.c1_ref.oc_ref, bf16[4,272,256]{2,1,0:T(8,128)(2,1)S(1)} %copy-done.6, ...), custom_call_target="tpu_custom_call" | custom-call | flops 6039797760 | bytes 2097152 | tf_op jit(solution)/shard_map/span_attend/pallas_call | solution.py:325
  149.1 1.1 copy-done.2
  150.1 1.1 collective-permute-start.27
  151.2 1.0 collective-permute-done.21.refs_7_
  154.0 0.7 fusion.2
  154.7 1.4 all-to-all-done.2
  157.3 1.1 collective-permute-done.29.refs_15_
  158.5 10.7 %finish.1 = (bf16[256,2560]{1,0:T(8,128)(2,1)}, bf16[2,2560]{1,0:T(2,128)(2,1)}) custom-call(s32[17]{0:T(128)} %pad_add_fusion.info_ref, bf16[2,256,1280]{2,1,0:T(8,128)(2,1)} %copy-done.2, bf16[16,2560]{1,0:T(8,128)(2,1)} %pad.18.datt_ref, bf16[256,2560]{1,0:T(8,128)(2,1)} %bitcast.74, bf16[2,2560]{1,0:T(2,128)(2,1)} %dx_ref.1, ...), custom_call_target="tpu_custom_call" | custom-call | flops 3355443200 | bytes 13107200 | tf_op jit(solution)/shard_map/finish/pallas_call | solution.py:397
  (93 shorter events, 10.9 us)
Async XLA Ops:
  7.2 98.7 %all-gather.2.cloned.1.call-start = ((), (), s32[]{:S(2)}) async-start(), calls=%async_computation.3 | async-start | bytes 7987200 | tf_op jit(solution)/shard_map/all_gather | solution.py:508
  9.8 2.5 %collective-permute-start = (bf16[20,2816]{1,0:T(8,128)(2,1)S(1)}, bf16[20,2816]{1,0:T(8,128)(2,1)S(1)}, u32[]{:S(2)}, u32[]{:S(2)}) collective-permute-start(bf16[20,2816]{1,0:T(8,128)(2,1)S(1)} %maximum_select_fusion.3), channel_id=1, source_target_pairs={{0,16},{1,17},{2,18},{3,19},{4,20},{5,21},{6,22},{7,23},{8,24},{9,... | collective-permute-start | bytes 337928 | tf_op jit(solution)/shard_map/ppermute | solution.py:449
  13.0 67.9 %collective-permute-start.13 = (bf16[256,2560]{1,0:T(8,128)(2,1)}, bf16[256,2560]{1,0:T(8,128)(2,1)S(1)}, u32[]{:S(2)}, u32[]{:S(2)}) collective-permute-start(bf16[256,2560]{1,0:T(8,128)(2,1)} %bitcast.73), channel_id=1, source_target_pairs={{0,16},{1,17},{2,18},{3,19},{4,20},{5,21},{6,22},{7,23},{8,24},{9,... | collective-permute-start | bytes 3932168 | tf_op jit(solution)/shard_map/ppermute | solution.py:449
  14.1 50.0 %collective-permute-start.14 = (s32[256]{0:T(256)S(1)}, s32[256]{0:T(256)S(1)}, u32[]{:S(2)}, u32[]{:S(2)}) collective-permute-start(s32[256]{0:T(256)S(1)} %iota_add_fusion), channel_id=1, source_target_pairs={{0,16},{1,17},{2,18},{3,19},{4,20},{5,21},{6,22},{7,23},{8,24},{9,... | collective-permute-start | bytes 3080 | tf_op jit(solution)/shard_map/ppermute | solution.py:449
  18.7 27.3 %copy-start.7 = (s32[256]{0:T(256)S(1)}, s32[256]{0:T(256)}, u32[]{:S(2)}) copy-start(s32[256]{0:T(256)} %slot_ref.1) | copy-start | bytes 3076
  20.5 6.9 %collective-permute-start.1 = (bf16[40,1280]{1,0:T(8,128)(2,1)S(1)}, bf16[40,1280]{1,0:T(8,128)(2,1)S(1)}, u32[]{:S(2)}, u32[]{:S(2)}) collective-permute-start(bf16[40,1280]{1,0:T(8,128)(2,1)S(1)} %slice.78.refs_0_), channel_id=1, source_target_pairs={{0,1},{1,2},{2,3},{3,0},{4,5},{5,6},{6,7},{7,4},{8,9},{9,10},{10,1... | collective-permute-start | bytes 307208 | tf_op jit(solution)/shard_map/ppermute | solution.py:445
  22.3 8.1 %collective-permute-start.2 = (bf16[40,1280]{1,0:T(8,128)(2,1)S(1)}, bf16[40,1280]{1,0:T(8,128)(2,1)S(1)}, u32[]{:S(2)}, u32[]{:S(2)}) collective-permute-start(bf16[40,1280]{1,0:T(8,128)(2,1)S(1)} %slice.78.refs_0_), channel_id=1, source_target_pairs={{0,2},{1,3},{2,0},{3,1},{4,6},{5,7},{6,4},{7,5},{8,10},{9,11},{10,... | collective-permute-start | bytes 307208 | tf_op jit(solution)/shard_map/ppermute | solution.py:445
  25.6 4.8 %collective-permute-start.3 = (bf16[40,1280]{1,0:T(8,128)(2,1)S(1)}, bf16[40,1280]{1,0:T(8,128)(2,1)S(1)}, u32[]{:S(2)}, u32[]{:S(2)}) collective-permute-start(bf16[40,1280]{1,0:T(8,128)(2,1)S(1)} %slice.78.refs_0_), channel_id=1, source_target_pairs={{0,3},{1,0},{2,1},{3,2},{4,7},{5,4},{6,5},{7,6},{8,11},{9,8},{10,9... | collective-permute-start | bytes 307208 | tf_op jit(solution)/shard_map/ppermute | solution.py:445
  30.6 21.5 %collective-permute-start.4 = (bf16[2,80,640]{2,1,0:T(8,128)(2,1)S(1)}, bf16[2,80,640]{2,1,0:T(8,128)(2,1)S(1)}, u32[]{:S(2)}, u32[]{:S(2)}) collective-permute-start(bf16[2,80,640]{2,1,0:T(8,128)(2,1)S(1)} %get-tuple-element.49), channel_id=1, source_target_pairs={{0,32},{1,33},{2,34},{3,35},{4,36},{5,37},{6,38},{7,39},{8,40},{9,... | collective-permute-start | bytes 614408 | tf_op jit(solution)/shard_map/ppermute | solution.py:445
  33.4 21.3 %collective-permute-start.8 = (bf16[2,80,640]{2,1,0:T(8,128)(2,1)S(1)}, bf16[2,80,640]{2,1,0:T(8,128)(2,1)S(1)}, u32[]{:S(2)}, u32[]{:S(2)}) collective-permute-start(bf16[2,80,640]{2,1,0:T(8,128)(2,1)S(1)} %get-tuple-element.48), channel_id=1, source_target_pairs={{0,4},{1,5},{2,6},{3,7},{4,8},{5,9},{6,10},{7,11},{8,12},{9,13},{1... | collective-permute-start | bytes 614408 | tf_op jit(solution)/shard_map/ppermute | solution.py:445
  36.6 9.4 %all-to-all-start = ((bf16[8,2,24,128]{3,2,1,0:T(8,128)(2,1)}), bf16[8,2,24,128]{3,2,1,0:T(8,128)(2,1)S(1)}, u32[]{:S(2)}, u32[]{:S(2)}) async-start(bf16[8,2,24,128]{3,2,1,0:T(8,128)(2,1)} %bitcast.16), calls=%async_computation | async-start | bytes 196608 | tf_op jit(solution)/shard_map/all_to_all | solution.py:430
  47.4 14.4 %all-to-all-start.1 = ((bf16[16,2,24,128]{3,2,1,0:T(8,128)(2,1)}), bf16[16,2,24,128]{3,2,1,0:T(8,128)(2,1)S(1)}, u32[]{:S(2)}, u32[]{:S(2)}) async-start(bf16[16,2,24,128]{3,2,1,0:T(8,128)(2,1)} %bitcast.18), calls=%async_computation.1 | async-start | bytes 393216 | tf_op jit(solution)/shard_map/all_to_all | solution.py:430
  52.1 16.1 %collective-permute-start.5 = (bf16[2,80,640]{2,1,0:T(8,128)(2,1)S(1)}, bf16[2,80,640]{2,1,0:T(8,128)(2,1)}, u32[]{:S(2)}, u32[]{:S(2)}) collective-permute-start(bf16[2,80,640]{2,1,0:T(8,128)(2,1)S(1)} %collective-permute-done.4), channel_id=1, source_target_pairs={{0,32},{1,33},{2,34},{3,35},{4,36},{5,37},{6,38},{7,39},{8,40},{9,... | collective-permute-start | bytes 614408 | tf_op jit(solution)/shard_map/ppermute | solution.py:445
  54.7 14.0 %collective-permute-start.9 = (bf16[2,80,640]{2,1,0:T(8,128)(2,1)S(1)}, bf16[2,80,640]{2,1,0:T(8,128)(2,1)S(1)}, u32[]{:S(2)}, u32[]{:S(2)}) collective-permute-start(bf16[2,80,640]{2,1,0:T(8,128)(2,1)S(1)} %collective-permute-done.8), channel_id=1, source_target_pairs={{0,4},{1,5},{2,6},{3,7},{4,8},{5,9},{6,10},{7,11},{8,12},{9,13},{1... | collective-permute-start | bytes 614408 | tf_op jit(solution)/shard_map/ppermute | solution.py:445
  62.7 2.2 %collective-permute-start.15 = (s32[16]{0:T(128)S(1)}, s32[16]{0:T(128)S(1)}, u32[]{:S(2)}, u32[]{:S(2)}) collective-permute-start(s32[16]{0:T(128)S(1)} %pad.17), channel_id=1, source_target_pairs={{0,16},{1,17},{2,18},{3,19},{4,20},{5,21},{6,22},{7,23},{8,24},{9,... | collective-permute-start | bytes 200 | tf_op jit(solution)/shard_map/ppermute | solution.py:449
  64.1 16.8 %collective-permute-start.12 = (bf16[16,2560]{1,0:T(8,128)(2,1)S(1)}, bf16[16,2560]{1,0:T(8,128)(2,1)S(1)}, u32[]{:S(2)}, u32[]{:S(2)}) collective-permute-start(bf16[16,2560]{1,0:T(8,128)(2,1)S(1)} %pad.16), channel_id=1, source_target_pairs={{0,16},{1,17},{2,18},{3,19},{4,20},{5,21},{6,22},{7,23},{8,24},{9,... | collective-permute-start | bytes 245768 | tf_op jit(solution)/shard_map/ppermute | solution.py:449
  66.3 14.6 %copy-start.9 = (bf16[1,256,2560]{2,1,0:T(8,128)(2,1)S(1)}, bf16[1,256,2560]{2,1,0:T(8,128)(2,1)}, u32[]{:S(2)}) copy-start(bf16[1,256,2560]{2,1,0:T(8,128)(2,1)} %param.14) | copy-start | bytes 3932164
  68.2 8.6 %collective-permute-start.6 = (bf16[2,80,640]{2,1,0:T(8,128)(2,1)}, bf16[2,80,640]{2,1,0:T(8,128)(2,1)S(1)}, u32[]{:S(2)}, u32[]{:S(2)}) collective-permute-start(bf16[2,80,640]{2,1,0:T(8,128)(2,1)} %collective-permute-done.5), channel_id=1, source_target_pairs={{0,32},{1,33},{2,34},{3,35},{4,36},{5,37},{6,38},{7,39},{8,40},{9,... | collective-permute-start | bytes 614408 | tf_op jit(solution)/shard_map/ppermute | solution.py:445
  68.8 9.1 %collective-permute-start.10 = (bf16[2,80,640]{2,1,0:T(8,128)(2,1)S(1)}, bf16[2,80,640]{2,1,0:T(8,128)(2,1)S(1)}, u32[]{:S(2)}, u32[]{:S(2)}) collective-permute-start(bf16[2,80,640]{2,1,0:T(8,128)(2,1)S(1)} %collective-permute-done.9), channel_id=1, source_target_pairs={{0,4},{1,5},{2,6},{3,7},{4,8},{5,9},{6,10},{7,11},{8,12},{9,13},{1... | collective-permute-start | bytes 614408 | tf_op jit(solution)/shard_map/ppermute | solution.py:445
  77.6 26.1 %collective-permute-start.7 = (bf16[4,2,80,640]{3,2,1,0:T(8,128)(2,1)}, bf16[4,2,80,640]{3,2,1,0:T(8,128)(2,1)}, u32[]{:S(2)}, u32[]{:S(2)}) collective-permute-start(bf16[4,2,80,640]{3,2,1,0:T(8,128)(2,1)} %bitcast_dynamic-update-slice_fusion.4.refs_0_), channel_id=1, source_target_pairs={{0,4},{1,5},{2,6},{3,7},{4,8},{5,9},{6,10},{7,11},{8,12},{9,13},{1... | collective-permute-start | bytes 2457608 | tf_op jit(solution)/shard_map/ppermute | solution.py:445
  78.6 25.1 %collective-permute-start.11 = (bf16[2,4,80,640]{3,2,1,0:T(8,128)(2,1)}, bf16[2,4,80,640]{3,2,1,0:T(8,128)(2,1)}, u32[]{:S(2)}, u32[]{:S(2)}) collective-permute-start(bf16[2,4,80,640]{3,2,1,0:T(8,128)(2,1)} %bitcast_dynamic-update-slice_fusion.3.refs_4_), channel_id=1, source_target_pairs={{0,32},{1,33},{2,34},{3,35},{4,36},{5,37},{6,38},{7,39},{8,40},{9,... | collective-permute-start | bytes 2457608 | tf_op jit(solution)/shard_map/ppermute | solution.py:445
  80.9 1.2 copy-start
  103.6 18.4 %collective-permute-start.18 = (bf16[4,2,80,640]{3,2,1,0:T(8,128)(2,1)}, bf16[4,2,80,640]{3,2,1,0:T(8,128)(2,1)}, u32[]{:S(2)}, u32[]{:S(2)}) collective-permute-start(bf16[4,2,80,640]{3,2,1,0:T(8,128)(2,1)} %collective-permute-done.7.refs_1_), channel_id=1, source_target_pairs={{0,4},{1,5},{2,6},{3,7},{4,8},{5,9},{6,10},{7,11},{8,12},{9,13},{1... | collective-permute-start | bytes 2457608 | tf_op jit(solution)/shard_map/ppermute | solution.py:445
  105.0 17.0 %collective-permute-start.19 = (bf16[2,4,80,640]{3,2,1,0:T(8,128)(2,1)}, bf16[2,4,80,640]{3,2,1,0:T(8,128)(2,1)}, u32[]{:S(2)}, u32[]{:S(2)}) collective-permute-start(bf16[2,4,80,640]{3,2,1,0:T(8,128)(2,1)} %collective-permute-done.11.refs_5_), channel_id=1, source_target_pairs={{0,32},{1,33},{2,34},{3,35},{4,36},{5,37},{6,38},{7,39},{8,40},{9,... | collective-permute-start | bytes 2457608 | tf_op jit(solution)/shard_map/ppermute | solution.py:445
  109.3 6.9 %collective-permute-start.17 = (bf16[2,272,256]{2,1,0:T(8,128)(2,1)S(1)}, bf16[2,272,256]{2,1,0:T(8,128)(2,1)S(1)}, u32[]{:S(2)}, u32[]{:S(2)}) collective-permute-start(bf16[2,272,256]{2,1,0:T(8,128)(2,1)S(1)} %get-tuple-element.34), channel_id=1, source_target_pairs={{0,16},{1,17},{2,18},{3,19},{4,20},{5,21},{6,22},{7,23},{8,24},{9,... | collective-permute-start | bytes 835592 | tf_op jit(solution)/shard_map/ppermute | solution.py:449
  110.1 8.0 %copy-start.1 = (bf16[2,2048,512]{2,1,0:T(8,128)(2,1)S(1)}, bf16[2,2048,512]{2,1,0:T(8,128)(2,1)}, u32[]{:S(2)}) copy-start(bf16[2,2048,512]{2,1,0:T(8,128)(2,1)} %cache_ref.3) | copy-start | bytes 12582916
  116.0 6.0 %copy-start.3 = (bf16[4,272,256]{2,1,0:T(8,128)(2,1)}, bf16[4,272,256]{2,1,0:T(8,128)(2,1)S(1)}, u32[]{:S(2)}) copy-start(bf16[4,272,256]{2,1,0:T(8,128)(2,1)S(1)} %get-tuple-element.31.ab1_ref.oab_ref) | copy-start | bytes 1671172
  116.0 2.0 %collective-permute-start.16 = (bf16[4,272,256]{2,1,0:T(8,128)(2,1)S(1)}, bf16[4,272,256]{2,1,0:T(8,128)(2,1)S(1)}, u32[]{:S(2)}, u32[]{:S(2)}) collective-permute-start(bf16[4,272,256]{2,1,0:T(8,128)(2,1)S(1)} %get-tuple-element.33), channel_id=1, source_target_pairs={{0,16},{1,17},{2,18},{3,19},{4,20},{5,21},{6,22},{7,23},{8,24},{9,... | collective-permute-start | bytes 1671176 | tf_op jit(solution)/shard_map/ppermute | solution.py:449
  118.1 3.9 %copy-start.5 = (bf16[4,272,256]{2,1,0:T(8,128)(2,1)}, bf16[4,272,256]{2,1,0:T(8,128)(2,1)S(1)}, u32[]{:S(2)}) copy-start(bf16[4,272,256]{2,1,0:T(8,128)(2,1)S(1)} %collective-permute-done.16.ab2_ref.tab_ref) | copy-start | bytes 1671172
  122.0 9.9 %copy-start.4 = (bf16[4,272,256]{2,1,0:T(8,128)(2,1)S(1)}, bf16[4,272,256]{2,1,0:T(8,128)(2,1)}, u32[]{:S(2)}) copy-start(bf16[4,272,256]{2,1,0:T(8,128)(2,1)} %copy-done.3) | copy-start | bytes 1671172
  122.1 28.1 %collective-permute-start.20 = (bf16[4,2,80,640]{3,2,1,0:T(8,128)(2,1)}, bf16[4,2,80,640]{3,2,1,0:T(8,128)(2,1)}, u32[]{:S(2)}, u32[]{:S(2)}) collective-permute-start(bf16[4,2,80,640]{3,2,1,0:T(8,128)(2,1)} %collective-permute-done.18.refs_2_), channel_id=1, source_target_pairs={{0,4},{1,5},{2,6},{3,7},{4,8},{5,9},{6,10},{7,11},{8,12},{9,13},{1... | collective-permute-start | bytes 2457608 | tf_op jit(solution)/shard_map/ppermute | solution.py:445
  124.6 27.7 %collective-permute-start.21 = (bf16[2,4,80,640]{3,2,1,0:T(8,128)(2,1)}, bf16[2,4,80,640]{3,2,1,0:T(8,128)(2,1)}, u32[]{:S(2)}, u32[]{:S(2)}) collective-permute-start(bf16[2,4,80,640]{3,2,1,0:T(8,128)(2,1)} %collective-permute-done.19.refs_6_), channel_id=1, source_target_pairs={{0,32},{1,33},{2,34},{3,35},{4,36},{5,37},{6,38},{7,39},{8,40},{9,... | collective-permute-start | bytes 2457608 | tf_op jit(solution)/shard_map/ppermute | solution.py:445
  127.0 25.3 %collective-permute-start.22 = (bf16[4,2,80,640]{3,2,1,0:T(8,128)(2,1)}, bf16[4,2,80,640]{3,2,1,0:T(8,128)(2,1)}, u32[]{:S(2)}, u32[]{:S(2)}) collective-permute-start(bf16[4,2,80,640]{3,2,1,0:T(8,128)(2,1)} %bitcast_dynamic-update-slice_fusion.4.refs_0_), channel_id=1, source_target_pairs={{0,16},{1,17},{2,18},{3,19},{4,20},{5,21},{6,22},{7,23},{8,24},{9,... | collective-permute-start | bytes 2457608 | tf_op jit(solution)/shard_map/ppermute | solution.py:449
  127.0 25.8 %collective-permute-start.26 = (bf16[2,4,80,640]{3,2,1,0:T(8,128)(2,1)}, bf16[2,4,80,640]{3,2,1,0:T(8,128)(2,1)}, u32[]{:S(2)}, u32[]{:S(2)}) collective-permute-start(bf16[2,4,80,640]{3,2,1,0:T(8,128)(2,1)} %bitcast_dynamic-update-slice_fusion.3.refs_4_), channel_id=1, source_target_pairs={{0,16},{1,17},{2,18},{3,19},{4,20},{5,21},{6,22},{7,23},{8,24},{9,... | collective-permute-start | bytes 2457608 | tf_op jit(solution)/shard_map/ppermute | solution.py:449
  127.5 25.4 %collective-permute-start.23 = (bf16[4,2,80,640]{3,2,1,0:T(8,128)(2,1)}, bf16[4,2,80,640]{3,2,1,0:T(8,128)(2,1)}, u32[]{:S(2)}, u32[]{:S(2)}) collective-permute-start(bf16[4,2,80,640]{3,2,1,0:T(8,128)(2,1)} %collective-permute-done.7.refs_1_), channel_id=1, source_target_pairs={{0,16},{1,17},{2,18},{3,19},{4,20},{5,21},{6,22},{7,23},{8,24},{9,... | collective-permute-start | bytes 2457608 | tf_op jit(solution)/shard_map/ppermute | solution.py:449
  127.5 28.6 %all-to-all-start.2 = ((bf16[128,2,24,128]{3,2,1,0:T(8,128)(2,1)}), bf16[128,2,24,128]{3,2,1,0:T(8,128)(2,1)S(1)}, u32[]{:S(2)}, u32[]{:S(2)}) async-start(bf16[128,2,24,128]{3,2,1,0:T(8,128)(2,1)} %bitcast.30), calls=%async_computation.2 | async-start | bytes 3145728 | tf_op jit(solution)/shard_map/all_to_all | solution.py:430
  132.0 1.1 copy-start.6
  133.0 1.6 copy-start.8
  149.1 1.1 copy-start.2
  150.1 7.2 %collective-permute-start.27 = (bf16[2,4,80,640]{3,2,1,0:T(8,128)(2,1)}, bf16[2,4,80,640]{3,2,1,0:T(8,128)(2,1)S(1)}, u32[]{:S(2)}, u32[]{:S(2)}) collective-permute-start(bf16[2,4,80,640]{3,2,1,0:T(8,128)(2,1)} %collective-permute-done.11.refs_5_), channel_id=1, source_target_pairs={{0,16},{1,17},{2,18},{3,19},{4,20},{5,21},{6,22},{7,23},{8,24},{9,... | collective-permute-start | bytes 2457608 | tf_op jit(solution)/shard_map/ppermute | solution.py:449
  152.3 5.1 %collective-permute-start.24 = (bf16[4,2,80,640]{3,2,1,0:T(8,128)(2,1)}, bf16[4,2,80,640]{3,2,1,0:T(8,128)(2,1)}, u32[]{:S(2)}, u32[]{:S(2)}) collective-permute-start(bf16[4,2,80,640]{3,2,1,0:T(8,128)(2,1)} %collective-permute-done.18.refs_2_), channel_id=1, source_target_pairs={{0,16},{1,17},{2,18},{3,19},{4,20},{5,21},{6,22},{7,23},{8,24},{9,... | collective-permute-start | bytes 2457608 | tf_op jit(solution)/shard_map/ppermute | solution.py:449
  152.3 5.1 %collective-permute-start.28 = (bf16[2,4,80,640]{3,2,1,0:T(8,128)(2,1)}, bf16[2,4,80,640]{3,2,1,0:T(8,128)(2,1)}, u32[]{:S(2)}, u32[]{:S(2)}) collective-permute-start(bf16[2,4,80,640]{3,2,1,0:T(8,128)(2,1)} %collective-permute-done.19.refs_6_), channel_id=1, source_target_pairs={{0,16},{1,17},{2,18},{3,19},{4,20},{5,21},{6,22},{7,23},{8,24},{9,... | collective-permute-start | bytes 2457608 | tf_op jit(solution)/shard_map/ppermute | solution.py:449
  152.8 4.6 %collective-permute-start.25 = (bf16[4,2,80,640]{3,2,1,0:T(8,128)(2,1)}, bf16[4,2,80,640]{3,2,1,0:T(8,128)(2,1)}, u32[]{:S(2)}, u32[]{:S(2)}) collective-permute-start(bf16[4,2,80,640]{3,2,1,0:T(8,128)(2,1)} %collective-permute-done.20.refs_3_), channel_id=1, source_target_pairs={{0,16},{1,17},{2,18},{3,19},{4,20},{5,21},{6,22},{7,23},{8,24},{9,... | collective-permute-start | bytes 2457608 | tf_op jit(solution)/shard_map/ppermute | solution.py:449
  152.9 5.6 %collective-permute-start.29 = (bf16[2,4,80,640]{3,2,1,0:T(8,128)(2,1)}, bf16[2,4,80,640]{3,2,1,0:T(8,128)(2,1)}, u32[]{:S(2)}, u32[]{:S(2)}) collective-permute-start(bf16[2,4,80,640]{3,2,1,0:T(8,128)(2,1)} %collective-permute-done.21.refs_7_), channel_id=1, source_target_pairs={{0,16},{1,17},{2,18},{3,19},{4,20},{5,21},{6,22},{7,23},{8,24},{9,... | collective-permute-start | bytes 2457608 | tf_op jit(solution)/shard_map/ppermute | solution.py:449
  157.3 1.1 copy-start.10
Sparse Core Ops, SparseCore 0:
  13.2 89.1 all-gather.1
